TPU v7x, 32 devices: a whole 2x2x4 slice. The times are simulated.
32 devices in a mesh: comp: 2 (over core), gy: 4 (over y, x), gx: 4 (over z).
Axes of the slice: x: 2, y: 2, z: 4, core: 2. Of those that a mesh axis runs over, the one named last changes fastest.
Arguments:
- ocean_state: float32 [16, 8, 16, 512], P('comp', None, 'gx', 'gy'), may hold values from -4 to 4, as said below
- irradiance: float32 [16, 512], P('gx', 'gy'), may hold values from 0.5 to 4
- land_mask: int32 [16, 512], P('gx', 'gy'), may hold values 0 or 1
- bottom_level: int32 [16, 512], P('gx', 'gy'), may hold values from 1 to 8
Outputs:
- new_state: float32 [16, 8, 16, 512], P('comp', None, 'gx', 'gy')
Inputs may be any that keep to these rules, and one draw needn't show every extreme that they name: `ocean_state`: channels 0 to 3 hold velocity along x, velocity along y, temperature and salinity now, channels 4 to 7 the same one step earlier; the 8 tracer channels are positive.
All inputs are finite; a program needn't handle non-finite values. No bound on the sum of `land_mask` on one device may be relied on, other than what follows from the above.
Results may differ from a plain program's by a relative error of at most 0.0003.
Values sent between devices are 32-bit elements; how exact they have to be, the bound alone decides.
No kernel may reach another device: no remote copies, remote signals or barrier semaphores. Data moves between devices by JAX's collectives and lax.ppermute only.
A program may use at most 64 MiB of HBM per device.

v0:
```python
import jax
import jax.numpy as jnp
from jax import lax
from jax.experimental import pallas as pl
from jax.experimental.pallas import tpu as pltpu
from jax.sharding import PartitionSpec as P


HALO = 2
FIELDS = 8
U, V, TEMP, SALT, UB, VB, TB, SB = range(FIELDS)
VEL_X = (U, UB)


def lane_roll(x, shift):
    shift %= x.shape[1]
    return pltpu.roll(x, shift, 1) if shift else x


def level_roll(x, shift):
    shift %= x.shape[0]
    return pltpu.roll(x, shift, 0) if shift else x


class Shape:
    def __init__(self, lev, cx, rows):
        self.lev, self.cx, self.rows = lev, cx, rows
        self.cols = cx + 2 * HALO
        self.group = rows // self.cols
        self.per_tile = self.group // (2 * HALO)
        self.half = self.group // 2
        self.edge_tiles = -(-FIELDS // self.per_tile) + 1
        assert self.per_tile >= 2 and self.group >= 4 * HALO and 2 * cx <= lev
        assert self.cols * self.group == rows
        self.mask_tile = FIELDS * cx
        self.halo_tiles = FIELDS * HALO
        self.edge_base = 2 * self.halo_tiles + 2

    def lanes(self):
        return lax.broadcasted_iota(jnp.int32, (self.lev, self.rows), 1)

    def levels(self):
        return lax.broadcasted_iota(jnp.int32, (self.lev, self.rows), 0)

    def row(self, ref, tile, r):
        return jnp.broadcast_to(ref[tile, r : r + 1, :], (self.lev, self.rows))

    def edge_place(self, acc, value, j, channel, lane):
        at = j * self.group + channel * 2 * HALO + HALO
        return jnp.where((lane >= at - HALO) & (lane < at + HALO), lane_roll(value, at), acc)


def pack_kernel(sh, *refs):
    sources, (x_ref, e_ref, ma_ref, mb_ref), arrived, sem = refs[:4], refs[4:8], refs[8:12], refs[12]
    copies = [
        pltpu.make_async_copy(a, b, sem.at[i]) for i, (a, b) in enumerate(zip(sources, arrived))
    ]
    for copy in copies:
        copy.start()
    for copy in copies:
        copy.wait()
    state_ref, irr_ref, land_ref, bottom_ref = arrived
    odd = lax.axis_index("gx") % 2 == 1
    flip = jnp.where(odd & (lax.axis_index("comp") == 0), -1.0, 1.0)
    lane = sh.lanes()
    cx = sh.cx
    zero = jnp.zeros((sh.lev, sh.rows), jnp.float32)
    edges = [zero] * sh.edge_tiles
    for ch in range(FIELDS):
        raw = [state_ref[pl.ds(ch * sh.lev * cx + i, sh.lev, stride=cx), :] for i in range(cx)]
        cols = [jnp.where(odd, raw[cx - 1 - k], raw[k]) for k in range(cx)]
        if ch in VEL_X:
            cols = [c * flip for c in cols]
        t, q = divmod(ch, sh.per_tile)
        for k in range(cx):
            x_ref[ch * cx + k] = cols[k]
            edges[t] = sh.edge_place(edges[t], cols[k], k + HALO, q, lane)
        for d in range(HALO):
            mb_ref[ch * HALO + d] = cols[d]
            ma_ref[ch * HALO + d] = cols[cx - 1 - d]
    depth = jnp.where(land_ref[...] == 1, bottom_ref[...], 0).astype(jnp.float32)
    irr = irr_ref[...]
    rows = []
    for value in (irr, depth):
        rows += [
            jnp.where(odd, value[cx - 1 - k : cx - k, :], value[k : k + 1, :]) for k in range(cx)
        ]
    for r, value in enumerate(rows):
        x_ref[sh.mask_tile, r : r + 1, :] = value
        mb_ref[sh.halo_tiles, r : r + 1, :] = value
        ma_ref[sh.halo_tiles, r : r + 1, :] = value
        q, k = divmod(r, cx)
        wide = jnp.broadcast_to(value, (sh.lev, sh.rows))
        edges[-1] = sh.edge_place(edges[-1], wide, k + HALO, q, lane)
    for t in range(sh.edge_tiles):
        e_ref[t] = edges[t]


def merge_kernel(sh, e_ref, ra_ref, rb_ref, eo_ref, h_ref):
    flip = jnp.where(lax.axis_index("comp") == 0, -1.0, 1.0)
    lane = sh.lanes()
    cx = sh.cx
    edges = [e_ref[t] for t in range(sh.edge_tiles)]
    sides = (
        (ra_ref, 0, lambda d: cx + HALO + d, lambda d: cx - 1 - d),
        (rb_ref, 1, lambda d: HALO - 1 - d, lambda d: d),
    )
    for ref, side, place, source in sides:
        for ch in range(FIELDS):
            t, q = divmod(ch, sh.per_tile)
            for d in range(HALO):
                value = ref[ch * HALO + d]
                if ch in VEL_X:
                    value = value * flip
                h_ref[side * sh.halo_tiles + ch * HALO + d] = value
                edges[t] = sh.edge_place(edges[t], value, place(d), q, lane)
        h_ref[2 * sh.halo_tiles + side] = ref[sh.halo_tiles]
        for q in range(2):
            for d in range(HALO):
                value = sh.row(ref, sh.halo_tiles, q * cx + source(d))
                edges[-1] = sh.edge_place(edges[-1], value, place(d), q, lane)
    for t in range(sh.edge_tiles):
        eo_ref[t] = edges[t]
        h_ref[sh.edge_base + t] = edges[t]


STRIP = "strip"


class Field:
    def __init__(self, sh, lane, col, strip):
        self.sh, self.lane, self.col, self.strip = sh, lane, col, strip

    def centre(self, site):
        return self.strip() if site == STRIP else self.col(site)

    def east(self, site):
        return lane_roll(self.strip(), -self.sh.group) if site == STRIP else self.col(site + 1)

    def west(self, site):
        return lane_roll(self.strip(), self.sh.group) if site == STRIP else self.col(site - 1)

    def north(self, site):
        if site == STRIP:
            return lane_roll(self.strip(), -1)
        sh = self.sh
        end = sh.rows - 1
        beyond = lane_roll(self.strip(), end - (site * sh.group + sh.half + HALO))
        return jnp.where(self.lane == end, beyond, lane_roll(self.col(site), -1))

    def south(self, site):
        if site == STRIP:
            return lane_roll(self.strip(), 1)
        sh = self.sh
        beyond = lane_roll(self.strip(), -(site * sh.group + HALO - 1))
        return jnp.where(self.lane == 0, beyond, lane_roll(self.col(site), 1))

    def around(self, site):
        return self.east(site), self.west(site), self.north(site), self.south(site)


def step_kernel(sh, xo, xp, ho, hp, rao, rbo, rap, rbp, out_ref, strips, fresh, masks):
    lane, level = sh.lanes(), sh.levels()
    cx, group = sh.cx, sh.group
    gy, ny = lax.axis_index("gy"), lax.axis_size("gy")
    odd_x = lax.axis_index("gx") % 2 == 1
    mirror = jnp.where(odd_x, -1.0, 1.0)
    even_y = gy % 2 == 0
    slot = lane % (2 * HALO)
    in_group = lane % group
    first_step = list(range(1, sh.cols - 1))
    own = list(range(HALO, HALO + cx))
    sites = first_step + [STRIP]
    zero = jnp.zeros((sh.lev, sh.rows), jnp.float32)

    def cumulate(x):
        reach = 1
        while reach < sh.lev:
            x = x + jnp.where(level >= reach, level_roll(x, reach), 0.0)
            reach *= 2
        return x

    def place(site):
        return sh.cols if site == STRIP else site

    def build_strips(h, ra, rb, base, tiles, channels):
        for t in tiles:
            a, b, mine = ra[t], rb[t], h[sh.edge_base + t]
            left = jnp.where(gy > 0, jnp.where(even_y, b, a), zero)
            right = jnp.where(gy < ny - 1, jnp.where(even_y, a, b), zero)
            low = jnp.where(slot < HALO, left, mine)
            high = jnp.where(slot < HALO, mine, right)
            for q in range(channels):
                at = q * 2 * HALO
                strips[base + (t - tiles[0]) * channels + q] = jnp.where(
                    in_group < sh.half, lane_roll(low, -at), lane_roll(high, sh.half - at)
                )

    field_tiles = range(sh.edge_tiles - 1)
    build_strips(ho, rao, rbo, 0, field_tiles, sh.per_tile)
    build_strips(hp, rap, rbp, FIELDS, field_tiles, sh.per_tile)
    build_strips(ho, rao, rbo, 2 * FIELDS, [sh.edge_tiles - 1], 2)

    def mask_row(kind, j):
        if HALO <= j < HALO + cx:
            return sh.row(xo, sh.mask_tile, kind * cx + j - HALO)
        if j < HALO:
            return sh.row(ho, 2 * sh.halo_tiles + 1, kind * cx + HALO - 1 - j)
        return sh.row(ho, 2 * sh.halo_tiles, kind * cx + cx - 1 - (j - HALO - cx))

    levelf = level.astype(jnp.float32)

    def depth_at(site):
        return strips[2 * FIELDS + 1] if site == STRIP else mask_row(1, site)

    def irr_at(site):
        return strips[2 * FIELDS] if site == STRIP else mask_row(0, site)

    for j in range(sh.cols):
        masks[j] = jnp.where(levelf < depth_at(j), 1.0, 0.0)
    masks[sh.cols] = jnp.where(levelf < depth_at(STRIP), 1.0, 0.0)
    wet = Field(sh, lane, lambda j: masks[j], lambda: masks[sh.cols])
    face_base = sh.cols + 1
    for site in sites:
        w = wet.centre(site)
        for n, value in enumerate(wet.around(site)):
            masks[face_base + place(site) * 4 + n] = w * value

    def faces(site):
        return [masks[face_base + place(site) * 4 + n] for n in range(4)]

    def raw(x, h, base, ch):
        def col(j):
            if HALO <= j < HALO + cx:
                return x[ch * cx + j - HALO]
            if j < HALO:
                return h[sh.halo_tiles + ch * HALO + HALO - 1 - j]
            return h[ch * HALO + j - HALO - cx]

        return Field(sh, lane, col, lambda: strips[base + ch])

    slots = sh.cols + 1

    def stored(index):
        return Field(
            sh, lane, lambda j: fresh[index * slots + j], lambda: fresh[index * slots + sh.cols]
        )

    def store(index, site, value):
        fresh[index * slots + place(site)] = value

    def density_of(temp, salt, w):
        return (0.8 * salt - 0.2 * temp) * w

    def speeds(u, v, site, m):
        uc, vc = u.centre(site), v.centre(site)
        qe = 0.025 * (uc + u.east(site)) * m[0]
        qw = 0.025 * (uc + u.west(site)) * m[1]
        qn = 0.025 * (vc + v.north(site)) * m[2]
        qs = 0.025 * (vc + v.south(site)) * m[3]
        return qe, qw, qn, qs, (qw - qe) + (qs - qn)

    def laplacian(f, site, m, total):
        e, w, n, s = f.around(site)
        return (m[0] * e + m[1] * w) + (m[2] * n + m[3] * s) - total * f.centre(site)

    def coriolis(site):
        if site == STRIP:
            row = jnp.where(in_group < sh.half, in_group - HALO, sh.rows - HALO + in_group - sh.half)
        else:
            row = lane
        row = (row + gy * sh.rows).astype(jnp.float32)
        return mirror * (0.3 + 0.4 * row / (ny * sh.rows))

    def dynamics(d, pressure, site, heat, q, m, full):
        w = wet.centre(site)
        total = (m[0] + m[1]) + (m[2] + m[3])
        uc, vc = d[U].centre(site), d[V].centre(site)
        after = {}
        if "vel" in full:
            pc = pressure.centre(site)
            pe, pw, pn, ps = pressure.around(site)
            push_x = 0.1 * (m[0] * (pe - pc) + m[1] * (pc - pw))
            push_y = 0.1 * (m[2] * (pn - pc) + m[3] * (pc - ps))
            f = 0.2 * coriolis(site) * w
            after[U] = d[UB].centre(site) + (f * vc - push_x + 0.04 * laplacian(d[UB], site, m, total))
            after[V] = d[VB].centre(site) + (
                0.04 * laplacian(d[VB], site, m, total) - f * uc - push_y
            )
        if "tracer" in full:
            qe, qw, qn, qs, qc = q
            for now, before in ((TEMP, TB), (SALT, SB)):
                e, w_, n, s = d[now].around(site)
                carried = (qw * w_ - qe * e) + (qs * s - qn * n) + qc * d[now].centre(site)
                change = 2.0 * carried + 0.04 * laplacian(d[before], site, m, total)
                if now == TEMP:
                    change = change + 0.6 * heat
                after[now] = d[before].centre(site) + change
        return after

    def filtered(d, site, ch, after):
        w = wet.centre(site)
        now, before = d[ch].centre(site), d[ch + 4].centre(site)
        return now + 0.1 * (before - 2.0 * now + after) * w

    def optics(c2, c3):
        absorb = 0.08 + 0.05 * (jnp.abs(c2) + jnp.abs(c3))
        return absorb, cumulate(absorb)

    def heating(absorb, depthsum, site):
        fade = jnp.exp(-depthsum)
        above = jnp.where(level == 0, 1.0, level_roll(fade, 1))
        return irr_at(site) * wet.centre(site) * (above - fade)

    def light(absorb, depthsum, site):
        return irr_at(site) * jnp.exp(0.5 * absorb - depthsum)

    def mixing(temp, salt, site):
        rho = density_of(temp, salt, wet.centre(site))
        below = level_roll(rho, -1)
        wet_below = jnp.where(levelf + 1.0 < depth_at(site), 1.0, 0.0)
        return (0.005 + 0.1 / (1.0 + 4.0 * jnp.maximum(below - rho, 0.0))) * wet_below

    def reactions(c, temp, lit, which):
        nn, na = jnp.abs(c[0]), jnp.abs(c[1])
        base = jnp.exp(0.06 * temp) * (lit / (lit + 0.5))
        total = nn + na
        small = 0.6 * base * c[2] / (0.2 + total)
        large = 0.9 * base * c[3] / (0.8 + total)
        graze = 0.8 * c[4] / (1.0 + (jnp.abs(c[2]) + jnp.abs(c[3])))
        gs, gl = graze * c[2], graze * c[3]
        up_s, up_l = small * total, large * total
        r = {2: up_s - gs - 0.1 * c[2], 3: up_l - gl - 0.1 * c[3]}
        if len(which) > 2:
            both = small + large
            remin = 0.3 * c[5] + 0.1 * c[6]
            nitrify = 0.2 * c[1]
            r[0] = nitrify - both * nn
            r[1] = remin + 0.1 * c[4] - nitrify - both * na
            r[4] = 0.7 * (gs + gl) - 0.25 * c[4]
            r[5] = 0.1 * c[2] + 0.3 * gs - 0.3 * c[5]
            r[6] = 0.1 * c[3] + 0.15 * c[4] + 0.3 * gl - 0.1 * c[6]
            r[7] = 1.3 * (up_s + up_l) - (remin + 2.0 * nitrify)
        return r

    def tracer_step(c, site, q, m, kappa, temp, lit, which, emit):
        w = wet.centre(site)
        qe, qw, qn, qs, qc = q
        total = (m[0] + m[1]) + (m[2] + m[3])
        ke, kw = 0.02 * m[0] - qe, 0.02 * m[1] + qw
        kn, ks = 0.02 * m[2] - qn, 0.02 * m[3] + qs
        kc = (1.0 - 0.02 * total) + qc
        centre = {i: c[i].centre(site) for i in (which if len(which) > 2 else range(5))}
        r = reactions(centre, temp, lit, which)
        tenth = 0.1 * w
        for i in which:
            e, w_, n, s = c[i].around(site)
            here = centre[i]
            down = kappa * (level_roll(here, -1) - here)
            emit(
                i,
                kc * here
                + ((ke * e + kw * w_) + (kn * n + ks * s))
                + (down - level_roll(down, 1))
                + tenth * r[i],
            )

    def write(ch, k_values):
        for i in range(cx):
            out_ref[pl.ds(ch * sh.lev * cx + i, sh.lev, stride=cx), :] = jnp.where(
                odd_x, k_values[cx - 1 - i], k_values[i]
            )

    def make_pressure(d, index, all_sites):
        for site in all_sites:
            rho = density_of(d[TEMP].centre(site), d[SALT].centre(site), wet.centre(site))
            store(index, site, 0.1 * cumulate(rho))
        return stored(index)

    everywhere = list(range(sh.cols)) + [STRIP]

    @pl.when(lax.axis_index("comp") == 0)
    def _():
        d = [raw(xo, ho, 0, ch) for ch in range(FIELDS)]
        c = [raw(xp, hp, FIELDS, ch) for ch in range(FIELDS)]
        extra = FIELDS
        pressure = make_pressure(d, extra + 2, everywhere)
        for site in sites:
            m = faces(site)
            q = speeds(d[U], d[V], site, m)
            optic = optics(c[2].centre(site), c[3].centre(site))
            heat = heating(*optic, site)
            after = dynamics(d, pressure, site, heat, q, m, ("vel", "tracer"))
            for ch, value in after.items():
                store(ch, site, value)
                store(ch + 4, site, filtered(d, site, ch, value))
            if site in own:
                temp, salt = d[TEMP].centre(site), d[SALT].centre(site)
                tracer_step(
                    c, site, q, m, mixing(temp, salt, site), temp, light(*optic, site), (2, 3),
                    lambda i, value: store(extra + i - 2, site, value),
                )
        d = [stored(ch) for ch in range(FIELDS)]
        pressure = make_pressure(d, extra + 2, first_step + [STRIP])
        done = {}
        for site in own:
            m = faces(site)
            q = speeds(d[U], d[V], site, m)
            optic = optics(stored(extra).centre(site), stored(extra + 1).centre(site))
            heat = heating(*optic, site)
            after = dynamics(d, pressure, site, heat, q, m, ("vel", "tracer"))
            for ch, value in after.items():
                done[ch, site] = value
                done[ch + 4, site] = filtered(d, site, ch, value)
        for ch in range(FIELDS):
            factor = mirror if ch in VEL_X else 1.0
            write(ch, [done[ch, site] * factor if ch in VEL_X else done[ch, site] for site in own])

    @pl.when(lax.axis_index("comp") != 0)
    def _():
        d = [raw(xp, hp, FIELDS, ch) for ch in range(FIELDS)]
        c = [raw(xo, ho, 0, ch) for ch in range(FIELDS)]
        extra = FIELDS
        pressure = make_pressure(d, extra + 4, everywhere)
        for site in sites:
            m = faces(site)
            q = speeds(d[U], d[V], site, m)
            optic = optics(c[2].centre(site), c[3].centre(site))
            temp, salt = d[TEMP].centre(site), d[SALT].centre(site)
            inner = site in own
            heat = heating(*optic, site) if inner else None
            full = ("vel", "tracer") if inner else ("vel",)
            after = dynamics(d, pressure, site, heat, q, m, full)
            for ch, value in after.items():
                store(extra + ch, site, value)
            tracer_step(
                c, site, q, m, mixing(temp, salt, site), temp, light(*optic, site), range(FIELDS),
                lambda i, value: store(i, site, value),
            )
        c = [stored(ch) for ch in range(FIELDS)]
        d = [stored(extra + ch) for ch in range(4)]
        done = {}
        for site in own:
            m = faces(site)
            q = speeds(d[U], d[V], site, m)
            optic = optics(c[2].centre(site), c[3].centre(site))
            temp, salt = d[TEMP].centre(site), d[SALT].centre(site)

            def emit(i, value):
                done[i, site] = value

            tracer_step(
                c, site, q, m, mixing(temp, salt, site), temp, light(*optic, site), range(FIELDS),
                emit,
            )
        for ch in range(FIELDS):
            write(ch, [done[ch, site] for site in own])


def tiles(sh, n):
    return jax.ShapeDtypeStruct((n, sh.lev, sh.rows), jnp.float32)


def call(kernel, sh, outs, args, flops, scratch=(), source=pltpu.VMEM):
    spec = pl.BlockSpec(memory_space=pltpu.VMEM)
    size = sum(a.size for a in args) + sum(o.size for o in outs)
    return pl.pallas_call(
        lambda *refs: kernel(sh, *refs),
        out_shape=outs,
        in_specs=[pl.BlockSpec(memory_space=source)] * len(args),
        out_specs=[spec] * len(outs),
        scratch_shapes=list(scratch),
        compiler_params=pltpu.CompilerParams(vmem_limit_bytes=16 << 20),
        cost_estimate=pl.CostEstimate(flops=flops, bytes_accessed=4 * size, transcendentals=0),
    )(*args)


def local(ocean_state, irradiance, land_mask, bottom_level):
    fields, lev, cx, rows = ocean_state.shape
    assert fields == FIELDS
    sh = Shape(lev, cx, rows)
    nx, ny = lax.axis_size("gx"), lax.axis_size("gy")
    assert nx % 2 == 0 and ny % 2 == 0
    axes = ("comp", "gy", "gx")

    def send(value, target):
        pairs = []
        for c in range(2):
            for y in range(ny):
                for x in range(nx):
                    tc, ty, tx = target(c, y, x)
                    pairs.append(((c * ny + y) * nx + x, (tc * ny + ty) * nx + tx))
        return lax.ppermute(value, axes, pairs)

    def odd_pair(i, n):
        return (i + 1) % n if i % 2 else (i - 1) % n

    def x_a(v):
        return send(v, lambda c, y, x: (c, y, x ^ 1))

    def x_b(v):
        return send(v, lambda c, y, x: (c, y, odd_pair(x, nx)))

    def y_a(v):
        return send(v, lambda c, y, x: (c, y ^ 1, x))

    def y_b(v):
        return send(v, lambda c, y, x: (c, odd_pair(y, ny), x))

    def swap(v):
        return send(v, lambda c, y, x: (1 - c, y, x))

    flat = ocean_state.reshape(fields * lev * cx, rows)
    x, e0, ma, mb = call(
        pack_kernel,
        sh,
        [
            tiles(sh, fields * cx + 1),
            tiles(sh, sh.edge_tiles),
            tiles(sh, sh.halo_tiles + 1),
            tiles(sh, sh.halo_tiles + 1),
        ],
        tuple(pltpu.with_memory_space_constraint(a, pltpu.HBM) for a in (flat, irradiance, land_mask, bottom_level)),
        100_000,
        scratch=[
            pltpu.VMEM(a.shape, a.dtype) for a in (flat, irradiance, land_mask, bottom_level)
        ]
        + [pltpu.SemaphoreType.DMA((4,))],
        source=pltpu.HBM,
    )
    ra, rb = x_a(ma), x_b(mb)
    xp = swap(x)
    e1, h = call(
        merge_kernel,
        sh,
        [tiles(sh, sh.edge_tiles), tiles(sh, sh.edge_base + sh.edge_tiles)],
        (e0, ra, rb),
        100_000,
    )
    ya, yb = y_a(e1), y_b(e1)
    hp = swap(h)
    yap, ybp = swap(ya), swap(yb)
    width = sh.cols + 1
    (out,) = call(
        step_kernel,
        sh,
        [jax.ShapeDtypeStruct(flat.shape, jnp.float32)],
        (x, xp, h, hp, ya, yb, yap, ybp),
        10_000_000,
        scratch=[
            pltpu.VMEM((2 * FIELDS + 2, lev, rows), jnp.float32),
            pltpu.VMEM(((FIELDS + 5) * width, lev, rows), jnp.float32),
            pltpu.VMEM((width + 4 * width, lev, rows), jnp.float32),
        ],
    )
    return out.reshape(ocean_state.shape)


def solution(mesh):
    return jax.shard_map(
        local,
        mesh=mesh,
        in_specs=(P("comp", None, "gx", "gy"), P("gx", "gy"), P("gx", "gy"), P("gx", "gy")),
        out_specs=P("comp", None, "gx", "gy"),
        check_vma=False,
    )
```

profile of v0, /device:TPU:1, one launch (start us, length us, event | category | flops | bytes accessed | tf_op | source)
XLA Modules:
  0.0 19.7 jit_solution(1009456777546593395)
XLA Ops:
  0.0 1.1 %shard_map.46 = (f32[33,8,128]{2,1,0:T(8,128)S(1)}, f32[3,8,128]{2,1,0:T(8,128)S(1)}, f32[17,8,128]{2,1,0:T(8,128)S(1)}, f32[17,8,128]{2,1,0:T(8,128)S(1)}) custom-call(f32[256,128]{1,0:T(8,128)} %bitcast.2, f32[4,128]{1,0:T(4,128)} %refs_1_.1, s32[4,128]{1,0:T(4,128)} %refs_2_.1, s32[4,128]{1,0:T(4,128)} %refs_3_.1), custom_call_target="tpu_custom_call" | custom-call | flops 100000 | bytes 423936 | tf_op jit(solution)/shard_map/pallas_call | solution.py:467
  1.1 2.2 %collective-permute-start.1 = (f32[17,8,128]{2,1,0:T(8,128)S(1)}, f32[17,8,128]{2,1,0:T(8,128)S(1)}, u32[]{:S(2)}, u32[]{:S(2)}) collective-permute-start(f32[17,8,128]{2,1,0:T(8,128)S(1)} %get-tuple-element.13), channel_id=1, source_target_pairs={{0,1},{1,0},{2,3},{3,2},{4,5},{5,4},{6,7},{7,6},{8,9},{9,8},{10,11... | collective-permute-start | bytes 208904 | tf_op jit(solution)/shard_map/ppermute | solution.py:493
  3.3 2.2 %collective-permute-start.2 = (f32[17,8,128]{2,1,0:T(8,128)S(1)}, f32[17,8,128]{2,1,0:T(8,128)S(1)}, u32[]{:S(2)}, u32[]{:S(2)}) collective-permute-start(f32[17,8,128]{2,1,0:T(8,128)S(1)} %get-tuple-element.14), channel_id=1, source_target_pairs={{0,3},{1,2},{2,1},{3,0},{4,7},{5,6},{6,5},{7,4},{8,11},{9,10},{10,... | collective-permute-start | bytes 208904 | tf_op jit(solution)/shard_map/ppermute | solution.py:493
  5.5 0.0 collective-permute-done.1.refs_1_
  5.5 3.4 %collective-permute-done.2.refs_2_ = f32[17,8,128]{2,1,0:T(8,128)S(1)} collective-permute-done((f32[17,8,128]{2,1,0:T(8,128)S(1)}, f32[17,8,128]{2,1,0:T(8,128)S(1)}, u32[]{:S(2)}, u32[]{:S(2)}) %collective-permute-start.2) | collective-permute-done | bytes 69664 | tf_op jit(solution)/shard_map/ppermute | solution.py:493
  8.9 0.1 shard_map.47
  9.0 1.6 %collective-permute-start.3 = (f32[37,8,128]{2,1,0:T(8,128)S(1)}, f32[37,8,128]{2,1,0:T(8,128)S(1)}, u32[]{:S(2)}, u32[]{:S(2)}) collective-permute-start(f32[37,8,128]{2,1,0:T(8,128)S(1)} %get-tuple-element.15.refs_2_), channel_id=1, source_target_pairs={{0,16},{1,17},{2,18},{3,19},{4,20},{5,21},{6,22},{7,23},{8,24},{9,... | collective-permute-start | bytes 454664 | tf_op jit(solution)/shard_map/ppermute | solution.py:493
  10.6 0.1 collective-permute-start
  10.7 2.2 %collective-permute-start.5 = (f32[3,8,128]{2,1,0:T(8,128)S(1)}, f32[3,8,128]{2,1,0:T(8,128)S(1)}, u32[]{:S(2)}, u32[]{:S(2)}) collective-permute-start(f32[3,8,128]{2,1,0:T(8,128)S(1)} %get-tuple-element.16), channel_id=1, source_target_pairs={{0,12},{1,13},{2,14},{3,15},{4,8},{5,9},{6,10},{7,11},{8,4},{9,5},... | collective-permute-start | bytes 36872 | tf_op jit(solution)/shard_map/ppermute | solution.py:493
  12.9 0.3 %collective-permute-start.4 = (f32[3,8,128]{2,1,0:T(8,128)S(1)}, f32[3,8,128]{2,1,0:T(8,128)S(1)}, u32[]{:S(2)}, u32[]{:S(2)}) collective-permute-start(f32[3,8,128]{2,1,0:T(8,128)S(1)} %get-tuple-element.16), channel_id=1, source_target_pairs={{0,4},{1,5},{2,6},{3,7},{4,0},{5,1},{6,2},{7,3},{8,12},{9,13},{10,... | collective-permute-start | bytes 36872 | tf_op jit(solution)/shard_map/ppermute | solution.py:493
  13.1 1.0 %collective-permute-done.5.refs_5_ = f32[3,8,128]{2,1,0:T(8,128)S(1)} collective-permute-done((f32[3,8,128]{2,1,0:T(8,128)S(1)}, f32[3,8,128]{2,1,0:T(8,128)S(1)}, u32[]{:S(2)}, u32[]{:S(2)}) %collective-permute-start.5) | collective-permute-done | bytes 12320 | tf_op jit(solution)/shard_map/ppermute | solution.py:493
  14.2 1.6 %collective-permute-start.7 = (f32[3,8,128]{2,1,0:T(8,128)S(1)}, f32[3,8,128]{2,1,0:T(8,128)S(1)}, u32[]{:S(2)}, u32[]{:S(2)}) collective-permute-start(f32[3,8,128]{2,1,0:T(8,128)S(1)} %collective-permute-done.5.refs_5_), channel_id=1, source_target_pairs={{0,16},{1,17},{2,18},{3,19},{4,20},{5,21},{6,22},{7,23},{8,24},{9,... | collective-permute-start | bytes 36872 | tf_op jit(solution)/shard_map/ppermute | solution.py:493
  15.7 0.0 collective-permute-done.4.refs_4_
  15.7 1.5 %collective-permute-start.6 = (f32[3,8,128]{2,1,0:T(8,128)S(1)}, f32[3,8,128]{2,1,0:T(8,128)S(1)}, u32[]{:S(2)}, u32[]{:S(2)}) collective-permute-start(f32[3,8,128]{2,1,0:T(8,128)S(1)} %collective-permute-done.4.refs_4_), channel_id=1, source_target_pairs={{0,16},{1,17},{2,18},{3,19},{4,20},{5,21},{6,22},{7,23},{8,24},{9,... | collective-permute-start | bytes 36872 | tf_op jit(solution)/shard_map/ppermute | solution.py:493
  17.3 0.0 collective-permute-done.7.refs_7_
  17.3 0.8 %collective-permute-done.6.refs_6_ = f32[3,8,128]{2,1,0:T(8,128)S(1)} collective-permute-done((f32[3,8,128]{2,1,0:T(8,128)S(1)}, f32[3,8,128]{2,1,0:T(8,128)S(1)}, u32[]{:S(2)}, u32[]{:S(2)}) %collective-permute-start.6) | collective-permute-done | bytes 12320 | tf_op jit(solution)/shard_map/ppermute | solution.py:493
  18.1 0.0 collective-permute-done.refs_1_
  18.1 0.0 collective-permute-done.3.refs_3_
  18.1 1.5 %shard_map.48 = f32[256,128]{1,0:T(8,128)} custom-call(f32[33,8,128]{2,1,0:T(8,128)S(1)} %get-tuple-element.11.refs_0_, f32[33,8,128]{2,1,0:T(8,128)S(1)} %collective-permute-done.refs_1_, f32[37,8,128]{2,1,0:T(8,128)S(1)} %get-tuple-element.15.refs_2_, f32[37,8,128]{2,1,0:T(8,128)S(1)} %collective-permute-done.3.refs_3_, ...), custom_call_target="tpu_custom_call" | custom-call | flops 10000000 | bytes 753664 | tf_op jit(solution)/shard_map/pallas_call | solution.py:467
Async XLA Ops:
  1.1 4.4 %collective-permute-start.1 = (f32[17,8,128]{2,1,0:T(8,128)S(1)}, f32[17,8,128]{2,1,0:T(8,128)S(1)}, u32[]{:S(2)}, u32[]{:S(2)}) collective-permute-start(f32[17,8,128]{2,1,0:T(8,128)S(1)} %get-tuple-element.13), channel_id=1, source_target_pairs={{0,1},{1,0},{2,3},{3,2},{4,5},{5,4},{6,7},{7,6},{8,9},{9,8},{10,11... | collective-permute-start | bytes 208904 | tf_op jit(solution)/shard_map/ppermute | solution.py:493
  3.3 5.6 %collective-permute-start.2 = (f32[17,8,128]{2,1,0:T(8,128)S(1)}, f32[17,8,128]{2,1,0:T(8,128)S(1)}, u32[]{:S(2)}, u32[]{:S(2)}) collective-permute-start(f32[17,8,128]{2,1,0:T(8,128)S(1)} %get-tuple-element.14), channel_id=1, source_target_pairs={{0,3},{1,2},{2,1},{3,0},{4,7},{5,6},{6,5},{7,4},{8,11},{9,10},{10,... | collective-permute-start | bytes 208904 | tf_op jit(solution)/shard_map/ppermute | solution.py:493
  9.0 9.1 %collective-permute-start.3 = (f32[37,8,128]{2,1,0:T(8,128)S(1)}, f32[37,8,128]{2,1,0:T(8,128)S(1)}, u32[]{:S(2)}, u32[]{:S(2)}) collective-permute-start(f32[37,8,128]{2,1,0:T(8,128)S(1)} %get-tuple-element.15.refs_2_), channel_id=1, source_target_pairs={{0,16},{1,17},{2,18},{3,19},{4,20},{5,21},{6,22},{7,23},{8,24},{9,... | collective-permute-start | bytes 454664 | tf_op jit(solution)/shard_map/ppermute | solution.py:493
  10.6 7.5 %collective-permute-start = (f32[33,8,128]{2,1,0:T(8,128)S(1)}, f32[33,8,128]{2,1,0:T(8,128)S(1)}, u32[]{:S(2)}, u32[]{:S(2)}) collective-permute-start(f32[33,8,128]{2,1,0:T(8,128)S(1)} %get-tuple-element.11.refs_0_), channel_id=1, source_target_pairs={{0,16},{1,17},{2,18},{3,19},{4,20},{5,21},{6,22},{7,23},{8,24},{9,... | collective-permute-start | bytes 405512 | tf_op jit(solution)/shard_map/ppermute | solution.py:493
  10.7 3.4 %collective-permute-start.5 = (f32[3,8,128]{2,1,0:T(8,128)S(1)}, f32[3,8,128]{2,1,0:T(8,128)S(1)}, u32[]{:S(2)}, u32[]{:S(2)}) collective-permute-start(f32[3,8,128]{2,1,0:T(8,128)S(1)} %get-tuple-element.16), channel_id=1, source_target_pairs={{0,12},{1,13},{2,14},{3,15},{4,8},{5,9},{6,10},{7,11},{8,4},{9,5},... | collective-permute-start | bytes 36872 | tf_op jit(solution)/shard_map/ppermute | solution.py:493
  12.9 2.9 %collective-permute-start.4 = (f32[3,8,128]{2,1,0:T(8,128)S(1)}, f32[3,8,128]{2,1,0:T(8,128)S(1)}, u32[]{:S(2)}, u32[]{:S(2)}) collective-permute-start(f32[3,8,128]{2,1,0:T(8,128)S(1)} %get-tuple-element.16), channel_id=1, source_target_pairs={{0,4},{1,5},{2,6},{3,7},{4,0},{5,1},{6,2},{7,3},{8,12},{9,13},{10,... | collective-permute-start | bytes 36872 | tf_op jit(solution)/shard_map/ppermute | solution.py:493
  14.2 3.1 %collective-permute-start.7 = (f32[3,8,128]{2,1,0:T(8,128)S(1)}, f32[3,8,128]{2,1,0:T(8,128)S(1)}, u32[]{:S(2)}, u32[]{:S(2)}) collective-permute-start(f32[3,8,128]{2,1,0:T(8,128)S(1)} %collective-permute-done.5.refs_5_), channel_id=1, source_target_pairs={{0,16},{1,17},{2,18},{3,19},{4,20},{5,21},{6,22},{7,23},{8,24},{9,... | collective-permute-start | bytes 36872 | tf_op jit(solution)/shard_map/ppermute | solution.py:493
  15.7 2.4 %collective-permute-start.6 = (f32[3,8,128]{2,1,0:T(8,128)S(1)}, f32[3,8,128]{2,1,0:T(8,128)S(1)}, u32[]{:S(2)}, u32[]{:S(2)}) collective-permute-start(f32[3,8,128]{2,1,0:T(8,128)S(1)} %collective-permute-done.4.refs_4_), channel_id=1, source_target_pairs={{0,16},{1,17},{2,18},{3,19},{4,20},{5,21},{6,22},{7,23},{8,24},{9,... | collective-permute-start | bytes 36872 | tf_op jit(solution)/shard_map/ppermute | solution.py:493
where the time goes:
time: 20 us; the launch traced here: 19.7 us
  starting transfers between devices  11.6 us (58%)
  waiting for transfers between devices  5.31 us (27%)
  Pallas kernels  2.72 us (14%)
    ppermute x8, starting transfers between devices, send(): return lax.ppermute(value, axes, pairs)  11.6 us
    ppermute x8, waiting for transfers between devices, send(): return lax.ppermute(value, axes, pairs)  5.31 us
    pallas_call x3, Pallas kernels, call(): pl.pallas_call(lambda *refs: kernel(sh, *refs), out_shape=outs, in_specs=...  2.72 us
  transfers between devices with their start and end apart: 8, of which 3 were waited for; matrix products, arithmetic and copies ran while one was open for 0% of the time, Pallas kernels for 0%

commit v1 on v0

--- a/solution.py
+++ b/solution.py
@@ -29,12 +29,12 @@
         self.group = rows // self.cols
         self.per_tile = self.group // (2 * HALO)
         self.half = self.group // 2
-        self.edge_tiles = -(-FIELDS // self.per_tile) + 1
+        self.field_tiles = -(-FIELDS // self.per_tile)
+        self.edge_tiles = 2 * self.field_tiles + 1
         assert self.per_tile >= 2 and self.group >= 4 * HALO and 2 * cx <= lev
         assert self.cols * self.group == rows
         self.mask_tile = FIELDS * cx
         self.halo_tiles = FIELDS * HALO
-        self.edge_base = 2 * self.halo_tiles + 2
 
     def lanes(self):
         return lax.broadcasted_iota(jnp.int32, (self.lev, self.rows), 1)
@@ -44,14 +44,21 @@
 
     def row(self, ref, tile, r):
         return jnp.broadcast_to(ref[tile, r : r + 1, :], (self.lev, self.rows))
+
+    def edge_at(self, comp, ch):
+        t, q = divmod(ch, self.per_tile)
+        return comp * self.field_tiles + t, q
+
+    def halo_at(self, comp, side, ch, d):
+        return (self.halo_tiles if comp != side else 0) + ch * HALO + d
 
     def edge_place(self, acc, value, j, channel, lane):
         at = j * self.group + channel * 2 * HALO + HALO
         return jnp.where((lane >= at - HALO) & (lane < at + HALO), lane_roll(value, at), acc)
 
 
-def pack_kernel(sh, *refs):
-    sources, (x_ref, e_ref, ma_ref, mb_ref), arrived, sem = refs[:4], refs[4:8], refs[8:12], refs[12]
+def load_kernel(sh, *refs):
+    sources, x_ref, arrived, sem = refs[:4], refs[4], refs[5:9], refs[9]
     copies = [
         pltpu.make_async_copy(a, b, sem.at[i]) for i, (a, b) in enumerate(zip(sources, arrived))
     ]
@@ -60,68 +67,97 @@
     for copy in copies:
         copy.wait()
     state_ref, irr_ref, land_ref, bottom_ref = arrived
-    odd = lax.axis_index("gx") % 2 == 1
-    flip = jnp.where(odd & (lax.axis_index("comp") == 0), -1.0, 1.0)
-    lane = sh.lanes()
+    odd = is_odd("gx")
+    own_columns(sh, state_ref, x_ref, odd, first_core())
     cx = sh.cx
-    zero = jnp.zeros((sh.lev, sh.rows), jnp.float32)
-    edges = [zero] * sh.edge_tiles
+    depth = jnp.where(land_ref[...] == 1, bottom_ref[...], 0).astype(jnp.float32)
+    for base, value in ((0, irr_ref[...]), (cx, depth)):
+        for k in range(cx):
+            x_ref[sh.mask_tile, base + k : base + k + 1, :] = jnp.where(
+                odd, value[cx - 1 - k : cx - k, :], value[k : k + 1, :]
+            )
+
+
+def is_odd(axis):
+    return lax.axis_index(axis) % 2 == 1
+
+
+def first_core():
+    return lax.axis_index("comp") == 0
+
+
+def own_columns(sh, state_ref, x_ref, odd, dynamics):
+    flip = jnp.where(odd & dynamics, -1.0, 1.0)
+    cx = sh.cx
     for ch in range(FIELDS):
         raw = [state_ref[pl.ds(ch * sh.lev * cx + i, sh.lev, stride=cx), :] for i in range(cx)]
-        cols = [jnp.where(odd, raw[cx - 1 - k], raw[k]) for k in range(cx)]
-        if ch in VEL_X:
-            cols = [c * flip for c in cols]
-        t, q = divmod(ch, sh.per_tile)
         for k in range(cx):
-            x_ref[ch * cx + k] = cols[k]
-            edges[t] = sh.edge_place(edges[t], cols[k], k + HALO, q, lane)
-        for d in range(HALO):
-            mb_ref[ch * HALO + d] = cols[d]
-            ma_ref[ch * HALO + d] = cols[cx - 1 - d]
-    depth = jnp.where(land_ref[...] == 1, bottom_ref[...], 0).astype(jnp.float32)
-    irr = irr_ref[...]
-    rows = []
-    for value in (irr, depth):
-        rows += [
-            jnp.where(odd, value[cx - 1 - k : cx - k, :], value[k : k + 1, :]) for k in range(cx)
-        ]
-    for r, value in enumerate(rows):
-        x_ref[sh.mask_tile, r : r + 1, :] = value
-        mb_ref[sh.halo_tiles, r : r + 1, :] = value
-        ma_ref[sh.halo_tiles, r : r + 1, :] = value
-        q, k = divmod(r, cx)
-        wide = jnp.broadcast_to(value, (sh.lev, sh.rows))
-        edges[-1] = sh.edge_place(edges[-1], wide, k + HALO, q, lane)
+            value = jnp.where(odd, raw[cx - 1 - k], raw[k])
+            x_ref[ch * cx + k] = value * flip if ch in VEL_X else value
+
+
+def send_kernel(sh, state_ref, xo_ref, xp_ref, m_ref):
+    core0 = first_core()
+    own_columns(sh, state_ref, xp_ref, is_odd("gx"), jnp.logical_not(core0))
+    cx = sh.cx
+    for part, (x_ref, flip) in enumerate(
+        ((xo_ref, jnp.where(core0, -1.0, 1.0)), (xp_ref, jnp.where(core0, 1.0, -1.0)))
+    ):
+        for ch in range(FIELDS):
+            for d in range(HALO):
+                value = jnp.where(core0, x_ref[ch * cx + cx - 1 - d], x_ref[ch * cx + d])
+                m_ref[part * sh.halo_tiles + ch * HALO + d] = value * flip if ch in VEL_X else value
+    m_ref[2 * sh.halo_tiles] = xo_ref[sh.mask_tile]
+
+
+def edge_kernel(sh, xo_ref, xp_ref, e_ref):
+    lane = sh.lanes()
+    core0 = first_core()
+    cx = sh.cx
+    edges = [jnp.zeros((sh.lev, sh.rows), jnp.float32)] * sh.edge_tiles
+    for comp in range(2):
+        for ch in range(FIELDS):
+            t, q = sh.edge_at(comp, ch)
+            for k in range(cx):
+                own, partner = xo_ref[ch * cx + k], xp_ref[ch * cx + k]
+                value = jnp.where(core0, own, partner) if comp == 0 else jnp.where(core0, partner, own)
+                edges[t] = sh.edge_place(edges[t], value, k + HALO, q, lane)
+    for q in range(2):
+        for k in range(cx):
+            value = sh.row(xo_ref, sh.mask_tile, q * cx + k)
+            edges[-1] = sh.edge_place(edges[-1], value, k + HALO, q, lane)
     for t in range(sh.edge_tiles):
         e_ref[t] = edges[t]
 
 
-def merge_kernel(sh, e_ref, ra_ref, rb_ref, eo_ref, h_ref):
-    flip = jnp.where(lax.axis_index("comp") == 0, -1.0, 1.0)
+def merge_kernel(sh, e_ref, rx_ref, rp_ref, eo_ref):
     lane = sh.lanes()
+    core0 = first_core()
     cx = sh.cx
     edges = [e_ref[t] for t in range(sh.edge_tiles)]
     sides = (
-        (ra_ref, 0, lambda d: cx + HALO + d, lambda d: cx - 1 - d),
-        (rb_ref, 1, lambda d: HALO - 1 - d, lambda d: d),
+        (rx_ref, rp_ref, 0, lambda d: cx + HALO + d, lambda d: cx - 1 - d),
+        (rp_ref, rx_ref, 1, lambda d: HALO - 1 - d, lambda d: d),
     )
-    for ref, side, place, source in sides:
-        for ch in range(FIELDS):
-            t, q = divmod(ch, sh.per_tile)
-            for d in range(HALO):
-                value = ref[ch * HALO + d]
-                if ch in VEL_X:
-                    value = value * flip
-                h_ref[side * sh.halo_tiles + ch * HALO + d] = value
-                edges[t] = sh.edge_place(edges[t], value, place(d), q, lane)
-        h_ref[2 * sh.halo_tiles + side] = ref[sh.halo_tiles]
+    for on_first, on_second, side, place, source in sides:
+        for comp in range(2):
+            for ch in range(FIELDS):
+                t, q = sh.edge_at(comp, ch)
+                for d in range(HALO):
+                    at = sh.halo_at(comp, side, ch, d)
+                    value = jnp.where(core0, on_first[at], on_second[at])
+                    edges[t] = sh.edge_place(edges[t], value, place(d), q, lane)
         for q in range(2):
             for d in range(HALO):
-                value = sh.row(ref, sh.halo_tiles, q * cx + source(d))
+                at = q * cx + source(d)
+                value = jnp.where(
+                    core0,
+                    sh.row(on_first, 2 * sh.halo_tiles, at),
+                    sh.row(on_second, 2 * sh.halo_tiles, at),
+                )
                 edges[-1] = sh.edge_place(edges[-1], value, place(d), q, lane)
     for t in range(sh.edge_tiles):
         eo_ref[t] = edges[t]
-        h_ref[sh.edge_base + t] = edges[t]
 
 
 STRIP = "strip"
@@ -159,7 +195,8 @@
         return self.east(site), self.west(site), self.north(site), self.south(site)
 
 
-def step_kernel(sh, xo, xp, ho, hp, rao, rbo, rap, rbp, out_ref, strips, fresh, masks):
+def step_kernel(sh, xo, xp, rx, rp, edges, y, yp, out_ref, strips, fresh, masks):
+    core0 = first_core()
     lane, level = sh.lanes(), sh.levels()
     cx, group = sh.cx, sh.group
     gy, ny = lax.axis_index("gy"), lax.axis_size("gy")
@@ -183,30 +220,34 @@
     def place(site):
         return sh.cols if site == STRIP else site
 
-    def build_strips(h, ra, rb, base, tiles, channels):
+    def build_strips(base, tiles, channels):
         for t in tiles:
-            a, b, mine = ra[t], rb[t], h[sh.edge_base + t]
+            a, b = jnp.where(core0, y[t], yp[t]), jnp.where(core0, yp[t], y[t])
+            mine = edges[t]
             left = jnp.where(gy > 0, jnp.where(even_y, b, a), zero)
             right = jnp.where(gy < ny - 1, jnp.where(even_y, a, b), zero)
             low = jnp.where(slot < HALO, left, mine)
             high = jnp.where(slot < HALO, mine, right)
             for q in range(channels):
                 at = q * 2 * HALO
-                strips[base + (t - tiles[0]) * channels + q] = jnp.where(
+                strips[base + (t - tiles[0]) * sh.per_tile + q] = jnp.where(
                     in_group < sh.half, lane_roll(low, -at), lane_roll(high, sh.half - at)
                 )
 
-    field_tiles = range(sh.edge_tiles - 1)
-    build_strips(ho, rao, rbo, 0, field_tiles, sh.per_tile)
-    build_strips(hp, rap, rbp, FIELDS, field_tiles, sh.per_tile)
-    build_strips(ho, rao, rbo, 2 * FIELDS, [sh.edge_tiles - 1], 2)
+    build_strips(0, range(2 * sh.field_tiles), sh.per_tile)
+    build_strips(2 * FIELDS, [sh.edge_tiles - 1], 2)
 
     def mask_row(kind, j):
         if HALO <= j < HALO + cx:
             return sh.row(xo, sh.mask_tile, kind * cx + j - HALO)
         if j < HALO:
-            return sh.row(ho, 2 * sh.halo_tiles + 1, kind * cx + HALO - 1 - j)
-        return sh.row(ho, 2 * sh.halo_tiles, kind * cx + cx - 1 - (j - HALO - cx))
+            first, second, at = rp, rx, HALO - 1 - j
+        else:
+            first, second, at = rx, rp, cx - 1 - (j - HALO - cx)
+        tile = 2 * sh.halo_tiles
+        return jnp.where(
+            core0, sh.row(first, tile, kind * cx + at), sh.row(second, tile, kind * cx + at)
+        )
 
     levelf = level.astype(jnp.float32)
 
@@ -229,15 +270,15 @@
     def faces(site):
         return [masks[face_base + place(site) * 4 + n] for n in range(4)]
 
-    def raw(x, h, base, ch):
+    def raw(x, sides, comp, ch):
         def col(j):
             if HALO <= j < HALO + cx:
                 return x[ch * cx + j - HALO]
             if j < HALO:
-                return h[sh.halo_tiles + ch * HALO + HALO - 1 - j]
-            return h[ch * HALO + j - HALO - cx]
-
-        return Field(sh, lane, col, lambda: strips[base + ch])
+                return sides[1][sh.halo_at(comp, 1, ch, HALO - 1 - j)]
+            return sides[0][sh.halo_at(comp, 0, ch, j - HALO - cx)]
+
+        return Field(sh, lane, col, lambda: strips[comp * FIELDS + ch])
 
     slots = sh.cols + 1
 
@@ -381,8 +422,8 @@
 
     @pl.when(lax.axis_index("comp") == 0)
     def _():
-        d = [raw(xo, ho, 0, ch) for ch in range(FIELDS)]
-        c = [raw(xp, hp, FIELDS, ch) for ch in range(FIELDS)]
+        d = [raw(xo, (rx, rp), 0, ch) for ch in range(FIELDS)]
+        c = [raw(xp, (rx, rp), 1, ch) for ch in range(FIELDS)]
         extra = FIELDS
         pressure = make_pressure(d, extra + 2, everywhere)
         for site in sites:
@@ -418,8 +459,8 @@
 
     @pl.when(lax.axis_index("comp") != 0)
     def _():
-        d = [raw(xp, hp, FIELDS, ch) for ch in range(FIELDS)]
-        c = [raw(xo, ho, 0, ch) for ch in range(FIELDS)]
+        d = [raw(xp, (rp, rx), 0, ch) for ch in range(FIELDS)]
+        c = [raw(xo, (rp, rx), 1, ch) for ch in range(FIELDS)]
         extra = FIELDS
         pressure = make_pressure(d, extra + 4, everywhere)
         for site in sites:
@@ -495,57 +536,46 @@
     def odd_pair(i, n):
         return (i + 1) % n if i % 2 else (i - 1) % n
 
-    def x_a(v):
-        return send(v, lambda c, y, x: (c, y, x ^ 1))
-
-    def x_b(v):
-        return send(v, lambda c, y, x: (c, y, odd_pair(x, nx)))
-
-    def y_a(v):
-        return send(v, lambda c, y, x: (c, y ^ 1, x))
-
-    def y_b(v):
-        return send(v, lambda c, y, x: (c, odd_pair(y, ny), x))
+    def pair(i, n, core):
+        return i ^ 1 if core == 0 else odd_pair(i, n)
+
+    def along_x(v):
+        return send(v, lambda c, y, x: (c, y, pair(x, nx, c)))
+
+    def along_y(v):
+        return send(v, lambda c, y, x: (c, pair(y, ny, c), x))
 
     def swap(v):
         return send(v, lambda c, y, x: (1 - c, y, x))
 
     flat = ocean_state.reshape(fields * lev * cx, rows)
-    x, e0, ma, mb = call(
-        pack_kernel,
+    partner = swap(flat)
+    inputs = (flat, irradiance, land_mask, bottom_level)
+    (xo,) = call(
+        load_kernel,
         sh,
-        [
-            tiles(sh, fields * cx + 1),
-            tiles(sh, sh.edge_tiles),
-            tiles(sh, sh.halo_tiles + 1),
-            tiles(sh, sh.halo_tiles + 1),
-        ],
-        tuple(pltpu.with_memory_space_constraint(a, pltpu.HBM) for a in (flat, irradiance, land_mask, bottom_level)),
+        [tiles(sh, fields * cx + 1)],
+        tuple(pltpu.with_memory_space_constraint(a, pltpu.HBM) for a in inputs),
         100_000,
-        scratch=[
-            pltpu.VMEM(a.shape, a.dtype) for a in (flat, irradiance, land_mask, bottom_level)
-        ]
-        + [pltpu.SemaphoreType.DMA((4,))],
+        scratch=[pltpu.VMEM(a.shape, a.dtype) for a in inputs] + [pltpu.SemaphoreType.DMA((4,))],
         source=pltpu.HBM,
     )
-    ra, rb = x_a(ma), x_b(mb)
-    xp = swap(x)
-    e1, h = call(
-        merge_kernel,
-        sh,
-        [tiles(sh, sh.edge_tiles), tiles(sh, sh.edge_base + sh.edge_tiles)],
-        (e0, ra, rb),
-        100_000,
+    message = 2 * sh.halo_tiles + 1
+    xp, m = call(
+        send_kernel, sh, [tiles(sh, fields * cx), tiles(sh, message)], (partner, xo), 100_000
     )
-    ya, yb = y_a(e1), y_b(e1)
-    hp = swap(h)
-    yap, ybp = swap(ya), swap(yb)
+    rx = along_x(m)
+    (e0,) = call(edge_kernel, sh, [tiles(sh, sh.edge_tiles)], (xo, xp), 100_000)
+    rp = swap(rx)
+    (e1,) = call(merge_kernel, sh, [tiles(sh, sh.edge_tiles)], (e0, rx, rp), 100_000)
+    y = along_y(e1)
+    yp = swap(y)
     width = sh.cols + 1
     (out,) = call(
         step_kernel,
         sh,
         [jax.ShapeDtypeStruct(flat.shape, jnp.float32)],
-        (x, xp, h, hp, ya, yb, yap, ybp),
+        (xo, xp, rx, rp, e1, y, yp),
         10_000_000,
         scratch=[
             pltpu.VMEM((2 * FIELDS + 2, lev, rows), jnp.float32),

time: 20 us -> 17.3 us (0.86)
  the two profiles are of different devices: /device:TPU:1 before, /device:TPU:0 now
where the time goes in v1:
time: 17.3 us; the launch traced here: 17.1 us
  starting transfers between devices  7.29 us (42%)
  waiting for transfers between devices  7.11 us (41%)
  Pallas kernels  2.71 us (16%)
    ppermute x5, starting transfers between devices, send(): return lax.ppermute(value, axes, pairs)  7.29 us
    ppermute x5, waiting for transfers between devices, send(): return lax.ppermute(value, axes, pairs)  7.11 us
    pallas_call x5, Pallas kernels, call(): pl.pallas_call(lambda *refs: kernel(sh, *refs), out_shape=outs, in_specs=...  2.71 us
  transfers between devices with their start and end apart: 5, of which 5 were waited for; matrix products, arithmetic and copies ran while one was open for 0% of the time, Pallas kernels for 7%

profile of v1, /device:TPU:0, one launch (start us, length us, event | category | flops | bytes accessed | tf_op | source)
XLA Modules:
  0.0 17.1 jit_solution(11904951795761424604)
XLA Ops:
  0.0 0.5 %collective-permute-start = (f32[256,128]{1,0:T(8,128)}, f32[256,128]{1,0:T(8,128)S(1)}, u32[]{:S(2)}, u32[]{:S(2)}) collective-permute-start(f32[256,128]{1,0:T(8,128)} %bitcast.2), channel_id=1, source_target_pairs={{0,16},{1,17},{2,18},{3,19},{4,20},{5,21},{6,22},{7,23},{8,24},{9,... | collective-permute-start | bytes 393224 | tf_op jit(solution)/shard_map/ppermute | solution.py:534
  0.5 1.0 %shard_map.46.refs_1_.refs_0_ = f32[33,8,128]{2,1,0:T(8,128)S(1)} custom-call(f32[256,128]{1,0:T(8,128)} %bitcast.3, f32[4,128]{1,0:T(4,128)} %refs_1_.1, s32[4,128]{1,0:T(4,128)} %refs_2_.1, s32[4,128]{1,0:T(4,128)} %refs_3_.1), custom_call_target="tpu_custom_call" | custom-call | flops 100000 | bytes 272384 | tf_op jit(solution)/shard_map/pallas_call | solution.py:508
  1.5 0.2 %collective-permute-done.refs_0_ = f32[256,128]{1,0:T(8,128)S(1)} collective-permute-done((f32[256,128]{1,0:T(8,128)}, f32[256,128]{1,0:T(8,128)S(1)}, u32[]{:S(2)}, u32[]{:S(2)}) %collective-permute-start) | collective-permute-done | bytes 131104 | tf_op jit(solution)/shard_map/ppermute | solution.py:534
  1.7 3.0 %collective-permute-start.1 = (f32[33,8,128]{2,1,0:T(8,128)S(1)}, f32[33,8,128]{2,1,0:T(8,128)S(1)}, u32[]{:S(2)}, u32[]{:S(2)}) collective-permute-start(f32[33,8,128]{2,1,0:T(8,128)S(1)} %get-tuple-element.8), channel_id=1, source_target_pairs={{0,1},{1,0},{2,3},{3,2},{4,5},{5,4},{6,7},{7,6},{8,9},{9,8},{10,11... | collective-permute-start | bytes 405512 | tf_op jit(solution)/shard_map/ppermute | solution.py:534
  4.7 3.0 %collective-permute-done.1.refs_1_.refs_2_ = f32[33,8,128]{2,1,0:T(8,128)S(1)} collective-permute-done((f32[33,8,128]{2,1,0:T(8,128)S(1)}, f32[33,8,128]{2,1,0:T(8,128)S(1)}, u32[]{:S(2)}, u32[]{:S(2)}) %collective-permute-start.1) | collective-permute-done | bytes 135200 | tf_op jit(solution)/shard_map/ppermute | solution.py:534
  7.7 1.8 %collective-permute-start.2 = (f32[33,8,128]{2,1,0:T(8,128)S(1)}, f32[33,8,128]{2,1,0:T(8,128)S(1)}, u32[]{:S(2)}, u32[]{:S(2)}) collective-permute-start(f32[33,8,128]{2,1,0:T(8,128)S(1)} %collective-permute-done.1.refs_1_.refs_2_), channel_id=1, source_target_pairs={{0,16},{1,17},{2,18},{3,19},{4,20},{5,21},{6,22},{7,23},{8,24},{9,... | collective-permute-start | bytes 405512 | tf_op jit(solution)/shard_map/ppermute | solution.py:534
  9.5 0.1 shard_map.48.refs_0_
  9.7 0.8 %collective-permute-done.2.refs_2_.refs_3_ = f32[33,8,128]{2,1,0:T(8,128)S(1)} collective-permute-done((f32[33,8,128]{2,1,0:T(8,128)S(1)}, f32[33,8,128]{2,1,0:T(8,128)S(1)}, u32[]{:S(2)}, u32[]{:S(2)}) %collective-permute-start.2) | collective-permute-done | bytes 135200 | tf_op jit(solution)/shard_map/ppermute | solution.py:534
  10.5 0.2 shard_map.49.refs_4_
  10.7 1.9 %collective-permute-start.3 = (f32[5,8,128]{2,1,0:T(8,128)S(1)}, f32[5,8,128]{2,1,0:T(8,128)S(1)}, u32[]{:S(2)}, u32[]{:S(2)}) collective-permute-start(f32[5,8,128]{2,1,0:T(8,128)S(1)} %shard_map.49.refs_4_), channel_id=1, source_target_pairs={{0,4},{1,5},{2,6},{3,7},{4,0},{5,1},{6,2},{7,3},{8,12},{9,13},{10,... | collective-permute-start | bytes 61448 | tf_op jit(solution)/shard_map/ppermute | solution.py:534
  12.5 2.0 %collective-permute-done.3.refs_5_ = f32[5,8,128]{2,1,0:T(8,128)S(1)} collective-permute-done((f32[5,8,128]{2,1,0:T(8,128)S(1)}, f32[5,8,128]{2,1,0:T(8,128)S(1)}, u32[]{:S(2)}, u32[]{:S(2)}) %collective-permute-start.3) | collective-permute-done | bytes 20512 | tf_op jit(solution)/shard_map/ppermute | solution.py:534
  14.5 0.1 collective-permute-start.4
  14.6 1.1 %collective-permute-done.4.refs_6_ = f32[5,8,128]{2,1,0:T(8,128)S(1)} collective-permute-done((f32[5,8,128]{2,1,0:T(8,128)S(1)}, f32[5,8,128]{2,1,0:T(8,128)S(1)}, u32[]{:S(2)}, u32[]{:S(2)}) %collective-permute-start.4) | collective-permute-done | bytes 20512 | tf_op jit(solution)/shard_map/ppermute | solution.py:534
  15.7 1.4 %shard_map.50 = f32[256,128]{1,0:T(8,128)} custom-call(f32[33,8,128]{2,1,0:T(8,128)S(1)} %shard_map.46.refs_1_.refs_0_, f32[32,8,128]{2,1,0:T(8,128)S(1)} %get-tuple-element.7.refs_1_, f32[33,8,128]{2,1,0:T(8,128)S(1)} %collective-permute-done.1.refs_1_.refs_2_, f32[33,8,128]{2,1,0:T(8,128)S(1)} %collective-permute-done.2.refs_2_.refs_3_, ...), custom_call_target="tpu_custom_call" | custom-call | flops 10000000 | bytes 729088 | tf_op jit(solution)/shard_map/pallas_call | solution.py:508
  (1 shorter events, 0.0 us)
Async XLA Ops:
  0.0 1.7 %collective-permute-start = (f32[256,128]{1,0:T(8,128)}, f32[256,128]{1,0:T(8,128)S(1)}, u32[]{:S(2)}, u32[]{:S(2)}) collective-permute-start(f32[256,128]{1,0:T(8,128)} %bitcast.2), channel_id=1, source_target_pairs={{0,16},{1,17},{2,18},{3,19},{4,20},{5,21},{6,22},{7,23},{8,24},{9,... | collective-permute-start | bytes 393224 | tf_op jit(solution)/shard_map/ppermute | solution.py:534
  1.7 6.0 %collective-permute-start.1 = (f32[33,8,128]{2,1,0:T(8,128)S(1)}, f32[33,8,128]{2,1,0:T(8,128)S(1)}, u32[]{:S(2)}, u32[]{:S(2)}) collective-permute-start(f32[33,8,128]{2,1,0:T(8,128)S(1)} %get-tuple-element.8), channel_id=1, source_target_pairs={{0,1},{1,0},{2,3},{3,2},{4,5},{5,4},{6,7},{7,6},{8,9},{9,8},{10,11... | collective-permute-start | bytes 405512 | tf_op jit(solution)/shard_map/ppermute | solution.py:534
  7.7 2.8 %collective-permute-start.2 = (f32[33,8,128]{2,1,0:T(8,128)S(1)}, f32[33,8,128]{2,1,0:T(8,128)S(1)}, u32[]{:S(2)}, u32[]{:S(2)}) collective-permute-start(f32[33,8,128]{2,1,0:T(8,128)S(1)} %collective-permute-done.1.refs_1_.refs_2_), channel_id=1, source_target_pairs={{0,16},{1,17},{2,18},{3,19},{4,20},{5,21},{6,22},{7,23},{8,24},{9,... | collective-permute-start | bytes 405512 | tf_op jit(solution)/shard_map/ppermute | solution.py:534
  10.7 3.8 %collective-permute-start.3 = (f32[5,8,128]{2,1,0:T(8,128)S(1)}, f32[5,8,128]{2,1,0:T(8,128)S(1)}, u32[]{:S(2)}, u32[]{:S(2)}) collective-permute-start(f32[5,8,128]{2,1,0:T(8,128)S(1)} %shard_map.49.refs_4_), channel_id=1, source_target_pairs={{0,4},{1,5},{2,6},{3,7},{4,0},{5,1},{6,2},{7,3},{8,12},{9,13},{10,... | collective-permute-start | bytes 61448 | tf_op jit(solution)/shard_map/ppermute | solution.py:534
  14.5 1.2 %collective-permute-start.4 = (f32[5,8,128]{2,1,0:T(8,128)S(1)}, f32[5,8,128]{2,1,0:T(8,128)S(1)}, u32[]{:S(2)}, u32[]{:S(2)}) collective-permute-start(f32[5,8,128]{2,1,0:T(8,128)S(1)} %collective-permute-done.3.refs_5_), channel_id=1, source_target_pairs={{0,16},{1,17},{2,18},{3,19},{4,20},{5,21},{6,22},{7,23},{8,24},{9,... | collective-permute-start | bytes 61448 | tf_op jit(solution)/shard_map/ppermute | solution.py:534

commit v2 on v1

--- a/solution.py
+++ b/solution.py
@@ -50,7 +50,7 @@
         return comp * self.field_tiles + t, q
 
     def halo_at(self, comp, side, ch, d):
-        return (self.halo_tiles if comp != side else 0) + ch * HALO + d
+        return (self.halo_tiles if comp == side else 0) + ch * HALO + d
 
     def edge_place(self, acc, value, j, channel, lane):
         at = j * self.group + channel * 2 * HALO + HALO
@@ -58,7 +58,7 @@
 
 
 def load_kernel(sh, *refs):
-    sources, x_ref, arrived, sem = refs[:4], refs[4], refs[5:9], refs[9]
+    sources, x_ref, e_ref, arrived, sem = refs[:4], refs[4], refs[5], refs[6:10], refs[10]
     copies = [
         pltpu.make_async_copy(a, b, sem.at[i]) for i, (a, b) in enumerate(zip(sources, arrived))
     ]
@@ -68,14 +68,19 @@
         copy.wait()
     state_ref, irr_ref, land_ref, bottom_ref = arrived
     odd = is_odd("gx")
-    own_columns(sh, state_ref, x_ref, odd, first_core())
+    edges = own_columns(sh, state_ref, x_ref, odd, first_core())
     cx = sh.cx
+    lane = sh.lanes()
     depth = jnp.where(land_ref[...] == 1, bottom_ref[...], 0).astype(jnp.float32)
-    for base, value in ((0, irr_ref[...]), (cx, depth)):
+    last = jnp.zeros((sh.lev, sh.rows), jnp.float32)
+    for q, value in enumerate((irr_ref[...], depth)):
         for k in range(cx):
-            x_ref[sh.mask_tile, base + k : base + k + 1, :] = jnp.where(
-                odd, value[cx - 1 - k : cx - k, :], value[k : k + 1, :]
-            )
+            row = jnp.where(odd, value[cx - 1 - k : cx - k, :], value[k : k + 1, :])
+            x_ref[sh.mask_tile, q * cx + k : q * cx + k + 1, :] = row
+            wide = jnp.broadcast_to(row, (sh.lev, sh.rows))
+            last = sh.edge_place(last, wide, k + HALO, q, lane)
+    for t, edge in enumerate(edges + [last]):
+        e_ref[t] = edge
 
 
 def is_odd(axis):
@@ -89,75 +94,56 @@
 def own_columns(sh, state_ref, x_ref, odd, dynamics):
     flip = jnp.where(odd & dynamics, -1.0, 1.0)
     cx = sh.cx
+    lane = sh.lanes()
+    edges = [jnp.zeros((sh.lev, sh.rows), jnp.float32)] * sh.field_tiles
     for ch in range(FIELDS):
         raw = [state_ref[pl.ds(ch * sh.lev * cx + i, sh.lev, stride=cx), :] for i in range(cx)]
+        t, q = sh.edge_at(0, ch)
         for k in range(cx):
             value = jnp.where(odd, raw[cx - 1 - k], raw[k])
-            x_ref[ch * cx + k] = value * flip if ch in VEL_X else value
-
-
-def send_kernel(sh, state_ref, xo_ref, xp_ref, m_ref):
+            if ch in VEL_X:
+                value = value * flip
+            x_ref[ch * cx + k] = value
+            edges[t] = sh.edge_place(edges[t], value, k + HALO, q, lane)
+    return edges
+
+
+def send_kernel(sh, state_ref, xo_ref, eo_ref, xp_ref, e_ref, m_ref):
     core0 = first_core()
-    own_columns(sh, state_ref, xp_ref, is_odd("gx"), jnp.logical_not(core0))
+    edges = own_columns(sh, state_ref, xp_ref, is_odd("gx"), jnp.logical_not(core0))
     cx = sh.cx
+    for t in range(sh.field_tiles):
+        own = eo_ref[t]
+        e_ref[t] = jnp.where(core0, own, edges[t])
+        e_ref[sh.field_tiles + t] = jnp.where(core0, edges[t], own)
+    e_ref[sh.edge_tiles - 1] = eo_ref[sh.field_tiles]
     for part, (x_ref, flip) in enumerate(
         ((xo_ref, jnp.where(core0, -1.0, 1.0)), (xp_ref, jnp.where(core0, 1.0, -1.0)))
     ):
         for ch in range(FIELDS):
             for d in range(HALO):
-                value = jnp.where(core0, x_ref[ch * cx + cx - 1 - d], x_ref[ch * cx + d])
+                value = jnp.where(core0, x_ref[ch * cx + d], x_ref[ch * cx + cx - 1 - d])
                 m_ref[part * sh.halo_tiles + ch * HALO + d] = value * flip if ch in VEL_X else value
     m_ref[2 * sh.halo_tiles] = xo_ref[sh.mask_tile]
 
 
-def edge_kernel(sh, xo_ref, xp_ref, e_ref):
+def merge_kernel(sh, e_ref, a_ref, b_ref, eo_ref):
     lane = sh.lanes()
     core0 = first_core()
-    cx = sh.cx
-    edges = [jnp.zeros((sh.lev, sh.rows), jnp.float32)] * sh.edge_tiles
-    for comp in range(2):
-        for ch in range(FIELDS):
-            t, q = sh.edge_at(comp, ch)
-            for k in range(cx):
-                own, partner = xo_ref[ch * cx + k], xp_ref[ch * cx + k]
-                value = jnp.where(core0, own, partner) if comp == 0 else jnp.where(core0, partner, own)
-                edges[t] = sh.edge_place(edges[t], value, k + HALO, q, lane)
-    for q in range(2):
-        for k in range(cx):
-            value = sh.row(xo_ref, sh.mask_tile, q * cx + k)
-            edges[-1] = sh.edge_place(edges[-1], value, k + HALO, q, lane)
+    column, place = lane // sh.group, lane % sh.group // (2 * HALO)
     for t in range(sh.edge_tiles):
-        e_ref[t] = edges[t]
-
-
-def merge_kernel(sh, e_ref, rx_ref, rp_ref, eo_ref):
-    lane = sh.lanes()
-    core0 = first_core()
-    cx = sh.cx
-    edges = [e_ref[t] for t in range(sh.edge_tiles)]
-    sides = (
-        (rx_ref, rp_ref, 0, lambda d: cx + HALO + d, lambda d: cx - 1 - d),
-        (rp_ref, rx_ref, 1, lambda d: HALO - 1 - d, lambda d: d),
-    )
-    for on_first, on_second, side, place, source in sides:
-        for comp in range(2):
-            for ch in range(FIELDS):
-                t, q = sh.edge_at(comp, ch)
-                for d in range(HALO):
-                    at = sh.halo_at(comp, side, ch, d)
-                    value = jnp.where(core0, on_first[at], on_second[at])
-                    edges[t] = sh.edge_place(edges[t], value, place(d), q, lane)
-        for q in range(2):
-            for d in range(HALO):
-                at = q * cx + source(d)
-                value = jnp.where(
-                    core0,
-                    sh.row(on_first, 2 * sh.halo_tiles, at),
-                    sh.row(on_second, 2 * sh.halo_tiles, at),
-                )
-                edges[-1] = sh.edge_place(edges[-1], value, place(d), q, lane)
-    for t in range(sh.edge_tiles):
-        eo_ref[t] = edges[t]
+        got = a_ref[t], b_ref[t]
+        after, before = jnp.where(core0, got[0], got[1]), jnp.where(core0, got[1], got[0])
+        for ch in VEL_X:
+            if sh.edge_at(0, ch)[0] == t:
+                flip = jnp.where(place == sh.edge_at(0, ch)[1], -1.0, 1.0)
+                after, before = after * flip, before * flip
+        edge = e_ref[t]
+        for d in range(HALO):
+            shift = (2 * d + 1) * sh.group
+            edge = jnp.where(column == sh.cx + HALO + d, lane_roll(after, shift), edge)
+            edge = jnp.where(column == HALO - 1 - d, lane_roll(before, -shift), edge)
+        eo_ref[t] = edge
 
 
 STRIP = "strip"
@@ -241,9 +227,9 @@
         if HALO <= j < HALO + cx:
             return sh.row(xo, sh.mask_tile, kind * cx + j - HALO)
         if j < HALO:
-            first, second, at = rp, rx, HALO - 1 - j
+            first, second, at = rx, rp, HALO - 1 - j
         else:
-            first, second, at = rx, rp, cx - 1 - (j - HALO - cx)
+            first, second, at = rp, rx, cx - 1 - (j - HALO - cx)
         tile = 2 * sh.halo_tiles
         return jnp.where(
             core0, sh.row(first, tile, kind * cx + at), sh.row(second, tile, kind * cx + at)
@@ -422,8 +408,8 @@
 
     @pl.when(lax.axis_index("comp") == 0)
     def _():
-        d = [raw(xo, (rx, rp), 0, ch) for ch in range(FIELDS)]
-        c = [raw(xp, (rx, rp), 1, ch) for ch in range(FIELDS)]
+        d = [raw(xo, (rp, rx), 0, ch) for ch in range(FIELDS)]
+        c = [raw(xp, (rp, rx), 1, ch) for ch in range(FIELDS)]
         extra = FIELDS
         pressure = make_pressure(d, extra + 2, everywhere)
         for site in sites:
@@ -459,8 +445,8 @@
 
     @pl.when(lax.axis_index("comp") != 0)
     def _():
-        d = [raw(xp, (rp, rx), 0, ch) for ch in range(FIELDS)]
-        c = [raw(xo, (rp, rx), 1, ch) for ch in range(FIELDS)]
+        d = [raw(xp, (rx, rp), 0, ch) for ch in range(FIELDS)]
+        c = [raw(xo, (rx, rp), 1, ch) for ch in range(FIELDS)]
         extra = FIELDS
         pressure = make_pressure(d, extra + 4, everywhere)
         for site in sites:
@@ -539,8 +525,11 @@
     def pair(i, n, core):
         return i ^ 1 if core == 0 else odd_pair(i, n)
 
-    def along_x(v):
+    def edges_x(v):
         return send(v, lambda c, y, x: (c, y, pair(x, nx, c)))
+
+    def bulk_x(v):
+        return send(v, lambda c, y, x: (c, y, pair(x, nx, 1 - c)))
 
     def along_y(v):
         return send(v, lambda c, y, x: (c, pair(y, ny, c), x))
@@ -551,24 +540,25 @@
     flat = ocean_state.reshape(fields * lev * cx, rows)
     partner = swap(flat)
     inputs = (flat, irradiance, land_mask, bottom_level)
-    (xo,) = call(
+    xo, eo = call(
         load_kernel,
         sh,
-        [tiles(sh, fields * cx + 1)],
+        [tiles(sh, fields * cx + 1), tiles(sh, sh.field_tiles + 1)],
         tuple(pltpu.with_memory_space_constraint(a, pltpu.HBM) for a in inputs),
         100_000,
         scratch=[pltpu.VMEM(a.shape, a.dtype) for a in inputs] + [pltpu.SemaphoreType.DMA((4,))],
         source=pltpu.HBM,
     )
-    message = 2 * sh.halo_tiles + 1
-    xp, m = call(
-        send_kernel, sh, [tiles(sh, fields * cx), tiles(sh, message)], (partner, xo), 100_000
+    edge, message = tiles(sh, sh.edge_tiles), tiles(sh, 2 * sh.halo_tiles + 1)
+    xp, e0, m = call(
+        send_kernel, sh, [tiles(sh, fields * cx), edge, message], (partner, xo, eo), 100_000
     )
-    rx = along_x(m)
-    (e0,) = call(edge_kernel, sh, [tiles(sh, sh.edge_tiles)], (xo, xp), 100_000)
+    ex = edges_x(e0)
+    rx = bulk_x(m)
+    ep = swap(ex)
+    (e1,) = call(merge_kernel, sh, [edge], (e0, ex, ep), 10_000)
+    y = along_y(e1)
     rp = swap(rx)
-    (e1,) = call(merge_kernel, sh, [tiles(sh, sh.edge_tiles)], (e0, rx, rp), 100_000)
-    y = along_y(e1)
     yp = swap(y)
     width = sh.cols + 1
     (out,) = call(

time: 17.3 us -> 23.4 us (1.35)
  the two profiles are of different devices: /device:TPU:0 before, /device:TPU:1 now
where the time goes in v2:
time: 23.4 us; the launch traced here: 23 us
  starting transfers between devices  12 us (51%)
  waiting for transfers between devices  8.23 us (35%)
  Pallas kernels  2.79 us (12%)
    ppermute x7, starting transfers between devices, send(): return lax.ppermute(value, axes, pairs)  12 us
    ppermute x7, waiting for transfers between devices, send(): return lax.ppermute(value, axes, pairs)  8.23 us
    pallas_call x4, Pallas kernels, call(): pl.pallas_call(lambda *refs: kernel(sh, *refs), out_shape=outs, in_specs=...  2.79 us
  transfers between devices with their start and end apart: 7, of which 6 were waited for; matrix products, arithmetic and copies ran while one was open for 0% of the time, Pallas kernels for 5%

profile of v2, /device:TPU:1, one launch (start us, length us, event | category | flops | bytes accessed | tf_op | source)
XLA Modules:
  0.0 23.0 jit_solution(9660054344575057513)
XLA Ops:
  0.0 0.0 collective-permute-start
  0.0 1.1 %shard_map.46 = (f32[33,8,128]{2,1,0:T(8,128)S(1)}, f32[3,8,128]{2,1,0:T(8,128)S(1)}) custom-call(f32[256,128]{1,0:T(8,128)} %bitcast.3, f32[4,128]{1,0:T(4,128)} %refs_1_.1, s32[4,128]{1,0:T(4,128)} %refs_2_.1, s32[4,128]{1,0:T(4,128)} %refs_3_.1), custom_call_target="tpu_custom_call" | custom-call | flops 100000 | bytes 284672 | tf_op jit(solution)/shard_map/pallas_call | solution.py:494
  1.1 0.5 %collective-permute-done.refs_0_ = f32[256,128]{1,0:T(8,128)S(1)} collective-permute-done((f32[256,128]{1,0:T(8,128)}, f32[256,128]{1,0:T(8,128)S(1)}, u32[]{:S(2)}, u32[]{:S(2)}) %collective-permute-start) | collective-permute-done | bytes 131104 | tf_op jit(solution)/shard_map/ppermute | solution.py:520
  1.6 0.1 shard_map.47
  1.7 2.5 %collective-permute-start.1 = (f32[33,8,128]{2,1,0:T(8,128)S(1)}, f32[33,8,128]{2,1,0:T(8,128)S(1)}, u32[]{:S(2)}, u32[]{:S(2)}) collective-permute-start(f32[33,8,128]{2,1,0:T(8,128)S(1)} %get-tuple-element.13), channel_id=1, source_target_pairs={{0,3},{1,2},{2,1},{3,0},{4,7},{5,6},{6,5},{7,4},{8,11},{9,10},{10,... | collective-permute-start | bytes 405512 | tf_op jit(solution)/shard_map/ppermute | solution.py:520
  4.2 2.4 %collective-permute-done.1.refs_2_ = f32[33,8,128]{2,1,0:T(8,128)S(1)} collective-permute-done((f32[33,8,128]{2,1,0:T(8,128)S(1)}, f32[33,8,128]{2,1,0:T(8,128)S(1)}, u32[]{:S(2)}, u32[]{:S(2)}) %collective-permute-start.1) | collective-permute-done | bytes 135200 | tf_op jit(solution)/shard_map/ppermute | solution.py:520
  6.6 4.3 %collective-permute-start.2 = (f32[33,8,128]{2,1,0:T(8,128)S(1)}, f32[33,8,128]{2,1,0:T(8,128)S(1)}, u32[]{:S(2)}, u32[]{:S(2)}) collective-permute-start(f32[33,8,128]{2,1,0:T(8,128)S(1)} %collective-permute-done.1.refs_2_), channel_id=1, source_target_pairs={{0,16},{1,17},{2,18},{3,19},{4,20},{5,21},{6,22},{7,23},{8,24},{9,... | collective-permute-start | bytes 405512 | tf_op jit(solution)/shard_map/ppermute | solution.py:520
  10.9 2.5 %collective-permute-start.3 = (f32[5,8,128]{2,1,0:T(8,128)S(1)}, f32[5,8,128]{2,1,0:T(8,128)S(1)}, u32[]{:S(2)}, u32[]{:S(2)}) collective-permute-start(f32[5,8,128]{2,1,0:T(8,128)S(1)} %get-tuple-element.14.refs_0_), channel_id=1, source_target_pairs={{0,1},{1,0},{2,3},{3,2},{4,5},{5,4},{6,7},{7,6},{8,9},{9,8},{10,11... | collective-permute-start | bytes 61448 | tf_op jit(solution)/shard_map/ppermute | solution.py:520
  13.4 2.0 %collective-permute-done.3.refs_1_ = f32[5,8,128]{2,1,0:T(8,128)S(1)} collective-permute-done((f32[5,8,128]{2,1,0:T(8,128)S(1)}, f32[5,8,128]{2,1,0:T(8,128)S(1)}, u32[]{:S(2)}, u32[]{:S(2)}) %collective-permute-start.3) | collective-permute-done | bytes 20512 | tf_op jit(solution)/shard_map/ppermute | solution.py:520
  15.3 0.0 collective-permute-start.4
  15.3 1.2 %collective-permute-done.4.refs_2_ = f32[5,8,128]{2,1,0:T(8,128)S(1)} collective-permute-done((f32[5,8,128]{2,1,0:T(8,128)S(1)}, f32[5,8,128]{2,1,0:T(8,128)S(1)}, u32[]{:S(2)}, u32[]{:S(2)}) %collective-permute-start.4) | collective-permute-done | bytes 20512 | tf_op jit(solution)/shard_map/ppermute | solution.py:520
  16.5 0.1 shard_map.48.refs_4_
  16.6 2.2 %collective-permute-start.5 = (f32[5,8,128]{2,1,0:T(8,128)S(1)}, f32[5,8,128]{2,1,0:T(8,128)S(1)}, u32[]{:S(2)}, u32[]{:S(2)}) collective-permute-start(f32[5,8,128]{2,1,0:T(8,128)S(1)} %shard_map.48.refs_4_), channel_id=1, source_target_pairs={{0,4},{1,5},{2,6},{3,7},{4,0},{5,1},{6,2},{7,3},{8,12},{9,13},{10,... | collective-permute-start | bytes 61448 | tf_op jit(solution)/shard_map/ppermute | solution.py:520
  18.8 1.4 %collective-permute-done.5.refs_5_ = f32[5,8,128]{2,1,0:T(8,128)S(1)} collective-permute-done((f32[5,8,128]{2,1,0:T(8,128)S(1)}, f32[5,8,128]{2,1,0:T(8,128)S(1)}, u32[]{:S(2)}, u32[]{:S(2)}) %collective-permute-start.5) | collective-permute-done | bytes 20512 | tf_op jit(solution)/shard_map/ppermute | solution.py:520
  20.2 0.4 %collective-permute-start.6 = (f32[5,8,128]{2,1,0:T(8,128)S(1)}, f32[5,8,128]{2,1,0:T(8,128)S(1)}, u32[]{:S(2)}, u32[]{:S(2)}) collective-permute-start(f32[5,8,128]{2,1,0:T(8,128)S(1)} %collective-permute-done.5.refs_5_), channel_id=1, source_target_pairs={{0,16},{1,17},{2,18},{3,19},{4,20},{5,21},{6,22},{7,23},{8,24},{9,... | collective-permute-start | bytes 61448 | tf_op jit(solution)/shard_map/ppermute | solution.py:520
  20.6 0.8 %collective-permute-done.6.refs_6_ = f32[5,8,128]{2,1,0:T(8,128)S(1)} collective-permute-done((f32[5,8,128]{2,1,0:T(8,128)S(1)}, f32[5,8,128]{2,1,0:T(8,128)S(1)}, u32[]{:S(2)}, u32[]{:S(2)}) %collective-permute-start.6) | collective-permute-done | bytes 20512 | tf_op jit(solution)/shard_map/ppermute | solution.py:520
  21.5 0.0 collective-permute-done.2.refs_3_
  21.5 1.5 %shard_map.49 = f32[256,128]{1,0:T(8,128)} custom-call(f32[33,8,128]{2,1,0:T(8,128)S(1)} %get-tuple-element.10.refs_1_.refs_0_, f32[32,8,128]{2,1,0:T(8,128)S(1)} %get-tuple-element.12.refs_1_, f32[33,8,128]{2,1,0:T(8,128)S(1)} %collective-permute-done.1.refs_2_, f32[33,8,128]{2,1,0:T(8,128)S(1)} %collective-permute-done.2.refs_3_, ...), custom_call_target="tpu_custom_call" | custom-call | flops 10000000 | bytes 729088 | tf_op jit(solution)/shard_map/pallas_call | solution.py:494
Async XLA Ops:
  0.0 1.6 %collective-permute-start = (f32[256,128]{1,0:T(8,128)}, f32[256,128]{1,0:T(8,128)S(1)}, u32[]{:S(2)}, u32[]{:S(2)}) collective-permute-start(f32[256,128]{1,0:T(8,128)} %bitcast.2), channel_id=1, source_target_pairs={{0,16},{1,17},{2,18},{3,19},{4,20},{5,21},{6,22},{7,23},{8,24},{9,... | collective-permute-start | bytes 393224 | tf_op jit(solution)/shard_map/ppermute | solution.py:520
  1.7 4.9 %collective-permute-start.1 = (f32[33,8,128]{2,1,0:T(8,128)S(1)}, f32[33,8,128]{2,1,0:T(8,128)S(1)}, u32[]{:S(2)}, u32[]{:S(2)}) collective-permute-start(f32[33,8,128]{2,1,0:T(8,128)S(1)} %get-tuple-element.13), channel_id=1, source_target_pairs={{0,3},{1,2},{2,1},{3,0},{4,7},{5,6},{6,5},{7,4},{8,11},{9,10},{10,... | collective-permute-start | bytes 405512 | tf_op jit(solution)/shard_map/ppermute | solution.py:520
  6.6 14.9 %collective-permute-start.2 = (f32[33,8,128]{2,1,0:T(8,128)S(1)}, f32[33,8,128]{2,1,0:T(8,128)S(1)}, u32[]{:S(2)}, u32[]{:S(2)}) collective-permute-start(f32[33,8,128]{2,1,0:T(8,128)S(1)} %collective-permute-done.1.refs_2_), channel_id=1, source_target_pairs={{0,16},{1,17},{2,18},{3,19},{4,20},{5,21},{6,22},{7,23},{8,24},{9,... | collective-permute-start | bytes 405512 | tf_op jit(solution)/shard_map/ppermute | solution.py:520
  10.9 4.4 %collective-permute-start.3 = (f32[5,8,128]{2,1,0:T(8,128)S(1)}, f32[5,8,128]{2,1,0:T(8,128)S(1)}, u32[]{:S(2)}, u32[]{:S(2)}) collective-permute-start(f32[5,8,128]{2,1,0:T(8,128)S(1)} %get-tuple-element.14.refs_0_), channel_id=1, source_target_pairs={{0,1},{1,0},{2,3},{3,2},{4,5},{5,4},{6,7},{7,6},{8,9},{9,8},{10,11... | collective-permute-start | bytes 61448 | tf_op jit(solution)/shard_map/ppermute | solution.py:520
  15.3 1.2 %collective-permute-start.4 = (f32[5,8,128]{2,1,0:T(8,128)S(1)}, f32[5,8,128]{2,1,0:T(8,128)S(1)}, u32[]{:S(2)}, u32[]{:S(2)}) collective-permute-start(f32[5,8,128]{2,1,0:T(8,128)S(1)} %collective-permute-done.3.refs_1_), channel_id=1, source_target_pairs={{0,16},{1,17},{2,18},{3,19},{4,20},{5,21},{6,22},{7,23},{8,24},{9,... | collective-permute-start | bytes 61448 | tf_op jit(solution)/shard_map/ppermute | solution.py:520
  16.6 3.6 %collective-permute-start.5 = (f32[5,8,128]{2,1,0:T(8,128)S(1)}, f32[5,8,128]{2,1,0:T(8,128)S(1)}, u32[]{:S(2)}, u32[]{:S(2)}) collective-permute-start(f32[5,8,128]{2,1,0:T(8,128)S(1)} %shard_map.48.refs_4_), channel_id=1, source_target_pairs={{0,4},{1,5},{2,6},{3,7},{4,0},{5,1},{6,2},{7,3},{8,12},{9,13},{10,... | collective-permute-start | bytes 61448 | tf_op jit(solution)/shard_map/ppermute | solution.py:520
  20.2 1.3 %collective-permute-start.6 = (f32[5,8,128]{2,1,0:T(8,128)S(1)}, f32[5,8,128]{2,1,0:T(8,128)S(1)}, u32[]{:S(2)}, u32[]{:S(2)}) collective-permute-start(f32[5,8,128]{2,1,0:T(8,128)S(1)} %collective-permute-done.5.refs_5_), channel_id=1, source_target_pairs={{0,16},{1,17},{2,18},{3,19},{4,20},{5,21},{6,22},{7,23},{8,24},{9,... | collective-permute-start | bytes 61448 | tf_op jit(solution)/shard_map/ppermute | solution.py:520

commit v3 on v2

v3 whole, which is shorter than its diff:
```python
import jax
import jax.numpy as jnp
from jax import lax
from jax.experimental import pallas as pl
from jax.experimental.pallas import tpu as pltpu
from jax.sharding import PartitionSpec as P


HALO = 2
FIELDS = 8
U, V, TEMP, SALT, UB, VB, TB, SB = range(FIELDS)
VEL_X = (U, UB)


def lane_roll(x, shift):
    shift %= x.shape[1]
    return pltpu.roll(x, shift, 1) if shift else x


def level_roll(x, shift):
    shift %= x.shape[0]
    return pltpu.roll(x, shift, 0) if shift else x


class Shape:
    def __init__(self, lev, cx, rows):
        self.lev, self.cx, self.rows = lev, cx, rows
        self.cols = cx + 2 * HALO
        self.group = rows // self.cols
        self.per_tile = self.group // (2 * HALO)
        self.half = self.group // 2
        self.field_tiles = -(-FIELDS // self.per_tile)
        self.edge_tiles = 2 * self.field_tiles + 1
        assert self.per_tile >= 2 and self.group >= 4 * HALO and 2 * cx <= lev
        assert self.cols * self.group == rows
        self.mask_tile = FIELDS * cx
        self.halo_tiles = FIELDS * HALO

    def lanes(self):
        return lax.broadcasted_iota(jnp.int32, (self.lev, self.rows), 1)

    def levels(self):
        return lax.broadcasted_iota(jnp.int32, (self.lev, self.rows), 0)

    def row(self, ref, tile, r):
        return jnp.broadcast_to(ref[tile, r : r + 1, :], (self.lev, self.rows))

    def edge_at(self, comp, ch):
        t, q = divmod(ch, self.per_tile)
        return comp * self.field_tiles + t, q

    def halo_at(self, comp, side, ch, d):
        return (self.halo_tiles if comp == side else 0) + ch * HALO + d

    def edge_place(self, acc, value, j, channel, lane):
        at = j * self.group + channel * 2 * HALO + HALO
        return jnp.where((lane >= at - HALO) & (lane < at + HALO), lane_roll(value, at), acc)


def load_kernel(sh, *refs):
    sources, x_ref, e_ref, arrived, sem = refs[:4], refs[4], refs[5], refs[6:10], refs[10]
    copies = [
        pltpu.make_async_copy(a, b, sem.at[i]) for i, (a, b) in enumerate(zip(sources, arrived))
    ]
    for copy in copies:
        copy.start()
    for copy in copies:
        copy.wait()
    state_ref, irr_ref, land_ref, bottom_ref = arrived
    odd = is_odd("gx")
    edges = own_columns(sh, state_ref, x_ref, odd, first_core())
    cx = sh.cx
    lane = sh.lanes()
    depth = jnp.where(land_ref[...] == 1, bottom_ref[...], 0).astype(jnp.float32)
    last = jnp.zeros((sh.lev, sh.rows), jnp.float32)
    for q, value in enumerate((irr_ref[...], depth)):
        for k in range(cx):
            row = jnp.where(odd, value[cx - 1 - k : cx - k, :], value[k : k + 1, :])
            x_ref[sh.mask_tile, q * cx + k : q * cx + k + 1, :] = row
            wide = jnp.broadcast_to(row, (sh.lev, sh.rows))
            last = sh.edge_place(last, wide, k + HALO, q, lane)
    for t, edge in enumerate(edges + [last]):
        e_ref[t] = edge


def is_odd(axis):
    return lax.axis_index(axis) % 2 == 1


def first_core():
    return lax.axis_index("comp") == 0


def own_columns(sh, state_ref, x_ref, odd, dynamics):
    flip = jnp.where(odd & dynamics, -1.0, 1.0)
    cx = sh.cx
    lane = sh.lanes()
    edges = [jnp.zeros((sh.lev, sh.rows), jnp.float32)] * sh.field_tiles
    for ch in range(FIELDS):
        raw = [state_ref[pl.ds(ch * sh.lev * cx + i, sh.lev, stride=cx), :] for i in range(cx)]
        t, q = sh.edge_at(0, ch)
        for k in range(cx):
            value = jnp.where(odd, raw[cx - 1 - k], raw[k])
            if ch in VEL_X:
                value = value * flip
            x_ref[ch * cx + k] = value
            edges[t] = sh.edge_place(edges[t], value, k + HALO, q, lane)
    return edges


def send_kernel(sh, state_ref, xo_ref, eo_ref, xp_ref, e_ref, m_ref):
    core0 = first_core()
    edges = own_columns(sh, state_ref, xp_ref, is_odd("gx"), jnp.logical_not(core0))
    cx = sh.cx
    for t in range(sh.field_tiles):
        own = eo_ref[t]
        e_ref[t] = jnp.where(core0, own, edges[t])
        e_ref[sh.field_tiles + t] = jnp.where(core0, edges[t], own)
    e_ref[sh.edge_tiles - 1] = eo_ref[sh.field_tiles]
    for part, (x_ref, flip) in enumerate(
        ((xo_ref, jnp.where(core0, -1.0, 1.0)), (xp_ref, jnp.where(core0, 1.0, -1.0)))
    ):
        for ch in range(FIELDS):
            for d in range(HALO):
                value = jnp.where(core0, x_ref[ch * cx + d], x_ref[ch * cx + cx - 1 - d])
                m_ref[part * sh.halo_tiles + ch * HALO + d] = value * flip if ch in VEL_X else value
    m_ref[2 * sh.halo_tiles] = xo_ref[sh.mask_tile]


def merge_kernel(sh, e_ref, a_ref, b_ref, eo_ref):
    lane = sh.lanes()
    core0 = first_core()
    column, place = lane // sh.group, lane % sh.group // (2 * HALO)
    for t in range(sh.edge_tiles):
        got = a_ref[t], b_ref[t]
        after, before = jnp.where(core0, got[0], got[1]), jnp.where(core0, got[1], got[0])
        for ch in VEL_X:
            if sh.edge_at(0, ch)[0] == t:
                flip = jnp.where(place == sh.edge_at(0, ch)[1], -1.0, 1.0)
                after, before = after * flip, before * flip
        edge = e_ref[t]
        for d in range(HALO):
            shift = (2 * d + 1) * sh.group
            edge = jnp.where(column == sh.cx + HALO + d, lane_roll(after, shift), edge)
            edge = jnp.where(column == HALO - 1 - d, lane_roll(before, -shift), edge)
        eo_ref[t] = edge


STRIP = "strip"


class Field:
    def __init__(self, sh, lane, col=None, strip=None, seam=None, rough=None):
        self.sh, self.lane, self.col, self.strip = sh, lane, col, strip
        self.seam, self.rough = seam, rough

    def centre(self, site):
        return self.strip() if site == STRIP else self.col(site)

    def east(self, site):
        return lane_roll(self.strip(), -self.sh.group) if site == STRIP else self.col(site + 1)

    def west(self, site):
        return lane_roll(self.strip(), self.sh.group) if site == STRIP else self.col(site - 1)

    def along_rows(self, site):
        inner = site == STRIP or self.rough is None
        value = self.centre(site) if inner else self.rough(site)
        north, south = lane_roll(value, -1), lane_roll(value, 1)
        if site == STRIP or self.seam is None:
            return north, south
        beyond = self.seam(site)
        more = 0 if inner else 1
        last = self.lane >= self.sh.rows - 1 - more
        return jnp.where(last, beyond, north), jnp.where(self.lane <= more, beyond, south)

    def around(self, site):
        return (self.east(site), self.west(site)) + self.along_rows(site)


GRAZED = (FIELDS, FIELDS + 1)
FLOW = tuple(FIELDS + ch for ch in (U, V, TEMP, SALT))
PRESSURE = FIELDS + 2
FRESH = FIELDS + 4


class Model:
    def __init__(self, sh):
        self.sh = sh
        self.lane, self.level = sh.lanes(), sh.levels()
        self.levelf = self.level.astype(jnp.float32)
        self.in_group = self.lane % sh.group
        self.core0 = first_core()
        self.odd_x = is_odd("gx")
        self.mirror = jnp.where(self.odd_x, -1.0, 1.0)
        self.gy, self.ny = lax.axis_index("gy"), lax.axis_size("gy")
        self.first_step = list(range(1, sh.cols - 1))
        self.own = list(range(HALO, HALO + sh.cx))
        self.n_sites = len(self.first_step)

    def fresh_at(self, index, site):
        return index * self.n_sites + site - 1

    def cumulate(self, x):
        reach = 1
        while reach < self.sh.lev:
            x = x + jnp.where(self.level >= reach, level_roll(x, reach), 0.0)
            reach *= 2
        return x

    def wet_of(self, depth):
        return jnp.where(self.levelf < depth, 1.0, 0.0)

    def faces(self, site):
        w = self.wet.centre(site)
        return [w * value for value in self.wet.around(site)]

    def density(self, d, site):
        rho = 0.8 * d[SALT].centre(site) - 0.2 * d[TEMP].centre(site)
        return rho * self.wet.centre(site)

    def pressure(self, d, site):
        return 0.1 * self.cumulate(self.density(d, site))

    def speeds(self, u, v, site, m):
        uc, vc = u.centre(site), v.centre(site)
        north, south = v.along_rows(site)
        qe = 0.025 * (uc + u.east(site)) * m[0]
        qw = 0.025 * (uc + u.west(site)) * m[1]
        qn = 0.025 * (vc + north) * m[2]
        qs = 0.025 * (vc + south) * m[3]
        return qe, qw, qn, qs, (qw - qe) + (qs - qn)

    def laplacian(self, f, site, m, total):
        e, w, n, s = f.around(site)
        return (m[0] * e + m[1] * w) + (m[2] * n + m[3] * s) - total * f.centre(site)

    def coriolis(self, site):
        sh, at = self.sh, self.in_group
        row = self.lane
        if site == STRIP:
            row = jnp.where(at < sh.half, at - HALO, sh.rows - HALO + at - sh.half)
        row = (row + self.gy * sh.rows).astype(jnp.float32)
        return self.mirror * (0.3 + 0.4 * row / (self.ny * sh.rows))

    def dynamics(self, d, pressure, site, heat, q, m):
        w = self.wet.centre(site)
        total = (m[0] + m[1]) + (m[2] + m[3])
        uc, vc = d[U].centre(site), d[V].centre(site)
        pc = pressure.centre(site)
        pe, pw, pn, ps = pressure.around(site)
        push_x = 0.1 * (m[0] * (pe - pc) + m[1] * (pc - pw))
        push_y = 0.1 * (m[2] * (pn - pc) + m[3] * (pc - ps))
        f = 0.2 * self.coriolis(site) * w
        spread = {ch: 0.04 * self.laplacian(d[ch], site, m, total) for ch in (UB, VB)}
        after = {
            U: d[UB].centre(site) + (f * vc - push_x + spread[UB]),
            V: d[VB].centre(site) + (spread[VB] - f * uc - push_y),
        }
        if heat is None:
            return after
        qe, qw, qn, qs, qc = q
        for now, before in ((TEMP, TB), (SALT, SB)):
            e, w_, n, s = d[now].around(site)
            carried = (qw * w_ - qe * e) + (qs * s - qn * n) + qc * d[now].centre(site)
            change = 2.0 * carried + 0.04 * self.laplacian(d[before], site, m, total)
            if now == TEMP:
                change = change + 0.6 * heat
            after[now] = d[before].centre(site) + change
        return after

    def filtered(self, d, site, ch, after):
        now, before = d[ch].centre(site), d[ch + 4].centre(site)
        return now + 0.1 * (before - 2.0 * now + after) * self.wet.centre(site)

    def optics(self, c, site):
        absorb = 0.08 + 0.05 * (jnp.abs(c[2].centre(site)) + jnp.abs(c[3].centre(site)))
        return absorb, self.cumulate(absorb)

    def heating(self, absorb, depthsum, site):
        fade = jnp.exp(-depthsum)
        above = jnp.where(self.level == 0, 1.0, level_roll(fade, 1))
        return self.irr_at(site) * self.wet.centre(site) * (above - fade)

    def light(self, absorb, depthsum, site):
        return self.irr_at(site) * jnp.exp(0.5 * absorb - depthsum)

    def mixing(self, d, site):
        rho = self.density(d, site)
        below = level_roll(rho, -1)
        wet_below = jnp.where(self.levelf + 1.0 < self.depth_at(site), 1.0, 0.0)
        return (0.005 + 0.1 / (1.0 + 4.0 * jnp.maximum(below - rho, 0.0))) * wet_below

    def reactions(self, c, temp, lit, which):
        nn, na = jnp.abs(c[0]), jnp.abs(c[1])
        base = jnp.exp(0.06 * temp) * (lit / (lit + 0.5))
        total = nn + na
        small = 0.6 * base * c[2] / (0.2 + total)
        large = 0.9 * base * c[3] / (0.8 + total)
        graze = 0.8 * c[4] / (1.0 + (jnp.abs(c[2]) + jnp.abs(c[3])))
        gs, gl = graze * c[2], graze * c[3]
        up_s, up_l = small * total, large * total
        r = {2: up_s - gs - 0.1 * c[2], 3: up_l - gl - 0.1 * c[3]}
        if len(which) > 2:
            both = small + large
            remin = 0.3 * c[5] + 0.1 * c[6]
            nitrify = 0.2 * c[1]
            r[0] = nitrify - both * nn
            r[1] = remin + 0.1 * c[4] - nitrify - both * na
            r[4] = 0.7 * (gs + gl) - 0.25 * c[4]
            r[5] = 0.1 * c[2] + 0.3 * gs - 0.3 * c[5]
            r[6] = 0.1 * c[3] + 0.15 * c[4] + 0.3 * gl - 0.1 * c[6]
            r[7] = 1.3 * (up_s + up_l) - (remin + 2.0 * nitrify)
        return r

    def tracers(self, c, d, site, q, m, lit, which):
        w = self.wet.centre(site)
        qe, qw, qn, qs, qc = q
        total = (m[0] + m[1]) + (m[2] + m[3])
        ke, kw = 0.02 * m[0] - qe, 0.02 * m[1] + qw
        kn, ks = 0.02 * m[2] - qn, 0.02 * m[3] + qs
        kc = (1.0 - 0.02 * total) + qc
        kappa = self.mixing(d, site)
        centre = {i: c[i].centre(site) for i in (which if len(which) > 2 else range(5))}
        r = self.reactions(centre, d[TEMP].centre(site), lit, which)
        tenth = 0.1 * w
        for i in which:
            e, w_, n, s = c[i].around(site)
            here = centre[i]
            down = kappa * (level_roll(here, -1) - here)
            moved = (ke * e + kw * w_) + (kn * n + ks * s)
            yield i, kc * here + moved + (down - level_roll(down, 1)) + tenth * r[i]

    def first_core_site(self, d, c, pressure, site, store, plankton):
        m = self.faces(site)
        q = self.speeds(d[U], d[V], site, m)
        optic = self.optics(c, site)
        after = self.dynamics(d, pressure, site, self.heating(*optic, site), q, m)
        for ch, value in after.items():
            store(ch, site, value)
            store(ch + 4, site, self.filtered(d, site, ch, value))
        if plankton:
            for i, value in self.tracers(c, d, site, q, m, self.light(*optic, site), (2, 3)):
                store(GRAZED[i - 2], site, value)

    def second_core_site(self, d, c, pressure, site, store, heated):
        m = self.faces(site)
        q = self.speeds(d[U], d[V], site, m)
        optic = self.optics(c, site)
        if pressure is not None:
            heat = self.heating(*optic, site) if heated else None
            for ch, value in self.dynamics(d, pressure, site, heat, q, m).items():
                store(FLOW[ch], site, value)
        lit = self.light(*optic, site)
        for i, value in self.tracers(c, d, site, q, m, lit, range(FIELDS)):
            store(i, site, value)


def column_kernel(sh, xo, xp, rx, rp, fresh, wet_ref, press):
    md = Model(sh)
    cx = sh.cx

    def mask_row(kind, j):
        if HALO <= j < HALO + cx:
            return sh.row(xo, sh.mask_tile, kind * cx + j - HALO)
        if j < HALO:
            first, second, at = rx, rp, HALO - 1 - j
        else:
            first, second, at = rp, rx, cx - 1 - (j - HALO - cx)
        tile = 2 * sh.halo_tiles
        return jnp.where(
            md.core0, sh.row(first, tile, kind * cx + at), sh.row(second, tile, kind * cx + at)
        )

    md.irr_at = lambda site: mask_row(0, site)
    md.depth_at = lambda site: mask_row(1, site)
    for j in range(sh.cols):
        wet_ref[j] = md.wet_of(mask_row(1, j))
    md.wet = Field(sh, md.lane, lambda j: wet_ref[j])

    def raw(x, sides, comp, ch):
        def col(j):
            if HALO <= j < HALO + cx:
                return x[ch * cx + j - HALO]
            if j < HALO:
                return sides[1][sh.halo_at(comp, 1, ch, HALO - 1 - j)]
            return sides[0][sh.halo_at(comp, 0, ch, j - HALO - cx)]

        return Field(sh, md.lane, col)

    def store(index, site, value):
        fresh[md.fresh_at(index, site)] = value

    def fields(x, sides, comp):
        return [raw(x, sides, comp, ch) for ch in range(FIELDS)]

    def pressure_of(d):
        for j in range(sh.cols):
            press[j] = md.pressure(d, j)
        return Field(sh, md.lane, lambda j: press[j])

    @pl.when(md.core0)
    def _():
        d, c = fields(xo, (rp, rx), 0), fields(xp, (rp, rx), 1)
        pressure = pressure_of(d)
        for site in md.first_step:
            md.first_core_site(d, c, pressure, site, store, site in md.own)
        d = [
            Field(sh, md.lane, lambda j, ch=ch: fresh[md.fresh_at(ch, j)]) for ch in range(FIELDS)
        ]
        for site in md.first_step:
            store(PRESSURE, site, md.pressure(d, site))

    @pl.when(jnp.logical_not(md.core0))
    def _():
        d, c = fields(xp, (rx, rp), 0), fields(xo, (rx, rp), 1)
        pressure = pressure_of(d)
        for site in md.first_step:
            md.second_core_site(d, c, pressure, site, store, site in md.own)


def step_kernel(sh, xo, wet_ref, fresh, edges, y, yp, out_ref, strips, cols, rims, seams):
    md = Model(sh)
    cx, lane, in_group = sh.cx, md.lane, md.in_group
    end = sh.rows - 1
    even_y = md.gy % 2 == 0
    slot = lane % (2 * HALO)
    zero = jnp.zeros((sh.lev, sh.rows), jnp.float32)

    def build_strips(base, tiles, channels):
        for t in tiles:
            a, b = jnp.where(md.core0, y[t], yp[t]), jnp.where(md.core0, yp[t], y[t])
            mine = edges[t]
            left = jnp.where(md.gy > 0, jnp.where(even_y, b, a), zero)
            right = jnp.where(md.gy < md.ny - 1, jnp.where(even_y, a, b), zero)
            low = jnp.where(slot < HALO, left, mine)
            high = jnp.where(slot < HALO, mine, right)
            for q in range(channels):
                at = q * 2 * HALO
                strips[base + (t - tiles[0]) * sh.per_tile + q] = jnp.where(
                    in_group < sh.half, lane_roll(low, -at), lane_roll(high, sh.half - at)
                )

    build_strips(0, range(2 * sh.field_tiles), sh.per_tile)
    build_strips(2 * FIELDS, [sh.edge_tiles - 1], 2)

    def mask_at(kind, site):
        if site == STRIP:
            return strips[2 * FIELDS + kind]
        return sh.row(xo, sh.mask_tile, kind * cx + site - HALO)

    md.irr_at = lambda site: mask_at(0, site)
    md.depth_at = lambda site: mask_at(1, site)

    def beside(strip, low, high):
        at = sh.half + high
        return jnp.where(in_group > at, lane_roll(strip, at + 1 - low), strip)

    def to_ends(pair, site, high):
        return lane_roll(pair, end - (site * sh.group + sh.half + high))

    def seam_of(ref, index):
        return lambda site: to_ends(ref[index], site, HALO)

    wet_strip = md.wet_of(strips[2 * FIELDS + 1])
    wet_pair = beside(wet_strip, HALO - 1, HALO)
    md.wet = Field(
        sh, lane, lambda j: wet_ref[j], lambda: wet_strip, lambda site: to_ends(wet_pair, site, HALO)
    )

    def strip_field(index):
        return Field(sh, lane, strip=lambda: strips[index])

    def rim(index, site, value):
        rims[index] = value

    def renewed(index, sites):
        value = rims[index]
        seams[index] = beside(value, HALO - 1, HALO)
        ends = beside(value, HALO, HALO - 1)
        for site in sites:
            cols[md.fresh_at(index, site)] = jnp.where(
                (lane == 0) | (lane == end),
                to_ends(ends, site, HALO - 1),
                fresh[md.fresh_at(index, site)],
            )
        return stored(index)

    def stored(index):
        return Field(
            sh,
            lane,
            lambda j: cols[md.fresh_at(index, j)],
            lambda: rims[index],
            seam_of(seams, index),
            lambda j: fresh[md.fresh_at(index, j)],
        )

    def write(ch, k_values):
        for i in range(cx):
            out_ref[pl.ds(ch * sh.lev * cx + i, sh.lev, stride=cx), :] = jnp.where(
                md.odd_x, k_values[cx - 1 - i], k_values[i]
            )

    d = [strip_field(ch) for ch in range(FIELDS)]
    c = [strip_field(FIELDS + ch) for ch in range(FIELDS)]
    strip_pressure = md.pressure(d, STRIP)
    pressure = Field(sh, lane, strip=lambda: strip_pressure)
    done = {}

    def keep(ch, site, value):
        done[ch, site] = value

    @pl.when(md.core0)
    def _():
        md.first_core_site(d, c, pressure, STRIP, rim, True)
        d1 = [renewed(ch, md.own if ch == V else md.first_step) for ch in range(FIELDS)]
        c1 = {i: renewed(GRAZED[i - 2], md.own) for i in (2, 3)}
        rim(PRESSURE, STRIP, md.pressure(d1, STRIP))
        pressure1 = renewed(PRESSURE, md.first_step)
        for site in md.own:
            md.first_core_site(d1, c1, pressure1, site, keep, False)
        for ch in range(FIELDS):
            values = [done[ch, site] for site in md.own]
            write(ch, [v * md.mirror for v in values] if ch in VEL_X else values)

    @pl.when(jnp.logical_not(md.core0))
    def _():
        md.second_core_site(d, c, pressure, STRIP, rim, True)
        c1 = [renewed(ch, md.first_step) for ch in range(FIELDS)]
        d1 = [renewed(FLOW[ch], md.first_step if ch == U else md.own) for ch in range(4)]
        for site in md.own:
            md.second_core_site(d1, c1, None, site, keep, False)
        for ch in range(FIELDS):
            write(ch, [done[ch, site] for site in md.own])


def tiles(sh, n):
    return jax.ShapeDtypeStruct((n, sh.lev, sh.rows), jnp.float32)


def call(kernel, sh, outs, args, flops, scratch=(), source=pltpu.VMEM):
    spec = pl.BlockSpec(memory_space=pltpu.VMEM)
    size = sum(a.size for a in args) + sum(o.size for o in outs)
    return pl.pallas_call(
        lambda *refs: kernel(sh, *refs),
        out_shape=outs,
        in_specs=[pl.BlockSpec(memory_space=source)] * len(args),
        out_specs=[spec] * len(outs),
        scratch_shapes=list(scratch),
        compiler_params=pltpu.CompilerParams(vmem_limit_bytes=16 << 20),
        cost_estimate=pl.CostEstimate(flops=flops, bytes_accessed=4 * size, transcendentals=0),
    )(*args)


def local(ocean_state, irradiance, land_mask, bottom_level):
    fields, lev, cx, rows = ocean_state.shape
    assert fields == FIELDS
    sh = Shape(lev, cx, rows)
    nx, ny = lax.axis_size("gx"), lax.axis_size("gy")
    assert nx % 2 == 0 and ny % 2 == 0
    axes = ("comp", "gy", "gx")

    def send(value, target):
        pairs = []
        for c in range(2):
            for y in range(ny):
                for x in range(nx):
                    tc, ty, tx = target(c, y, x)
                    pairs.append(((c * ny + y) * nx + x, (tc * ny + ty) * nx + tx))
        return lax.ppermute(value, axes, pairs)

    def odd_pair(i, n):
        return (i + 1) % n if i % 2 else (i - 1) % n

    def pair(i, n, core):
        return i ^ 1 if core == 0 else odd_pair(i, n)

    def edges_x(v):
        return send(v, lambda c, y, x: (c, y, pair(x, nx, c)))

    def bulk_x(v):
        return send(v, lambda c, y, x: (c, y, pair(x, nx, 1 - c)))

    def along_y(v):
        return send(v, lambda c, y, x: (c, pair(y, ny, c), x))

    def swap(v):
        return send(v, lambda c, y, x: (1 - c, y, x))

    flat = ocean_state.reshape(fields * lev * cx, rows)
    partner = swap(flat)
    inputs = (flat, irradiance, land_mask, bottom_level)
    xo, eo = call(
        load_kernel,
        sh,
        [tiles(sh, fields * cx + 1), tiles(sh, sh.field_tiles + 1)],
        tuple(pltpu.with_memory_space_constraint(a, pltpu.HBM) for a in inputs),
        100_000,
        scratch=[pltpu.VMEM(a.shape, a.dtype) for a in inputs] + [pltpu.SemaphoreType.DMA((4,))],
        source=pltpu.HBM,
    )
    edge, message = tiles(sh, sh.edge_tiles), tiles(sh, 2 * sh.halo_tiles + 1)
    xp, e0, m = call(
        send_kernel, sh, [tiles(sh, fields * cx), edge, message], (partner, xo, eo), 100_000
    )
    ex = edges_x(e0)
    rx = bulk_x(m)
    ep = swap(ex)
    (e1,) = call(merge_kernel, sh, [edge], (e0, ex, ep), 10_000)
    y = along_y(e1)
    rp = swap(rx)
    yp = swap(y)
    n_sites = sh.cols - 2
    fresh, wet = call(
        column_kernel,
        sh,
        [tiles(sh, FRESH * n_sites), tiles(sh, sh.cols)],
        (xo, xp, rx, rp),
        1_000_000,
        scratch=[pltpu.VMEM((sh.cols, lev, rows), jnp.float32)],
    )
    (out,) = call(
        step_kernel,
        sh,
        [jax.ShapeDtypeStruct(flat.shape, jnp.float32)],
        (xo, wet, fresh, e1, y, yp),
        1_000_000,
        scratch=[
            pltpu.VMEM((2 * FIELDS + 2, lev, rows), jnp.float32),
            pltpu.VMEM((FRESH * n_sites, lev, rows), jnp.float32),
            pltpu.VMEM((FRESH, lev, rows), jnp.float32),
            pltpu.VMEM((FRESH, lev, rows), jnp.float32),
        ],
    )
    return out.reshape(ocean_state.shape)


def solution(mesh):
    return jax.shard_map(
        local,
        mesh=mesh,
        in_specs=(P("comp", None, "gx", "gy"), P("gx", "gy"), P("gx", "gy"), P("gx", "gy")),
        out_specs=P("comp", None, "gx", "gy"),
        check_vma=False,
    )
```

time: 23.4 us -> 23.2 us (level)
  waiting for transfers between devices: 8.23 us -> 7.88 us
  Pallas kernels: 2.79 us -> 3.07 us
    ppermute x7, waiting for transfers between devices: 8.23 us -> 7.88 us  [send(): return lax.ppermute(value, axes, pairs)]
    pallas_call x4 -> x5, Pallas kernels: 2.79 us -> 3.07 us  [call(): pl.pallas_call(lambda *refs: kernel(sh, *refs), out_shape=outs, in_specs=...]
  transfers between devices with their start and end apart: 7 -> 7, of which waited for: 6 -> 6; matrix products, arithmetic and copies ran while one was open for 0% -> 0% of each run, Pallas kernels for 5% -> 7%
where the time goes in v3:
time: 23.2 us; the launch traced here: 22.9 us
  starting transfers between devices  12 us (52%)
  waiting for transfers between devices  7.88 us (34%)
  Pallas kernels  3.07 us (13%)
    ppermute x7, starting transfers between devices, send(): return lax.ppermute(value, axes, pairs)  12 us
    ppermute x7, waiting for transfers between devices, send(): return lax.ppermute(value, axes, pairs)  7.88 us
    pallas_call x5, Pallas kernels, call(): pl.pallas_call(lambda *refs: kernel(sh, *refs), out_shape=outs, in_specs=...  3.07 us
  transfers between devices with their start and end apart: 7, of which 6 were waited for; matrix products, arithmetic and copies ran while one was open for 0% of the time, Pallas kernels for 7%

profile of v3, /device:TPU:1, one launch (start us, length us, event | category | flops | bytes accessed | tf_op | source)
XLA Modules:
  0.0 22.9 jit_solution(7833851623664533685)
XLA Ops:
  0.0 0.0 collective-permute-start
  0.0 1.1 %shard_map.46 = (f32[33,8,128]{2,1,0:T(8,128)S(1)}, f32[3,8,128]{2,1,0:T(8,128)S(1)}) custom-call(f32[256,128]{1,0:T(8,128)} %bitcast.3, f32[4,128]{1,0:T(4,128)} %refs_1_.1, s32[4,128]{1,0:T(4,128)} %refs_2_.1, s32[4,128]{1,0:T(4,128)} %refs_3_.1), custom_call_target="tpu_custom_call" | custom-call | flops 100000 | bytes 284672 | tf_op jit(solution)/shard_map/pallas_call | solution.py:545
  1.1 0.5 %collective-permute-done.refs_0_ = f32[256,128]{1,0:T(8,128)S(1)} collective-permute-done((f32[256,128]{1,0:T(8,128)}, f32[256,128]{1,0:T(8,128)S(1)}, u32[]{:S(2)}, u32[]{:S(2)}) %collective-permute-start) | collective-permute-done | bytes 131104 | tf_op jit(solution)/shard_map/ppermute | solution.py:571
  1.6 0.1 shard_map.47
  1.7 2.5 %collective-permute-start.1 = (f32[33,8,128]{2,1,0:T(8,128)S(1)}, f32[33,8,128]{2,1,0:T(8,128)S(1)}, u32[]{:S(2)}, u32[]{:S(2)}) collective-permute-start(f32[33,8,128]{2,1,0:T(8,128)S(1)} %get-tuple-element.15), channel_id=1, source_target_pairs={{0,3},{1,2},{2,1},{3,0},{4,7},{5,6},{6,5},{7,4},{8,11},{9,10},{10,... | collective-permute-start | bytes 405512 | tf_op jit(solution)/shard_map/ppermute | solution.py:571
  4.2 2.4 %collective-permute-done.1.refs_2_ = f32[33,8,128]{2,1,0:T(8,128)S(1)} collective-permute-done((f32[33,8,128]{2,1,0:T(8,128)S(1)}, f32[33,8,128]{2,1,0:T(8,128)S(1)}, u32[]{:S(2)}, u32[]{:S(2)}) %collective-permute-start.1) | collective-permute-done | bytes 135200 | tf_op jit(solution)/shard_map/ppermute | solution.py:571
  6.6 4.3 %collective-permute-start.2 = (f32[33,8,128]{2,1,0:T(8,128)S(1)}, f32[33,8,128]{2,1,0:T(8,128)S(1)}, u32[]{:S(2)}, u32[]{:S(2)}) collective-permute-start(f32[33,8,128]{2,1,0:T(8,128)S(1)} %collective-permute-done.1.refs_2_), channel_id=1, source_target_pairs={{0,16},{1,17},{2,18},{3,19},{4,20},{5,21},{6,22},{7,23},{8,24},{9,... | collective-permute-start | bytes 405512 | tf_op jit(solution)/shard_map/ppermute | solution.py:571
  10.9 2.5 %collective-permute-start.3 = (f32[5,8,128]{2,1,0:T(8,128)S(1)}, f32[5,8,128]{2,1,0:T(8,128)S(1)}, u32[]{:S(2)}, u32[]{:S(2)}) collective-permute-start(f32[5,8,128]{2,1,0:T(8,128)S(1)} %get-tuple-element.18.refs_0_), channel_id=1, source_target_pairs={{0,1},{1,0},{2,3},{3,2},{4,5},{5,4},{6,7},{7,6},{8,9},{9,8},{10,11... | collective-permute-start | bytes 61448 | tf_op jit(solution)/shard_map/ppermute | solution.py:571
  13.4 2.0 %collective-permute-done.3.refs_1_ = f32[5,8,128]{2,1,0:T(8,128)S(1)} collective-permute-done((f32[5,8,128]{2,1,0:T(8,128)S(1)}, f32[5,8,128]{2,1,0:T(8,128)S(1)}, u32[]{:S(2)}, u32[]{:S(2)}) %collective-permute-start.3) | collective-permute-done | bytes 20512 | tf_op jit(solution)/shard_map/ppermute | solution.py:571
  15.3 0.0 collective-permute-start.4
  15.3 1.2 %collective-permute-done.4.refs_2_ = f32[5,8,128]{2,1,0:T(8,128)S(1)} collective-permute-done((f32[5,8,128]{2,1,0:T(8,128)S(1)}, f32[5,8,128]{2,1,0:T(8,128)S(1)}, u32[]{:S(2)}, u32[]{:S(2)}) %collective-permute-start.4) | collective-permute-done | bytes 20512 | tf_op jit(solution)/shard_map/ppermute | solution.py:571
  16.5 0.1 shard_map.49.refs_3_
  16.6 2.2 %collective-permute-start.5 = (f32[5,8,128]{2,1,0:T(8,128)S(1)}, f32[5,8,128]{2,1,0:T(8,128)S(1)}, u32[]{:S(2)}, u32[]{:S(2)}) collective-permute-start(f32[5,8,128]{2,1,0:T(8,128)S(1)} %shard_map.49.refs_3_), channel_id=1, source_target_pairs={{0,4},{1,5},{2,6},{3,7},{4,0},{5,1},{6,2},{7,3},{8,12},{9,13},{10,... | collective-permute-start | bytes 61448 | tf_op jit(solution)/shard_map/ppermute | solution.py:571
  18.8 1.4 %collective-permute-done.5.refs_4_ = f32[5,8,128]{2,1,0:T(8,128)S(1)} collective-permute-done((f32[5,8,128]{2,1,0:T(8,128)S(1)}, f32[5,8,128]{2,1,0:T(8,128)S(1)}, u32[]{:S(2)}, u32[]{:S(2)}) %collective-permute-start.5) | collective-permute-done | bytes 20512 | tf_op jit(solution)/shard_map/ppermute | solution.py:571
  20.2 0.4 %collective-permute-start.6 = (f32[5,8,128]{2,1,0:T(8,128)S(1)}, f32[5,8,128]{2,1,0:T(8,128)S(1)}, u32[]{:S(2)}, u32[]{:S(2)}) collective-permute-start(f32[5,8,128]{2,1,0:T(8,128)S(1)} %collective-permute-done.5.refs_4_), channel_id=1, source_target_pairs={{0,16},{1,17},{2,18},{3,19},{4,20},{5,21},{6,22},{7,23},{8,24},{9,... | collective-permute-start | bytes 61448 | tf_op jit(solution)/shard_map/ppermute | solution.py:571
  20.6 0.0 collective-permute-done.2.refs_3_
  20.6 0.3 %shard_map.48 = (f32[72,8,128]{2,1,0:T(8,128)S(1)}, f32[8,8,128]{2,1,0:T(8,128)S(1)}) custom-call(f32[33,8,128]{2,1,0:T(8,128)S(1)} %get-tuple-element.12.refs_1_.refs_0_, f32[32,8,128]{2,1,0:T(8,128)S(1)} %get-tuple-element.14.refs_1_, f32[33,8,128]{2,1,0:T(8,128)S(1)} %collective-permute-done.1.refs_2_, f32[33,8,128]{2,1,0:T(8,128)S(1)} %collective-permute-done.2.refs_3_), custom_call_target="tpu_custom_call" | custom-call | flops 1000000 | bytes 864256 | tf_op jit(solution)/shard_map/pallas_call | solution.py:545
  21.0 0.5 %collective-permute-done.6.refs_5_ = f32[5,8,128]{2,1,0:T(8,128)S(1)} collective-permute-done((f32[5,8,128]{2,1,0:T(8,128)S(1)}, f32[5,8,128]{2,1,0:T(8,128)S(1)}, u32[]{:S(2)}, u32[]{:S(2)}) %collective-permute-start.6) | collective-permute-done | bytes 20512 | tf_op jit(solution)/shard_map/ppermute | solution.py:571
  21.5 1.5 %shard_map.50 = f32[256,128]{1,0:T(8,128)} custom-call(f32[33,8,128]{2,1,0:T(8,128)S(1)} %get-tuple-element.12.refs_1_.refs_0_, f32[8,8,128]{2,1,0:T(8,128)S(1)} %get-tuple-element.16.refs_1_, f32[72,8,128]{2,1,0:T(8,128)S(1)} %get-tuple-element.17.refs_2_, f32[5,8,128]{2,1,0:T(8,128)S(1)} %shard_map.49.refs_3_, ...), custom_call_target="tpu_custom_call" | custom-call | flops 1000000 | bytes 655360 | tf_op jit(solution)/shard_map/pallas_call | solution.py:545
Async XLA Ops:
  0.0 1.6 %collective-permute-start = (f32[256,128]{1,0:T(8,128)}, f32[256,128]{1,0:T(8,128)S(1)}, u32[]{:S(2)}, u32[]{:S(2)}) collective-permute-start(f32[256,128]{1,0:T(8,128)} %bitcast.2), channel_id=1, source_target_pairs={{0,16},{1,17},{2,18},{3,19},{4,20},{5,21},{6,22},{7,23},{8,24},{9,... | collective-permute-start | bytes 393224 | tf_op jit(solution)/shard_map/ppermute | solution.py:571
  1.7 4.9 %collective-permute-start.1 = (f32[33,8,128]{2,1,0:T(8,128)S(1)}, f32[33,8,128]{2,1,0:T(8,128)S(1)}, u32[]{:S(2)}, u32[]{:S(2)}) collective-permute-start(f32[33,8,128]{2,1,0:T(8,128)S(1)} %get-tuple-element.15), channel_id=1, source_target_pairs={{0,3},{1,2},{2,1},{3,0},{4,7},{5,6},{6,5},{7,4},{8,11},{9,10},{10,... | collective-permute-start | bytes 405512 | tf_op jit(solution)/shard_map/ppermute | solution.py:571
  6.6 14.1 %collective-permute-start.2 = (f32[33,8,128]{2,1,0:T(8,128)S(1)}, f32[33,8,128]{2,1,0:T(8,128)S(1)}, u32[]{:S(2)}, u32[]{:S(2)}) collective-permute-start(f32[33,8,128]{2,1,0:T(8,128)S(1)} %collective-permute-done.1.refs_2_), channel_id=1, source_target_pairs={{0,16},{1,17},{2,18},{3,19},{4,20},{5,21},{6,22},{7,23},{8,24},{9,... | collective-permute-start | bytes 405512 | tf_op jit(solution)/shard_map/ppermute | solution.py:571
  10.9 4.4 %collective-permute-start.3 = (f32[5,8,128]{2,1,0:T(8,128)S(1)}, f32[5,8,128]{2,1,0:T(8,128)S(1)}, u32[]{:S(2)}, u32[]{:S(2)}) collective-permute-start(f32[5,8,128]{2,1,0:T(8,128)S(1)} %get-tuple-element.18.refs_0_), channel_id=1, source_target_pairs={{0,1},{1,0},{2,3},{3,2},{4,5},{5,4},{6,7},{7,6},{8,9},{9,8},{10,11... | collective-permute-start | bytes 61448 | tf_op jit(solution)/shard_map/ppermute | solution.py:571
  15.3 1.2 %collective-permute-start.4 = (f32[5,8,128]{2,1,0:T(8,128)S(1)}, f32[5,8,128]{2,1,0:T(8,128)S(1)}, u32[]{:S(2)}, u32[]{:S(2)}) collective-permute-start(f32[5,8,128]{2,1,0:T(8,128)S(1)} %collective-permute-done.3.refs_1_), channel_id=1, source_target_pairs={{0,16},{1,17},{2,18},{3,19},{4,20},{5,21},{6,22},{7,23},{8,24},{9,... | collective-permute-start | bytes 61448 | tf_op jit(solution)/shard_map/ppermute | solution.py:571
  16.6 3.6 %collective-permute-start.5 = (f32[5,8,128]{2,1,0:T(8,128)S(1)}, f32[5,8,128]{2,1,0:T(8,128)S(1)}, u32[]{:S(2)}, u32[]{:S(2)}) collective-permute-start(f32[5,8,128]{2,1,0:T(8,128)S(1)} %shard_map.49.refs_3_), channel_id=1, source_target_pairs={{0,4},{1,5},{2,6},{3,7},{4,0},{5,1},{6,2},{7,3},{8,12},{9,13},{10,... | collective-permute-start | bytes 61448 | tf_op jit(solution)/shard_map/ppermute | solution.py:571
  20.2 1.3 %collective-permute-start.6 = (f32[5,8,128]{2,1,0:T(8,128)S(1)}, f32[5,8,128]{2,1,0:T(8,128)S(1)}, u32[]{:S(2)}, u32[]{:S(2)}) collective-permute-start(f32[5,8,128]{2,1,0:T(8,128)S(1)} %collective-permute-done.5.refs_4_), channel_id=1, source_target_pairs={{0,16},{1,17},{2,18},{3,19},{4,20},{5,21},{6,22},{7,23},{8,24},{9,... | collective-permute-start | bytes 61448 | tf_op jit(solution)/shard_map/ppermute | solution.py:571

commit v4 on v3

--- a/solution.py
+++ b/solution.py
@@ -427,7 +427,11 @@
     slot = lane % (2 * HALO)
     zero = jnp.zeros((sh.lev, sh.rows), jnp.float32)
 
-    def build_strips(base, tiles, channels):
+    def build_strips():
+        strips_of(2 * FIELDS, [sh.edge_tiles - 1], 2)
+        strips_of(0, range(2 * sh.field_tiles), sh.per_tile)
+
+    def strips_of(base, tiles, channels):
         for t in tiles:
             a, b = jnp.where(md.core0, y[t], yp[t]), jnp.where(md.core0, yp[t], y[t])
             mine = edges[t]
@@ -441,9 +445,6 @@
                     in_group < sh.half, lane_roll(low, -at), lane_roll(high, sh.half - at)
                 )
 
-    build_strips(0, range(2 * sh.field_tiles), sh.per_tile)
-    build_strips(2 * FIELDS, [sh.edge_tiles - 1], 2)
-
     def mask_at(kind, site):
         if site == STRIP:
             return strips[2 * FIELDS + kind]
@@ -462,11 +463,21 @@
     def seam_of(ref, index):
         return lambda site: to_ends(ref[index], site, HALO)
 
-    wet_strip = md.wet_of(strips[2 * FIELDS + 1])
-    wet_pair = beside(wet_strip, HALO - 1, HALO)
-    md.wet = Field(
-        sh, lane, lambda j: wet_ref[j], lambda: wet_strip, lambda site: to_ends(wet_pair, site, HALO)
-    )
+    def prepare():
+        build_strips()
+        wet_strip = md.wet_of(strips[2 * FIELDS + 1])
+        wet_pair = beside(wet_strip, HALO - 1, HALO)
+        md.wet = Field(
+            sh,
+            lane,
+            lambda j: wet_ref[j],
+            lambda: wet_strip,
+            lambda site: to_ends(wet_pair, site, HALO),
+        )
+        d = [strip_field(ch) for ch in range(FIELDS)]
+        c = [strip_field(FIELDS + ch) for ch in range(FIELDS)]
+        pressure = md.pressure(d, STRIP)
+        return d, c, Field(sh, lane, strip=lambda: pressure)
 
     def strip_field(index):
         return Field(sh, lane, strip=lambda: strips[index])
@@ -502,10 +513,6 @@
                 md.odd_x, k_values[cx - 1 - i], k_values[i]
             )
 
-    d = [strip_field(ch) for ch in range(FIELDS)]
-    c = [strip_field(FIELDS + ch) for ch in range(FIELDS)]
-    strip_pressure = md.pressure(d, STRIP)
-    pressure = Field(sh, lane, strip=lambda: strip_pressure)
     done = {}
 
     def keep(ch, site, value):
@@ -513,6 +520,7 @@
 
     @pl.when(md.core0)
     def _():
+        d, c, pressure = prepare()
         md.first_core_site(d, c, pressure, STRIP, rim, True)
         d1 = [renewed(ch, md.own if ch == V else md.first_step) for ch in range(FIELDS)]
         c1 = {i: renewed(GRAZED[i - 2], md.own) for i in (2, 3)}
@@ -526,6 +534,7 @@
 
     @pl.when(jnp.logical_not(md.core0))
     def _():
+        d, c, pressure = prepare()
         md.second_core_site(d, c, pressure, STRIP, rim, True)
         c1 = [renewed(ch, md.first_step) for ch in range(FIELDS)]
         d1 = [renewed(FLOW[ch], md.first_step if ch == U else md.own) for ch in range(4)]

time: 23.2 us -> 23.1 us (level)
  Pallas kernels: 3.07 us -> 2.82 us
    pallas_call x5, Pallas kernels: 3.07 us -> 2.82 us  [call(): pl.pallas_call(lambda *refs: kernel(sh, *refs), out_shape=outs, in_specs=...]
where the time goes in v4:
time: 23.1 us; the launch traced here: 22.7 us
  starting transfers between devices  12 us (52%)
  waiting for transfers between devices  7.88 us (34%)
  Pallas kernels  2.82 us (12%)
    ppermute x7, starting transfers between devices, send(): return lax.ppermute(value, axes, pairs)  12 us
    ppermute x7, waiting for transfers between devices, send(): return lax.ppermute(value, axes, pairs)  7.88 us
    pallas_call x5, Pallas kernels, call(): pl.pallas_call(lambda *refs: kernel(sh, *refs), out_shape=outs, in_specs=...  2.82 us
  transfers between devices with their start and end apart: 7, of which 6 were waited for; matrix products, arithmetic and copies ran while one was open for 0% of the time, Pallas kernels for 7%

profile of v4, /device:TPU:1, one launch (start us, length us, event | category | flops | bytes accessed | tf_op | source)
XLA Modules:
  0.0 22.7 jit_solution(13885755465900477297)
XLA Ops:
  0.0 0.0 collective-permute-start
  0.0 1.1 %shard_map.46 = (f32[33,8,128]{2,1,0:T(8,128)S(1)}, f32[3,8,128]{2,1,0:T(8,128)S(1)}) custom-call(f32[256,128]{1,0:T(8,128)} %bitcast.3, f32[4,128]{1,0:T(4,128)} %refs_1_.1, s32[4,128]{1,0:T(4,128)} %refs_2_.1, s32[4,128]{1,0:T(4,128)} %refs_3_.1), custom_call_target="tpu_custom_call" | custom-call | flops 100000 | bytes 284672 | tf_op jit(solution)/shard_map/pallas_call | solution.py:554
  1.1 0.5 %collective-permute-done.refs_0_ = f32[256,128]{1,0:T(8,128)S(1)} collective-permute-done((f32[256,128]{1,0:T(8,128)}, f32[256,128]{1,0:T(8,128)S(1)}, u32[]{:S(2)}, u32[]{:S(2)}) %collective-permute-start) | collective-permute-done | bytes 131104 | tf_op jit(solution)/shard_map/ppermute | solution.py:580
  1.6 0.1 shard_map.47
  1.7 2.5 %collective-permute-start.1 = (f32[33,8,128]{2,1,0:T(8,128)S(1)}, f32[33,8,128]{2,1,0:T(8,128)S(1)}, u32[]{:S(2)}, u32[]{:S(2)}) collective-permute-start(f32[33,8,128]{2,1,0:T(8,128)S(1)} %get-tuple-element.15), channel_id=1, source_target_pairs={{0,3},{1,2},{2,1},{3,0},{4,7},{5,6},{6,5},{7,4},{8,11},{9,10},{10,... | collective-permute-start | bytes 405512 | tf_op jit(solution)/shard_map/ppermute | solution.py:580
  4.2 2.4 %collective-permute-done.1.refs_2_ = f32[33,8,128]{2,1,0:T(8,128)S(1)} collective-permute-done((f32[33,8,128]{2,1,0:T(8,128)S(1)}, f32[33,8,128]{2,1,0:T(8,128)S(1)}, u32[]{:S(2)}, u32[]{:S(2)}) %collective-permute-start.1) | collective-permute-done | bytes 135200 | tf_op jit(solution)/shard_map/ppermute | solution.py:580
  6.6 4.3 %collective-permute-start.2 = (f32[33,8,128]{2,1,0:T(8,128)S(1)}, f32[33,8,128]{2,1,0:T(8,128)S(1)}, u32[]{:S(2)}, u32[]{:S(2)}) collective-permute-start(f32[33,8,128]{2,1,0:T(8,128)S(1)} %collective-permute-done.1.refs_2_), channel_id=1, source_target_pairs={{0,16},{1,17},{2,18},{3,19},{4,20},{5,21},{6,22},{7,23},{8,24},{9,... | collective-permute-start | bytes 405512 | tf_op jit(solution)/shard_map/ppermute | solution.py:580
  10.9 2.5 %collective-permute-start.3 = (f32[5,8,128]{2,1,0:T(8,128)S(1)}, f32[5,8,128]{2,1,0:T(8,128)S(1)}, u32[]{:S(2)}, u32[]{:S(2)}) collective-permute-start(f32[5,8,128]{2,1,0:T(8,128)S(1)} %get-tuple-element.18.refs_0_), channel_id=1, source_target_pairs={{0,1},{1,0},{2,3},{3,2},{4,5},{5,4},{6,7},{7,6},{8,9},{9,8},{10,11... | collective-permute-start | bytes 61448 | tf_op jit(solution)/shard_map/ppermute | solution.py:580
  13.4 2.0 %collective-permute-done.3.refs_1_ = f32[5,8,128]{2,1,0:T(8,128)S(1)} collective-permute-done((f32[5,8,128]{2,1,0:T(8,128)S(1)}, f32[5,8,128]{2,1,0:T(8,128)S(1)}, u32[]{:S(2)}, u32[]{:S(2)}) %collective-permute-start.3) | collective-permute-done | bytes 20512 | tf_op jit(solution)/shard_map/ppermute | solution.py:580
  15.3 0.0 collective-permute-start.4
  15.3 1.2 %collective-permute-done.4.refs_2_ = f32[5,8,128]{2,1,0:T(8,128)S(1)} collective-permute-done((f32[5,8,128]{2,1,0:T(8,128)S(1)}, f32[5,8,128]{2,1,0:T(8,128)S(1)}, u32[]{:S(2)}, u32[]{:S(2)}) %collective-permute-start.4) | collective-permute-done | bytes 20512 | tf_op jit(solution)/shard_map/ppermute | solution.py:580
  16.5 0.1 shard_map.49.refs_3_
  16.6 2.2 %collective-permute-start.5 = (f32[5,8,128]{2,1,0:T(8,128)S(1)}, f32[5,8,128]{2,1,0:T(8,128)S(1)}, u32[]{:S(2)}, u32[]{:S(2)}) collective-permute-start(f32[5,8,128]{2,1,0:T(8,128)S(1)} %shard_map.49.refs_3_), channel_id=1, source_target_pairs={{0,4},{1,5},{2,6},{3,7},{4,0},{5,1},{6,2},{7,3},{8,12},{9,13},{10,... | collective-permute-start | bytes 61448 | tf_op jit(solution)/shard_map/ppermute | solution.py:580
  18.8 1.4 %collective-permute-done.5.refs_4_ = f32[5,8,128]{2,1,0:T(8,128)S(1)} collective-permute-done((f32[5,8,128]{2,1,0:T(8,128)S(1)}, f32[5,8,128]{2,1,0:T(8,128)S(1)}, u32[]{:S(2)}, u32[]{:S(2)}) %collective-permute-start.5) | collective-permute-done | bytes 20512 | tf_op jit(solution)/shard_map/ppermute | solution.py:580
  20.2 0.4 %collective-permute-start.6 = (f32[5,8,128]{2,1,0:T(8,128)S(1)}, f32[5,8,128]{2,1,0:T(8,128)S(1)}, u32[]{:S(2)}, u32[]{:S(2)}) collective-permute-start(f32[5,8,128]{2,1,0:T(8,128)S(1)} %collective-permute-done.5.refs_4_), channel_id=1, source_target_pairs={{0,16},{1,17},{2,18},{3,19},{4,20},{5,21},{6,22},{7,23},{8,24},{9,... | collective-permute-start | bytes 61448 | tf_op jit(solution)/shard_map/ppermute | solution.py:580
  20.6 0.0 collective-permute-done.2.refs_3_
  20.6 0.3 %shard_map.48 = (f32[72,8,128]{2,1,0:T(8,128)S(1)}, f32[8,8,128]{2,1,0:T(8,128)S(1)}) custom-call(f32[33,8,128]{2,1,0:T(8,128)S(1)} %get-tuple-element.12.refs_1_.refs_0_, f32[32,8,128]{2,1,0:T(8,128)S(1)} %get-tuple-element.14.refs_1_, f32[33,8,128]{2,1,0:T(8,128)S(1)} %collective-permute-done.1.refs_2_, f32[33,8,128]{2,1,0:T(8,128)S(1)} %collective-permute-done.2.refs_3_), custom_call_target="tpu_custom_call" | custom-call | flops 1000000 | bytes 864256 | tf_op jit(solution)/shard_map/pallas_call | solution.py:554
  21.0 0.5 %collective-permute-done.6.refs_5_ = f32[5,8,128]{2,1,0:T(8,128)S(1)} collective-permute-done((f32[5,8,128]{2,1,0:T(8,128)S(1)}, f32[5,8,128]{2,1,0:T(8,128)S(1)}, u32[]{:S(2)}, u32[]{:S(2)}) %collective-permute-start.6) | collective-permute-done | bytes 20512 | tf_op jit(solution)/shard_map/ppermute | solution.py:580
  21.5 1.2 %shard_map.50 = f32[256,128]{1,0:T(8,128)} custom-call(f32[33,8,128]{2,1,0:T(8,128)S(1)} %get-tuple-element.12.refs_1_.refs_0_, f32[8,8,128]{2,1,0:T(8,128)S(1)} %get-tuple-element.16.refs_1_, f32[72,8,128]{2,1,0:T(8,128)S(1)} %get-tuple-element.17.refs_2_, f32[5,8,128]{2,1,0:T(8,128)S(1)} %shard_map.49.refs_3_, ...), custom_call_target="tpu_custom_call" | custom-call | flops 1000000 | bytes 655360 | tf_op jit(solution)/shard_map/pallas_call | solution.py:554
Async XLA Ops:
  0.0 1.6 %collective-permute-start = (f32[256,128]{1,0:T(8,128)}, f32[256,128]{1,0:T(8,128)S(1)}, u32[]{:S(2)}, u32[]{:S(2)}) collective-permute-start(f32[256,128]{1,0:T(8,128)} %bitcast.2), channel_id=1, source_target_pairs={{0,16},{1,17},{2,18},{3,19},{4,20},{5,21},{6,22},{7,23},{8,24},{9,... | collective-permute-start | bytes 393224 | tf_op jit(solution)/shard_map/ppermute | solution.py:580
  1.7 4.9 %collective-permute-start.1 = (f32[33,8,128]{2,1,0:T(8,128)S(1)}, f32[33,8,128]{2,1,0:T(8,128)S(1)}, u32[]{:S(2)}, u32[]{:S(2)}) collective-permute-start(f32[33,8,128]{2,1,0:T(8,128)S(1)} %get-tuple-element.15), channel_id=1, source_target_pairs={{0,3},{1,2},{2,1},{3,0},{4,7},{5,6},{6,5},{7,4},{8,11},{9,10},{10,... | collective-permute-start | bytes 405512 | tf_op jit(solution)/shard_map/ppermute | solution.py:580
  6.6 14.1 %collective-permute-start.2 = (f32[33,8,128]{2,1,0:T(8,128)S(1)}, f32[33,8,128]{2,1,0:T(8,128)S(1)}, u32[]{:S(2)}, u32[]{:S(2)}) collective-permute-start(f32[33,8,128]{2,1,0:T(8,128)S(1)} %collective-permute-done.1.refs_2_), channel_id=1, source_target_pairs={{0,16},{1,17},{2,18},{3,19},{4,20},{5,21},{6,22},{7,23},{8,24},{9,... | collective-permute-start | bytes 405512 | tf_op jit(solution)/shard_map/ppermute | solution.py:580
  10.9 4.4 %collective-permute-start.3 = (f32[5,8,128]{2,1,0:T(8,128)S(1)}, f32[5,8,128]{2,1,0:T(8,128)S(1)}, u32[]{:S(2)}, u32[]{:S(2)}) collective-permute-start(f32[5,8,128]{2,1,0:T(8,128)S(1)} %get-tuple-element.18.refs_0_), channel_id=1, source_target_pairs={{0,1},{1,0},{2,3},{3,2},{4,5},{5,4},{6,7},{7,6},{8,9},{9,8},{10,11... | collective-permute-start | bytes 61448 | tf_op jit(solution)/shard_map/ppermute | solution.py:580
  15.3 1.2 %collective-permute-start.4 = (f32[5,8,128]{2,1,0:T(8,128)S(1)}, f32[5,8,128]{2,1,0:T(8,128)S(1)}, u32[]{:S(2)}, u32[]{:S(2)}) collective-permute-start(f32[5,8,128]{2,1,0:T(8,128)S(1)} %collective-permute-done.3.refs_1_), channel_id=1, source_target_pairs={{0,16},{1,17},{2,18},{3,19},{4,20},{5,21},{6,22},{7,23},{8,24},{9,... | collective-permute-start | bytes 61448 | tf_op jit(solution)/shard_map/ppermute | solution.py:580
  16.6 3.6 %collective-permute-start.5 = (f32[5,8,128]{2,1,0:T(8,128)S(1)}, f32[5,8,128]{2,1,0:T(8,128)S(1)}, u32[]{:S(2)}, u32[]{:S(2)}) collective-permute-start(f32[5,8,128]{2,1,0:T(8,128)S(1)} %shard_map.49.refs_3_), channel_id=1, source_target_pairs={{0,4},{1,5},{2,6},{3,7},{4,0},{5,1},{6,2},{7,3},{8,12},{9,13},{10,... | collective-permute-start | bytes 61448 | tf_op jit(solution)/shard_map/ppermute | solution.py:580
  20.2 1.3 %collective-permute-start.6 = (f32[5,8,128]{2,1,0:T(8,128)S(1)}, f32[5,8,128]{2,1,0:T(8,128)S(1)}, u32[]{:S(2)}, u32[]{:S(2)}) collective-permute-start(f32[5,8,128]{2,1,0:T(8,128)S(1)} %collective-permute-done.5.refs_4_), channel_id=1, source_target_pairs={{0,16},{1,17},{2,18},{3,19},{4,20},{5,21},{6,22},{7,23},{8,24},{9,... | collective-permute-start | bytes 61448 | tf_op jit(solution)/shard_map/ppermute | solution.py:580

commit v5 on v4

--- a/solution.py
+++ b/solution.py
@@ -32,7 +32,7 @@
         self.field_tiles = -(-FIELDS // self.per_tile)
         self.edge_tiles = 2 * self.field_tiles + 1
         assert self.per_tile >= 2 and self.group >= 4 * HALO and 2 * cx <= lev
-        assert self.cols * self.group == rows
+        assert self.cols * self.group == rows and HALO * 2 * self.field_tiles <= self.cols
         self.mask_tile = FIELDS * cx
         self.halo_tiles = FIELDS * HALO
 
@@ -52,13 +52,16 @@
     def halo_at(self, comp, side, ch, d):
         return (self.halo_tiles if comp == side else 0) + ch * HALO + d
 
+    def near_block(self, part, t, d):
+        return (d * 2 + part) * self.field_tiles + t
+
     def edge_place(self, acc, value, j, channel, lane):
-        at = j * self.group + channel * 2 * HALO + HALO
+        at = (j * self.group + channel * 2 * HALO + HALO) % self.rows
         return jnp.where((lane >= at - HALO) & (lane < at + HALO), lane_roll(value, at), acc)
 
 
 def load_kernel(sh, *refs):
-    sources, x_ref, e_ref, arrived, sem = refs[:4], refs[4], refs[5], refs[6:10], refs[10]
+    sources, x_ref, near_ref, arrived, sem = refs[:4], refs[4], refs[5], refs[6:10], refs[10]
     copies = [
         pltpu.make_async_copy(a, b, sem.at[i]) for i, (a, b) in enumerate(zip(sources, arrived))
     ]
@@ -67,20 +70,42 @@
     for copy in copies:
         copy.wait()
     state_ref, irr_ref, land_ref, bottom_ref = arrived
-    odd = is_odd("gx")
-    edges = own_columns(sh, state_ref, x_ref, odd, first_core())
+    odd, core0 = is_odd("gx"), first_core()
+    zero = jnp.zeros((sh.lev, sh.rows), jnp.float32)
+    own_columns(sh, state_ref, x_ref, odd, core0)
+    near_ref[0] = near_edges(sh, x_ref, 0, core0, zero)
     cx = sh.cx
     lane = sh.lanes()
     depth = jnp.where(land_ref[...] == 1, bottom_ref[...], 0).astype(jnp.float32)
-    last = jnp.zeros((sh.lev, sh.rows), jnp.float32)
+    masks = zero
     for q, value in enumerate((irr_ref[...], depth)):
+        rows = [
+            jnp.where(odd, value[cx - 1 - k : cx - k, :], value[k : k + 1, :]) for k in range(cx)
+        ]
         for k in range(cx):
-            row = jnp.where(odd, value[cx - 1 - k : cx - k, :], value[k : k + 1, :])
-            x_ref[sh.mask_tile, q * cx + k : q * cx + k + 1, :] = row
+            x_ref[sh.mask_tile, q * cx + k : q * cx + k + 1, :] = rows[k]
+        for d in range(HALO):
+            row = jnp.where(core0, rows[cx - 1 - d], rows[d])
             wide = jnp.broadcast_to(row, (sh.lev, sh.rows))
-            last = sh.edge_place(last, wide, k + HALO, q, lane)
-    for t, edge in enumerate(edges + [last]):
-        e_ref[t] = edge
+            masks = sh.edge_place(masks, wide, d, q, lane)
+    near_ref[1] = masks
+
+
+def near_edges(sh, x_ref, part, core0, acc):
+    lane = sh.lanes()
+    flip = turned(part, core0)
+    for ch in range(FIELDS):
+        t, q = sh.edge_at(0, ch)
+        for d in range(HALO):
+            value = jnp.where(core0, x_ref[ch * sh.cx + sh.cx - 1 - d], x_ref[ch * sh.cx + d])
+            if ch in VEL_X:
+                value = value * flip
+            acc = sh.edge_place(acc, value, sh.near_block(part, t, d), q, lane)
+    return acc
+
+
+def turned(part, core0):
+    return jnp.where(core0, -1.0, 1.0) if part == 0 else jnp.where(core0, 1.0, -1.0)
 
 
 def is_odd(axis):
@@ -94,56 +119,68 @@
 def own_columns(sh, state_ref, x_ref, odd, dynamics):
     flip = jnp.where(odd & dynamics, -1.0, 1.0)
     cx = sh.cx
-    lane = sh.lanes()
-    edges = [jnp.zeros((sh.lev, sh.rows), jnp.float32)] * sh.field_tiles
     for ch in range(FIELDS):
         raw = [state_ref[pl.ds(ch * sh.lev * cx + i, sh.lev, stride=cx), :] for i in range(cx)]
-        t, q = sh.edge_at(0, ch)
         for k in range(cx):
             value = jnp.where(odd, raw[cx - 1 - k], raw[k])
-            if ch in VEL_X:
-                value = value * flip
-            x_ref[ch * cx + k] = value
-            edges[t] = sh.edge_place(edges[t], value, k + HALO, q, lane)
-    return edges
-
-
-def send_kernel(sh, state_ref, xo_ref, eo_ref, xp_ref, e_ref, m_ref):
+            x_ref[ch * cx + k] = value * flip if ch in VEL_X else value
+
+
+def send_kernel(sh, state_ref, xo_ref, own_ref, xp_ref, near_ref, m_ref):
     core0 = first_core()
-    edges = own_columns(sh, state_ref, xp_ref, is_odd("gx"), jnp.logical_not(core0))
+    own_columns(sh, state_ref, xp_ref, is_odd("gx"), jnp.logical_not(core0))
+    near_ref[0] = near_edges(sh, xp_ref, 1, core0, own_ref[0])
+    near_ref[1] = own_ref[1]
     cx = sh.cx
-    for t in range(sh.field_tiles):
-        own = eo_ref[t]
-        e_ref[t] = jnp.where(core0, own, edges[t])
-        e_ref[sh.field_tiles + t] = jnp.where(core0, edges[t], own)
-    e_ref[sh.edge_tiles - 1] = eo_ref[sh.field_tiles]
-    for part, (x_ref, flip) in enumerate(
-        ((xo_ref, jnp.where(core0, -1.0, 1.0)), (xp_ref, jnp.where(core0, 1.0, -1.0)))
-    ):
+    for part, x_ref in enumerate((xo_ref, xp_ref)):
         for ch in range(FIELDS):
             for d in range(HALO):
                 value = jnp.where(core0, x_ref[ch * cx + d], x_ref[ch * cx + cx - 1 - d])
-                m_ref[part * sh.halo_tiles + ch * HALO + d] = value * flip if ch in VEL_X else value
+                if ch in VEL_X:
+                    value = value * turned(part, core0)
+                m_ref[part * sh.halo_tiles + ch * HALO + d] = value
     m_ref[2 * sh.halo_tiles] = xo_ref[sh.mask_tile]
 
 
-def merge_kernel(sh, e_ref, a_ref, b_ref, eo_ref):
+def edge_kernel(sh, xo_ref, xp_ref, e_ref):
     lane = sh.lanes()
     core0 = first_core()
-    column, place = lane // sh.group, lane % sh.group // (2 * HALO)
+    cx = sh.cx
+    edges = [jnp.zeros((sh.lev, sh.rows), jnp.float32)] * sh.edge_tiles
+    for comp in range(2):
+        for ch in range(FIELDS):
+            t, q = sh.edge_at(comp, ch)
+            for k in range(cx):
+                pair = xo_ref[ch * cx + k], xp_ref[ch * cx + k]
+                value = jnp.where(core0, pair[comp], pair[1 - comp])
+                edges[t] = sh.edge_place(edges[t], value, k + HALO, q, lane)
+    for q in range(2):
+        for k in range(cx):
+            value = sh.row(xo_ref, sh.mask_tile, q * cx + k)
+            edges[-1] = sh.edge_place(edges[-1], value, k + HALO, q, lane)
     for t in range(sh.edge_tiles):
-        got = a_ref[t], b_ref[t]
-        after, before = jnp.where(core0, got[0], got[1]), jnp.where(core0, got[1], got[0])
-        for ch in VEL_X:
-            if sh.edge_at(0, ch)[0] == t:
-                flip = jnp.where(place == sh.edge_at(0, ch)[1], -1.0, 1.0)
-                after, before = after * flip, before * flip
-        edge = e_ref[t]
-        for d in range(HALO):
-            shift = (2 * d + 1) * sh.group
-            edge = jnp.where(column == sh.cx + HALO + d, lane_roll(after, shift), edge)
-            edge = jnp.where(column == HALO - 1 - d, lane_roll(before, -shift), edge)
-        eo_ref[t] = edge
+        e_ref[t] = edges[t]
+
+
+def merge_kernel(sh, e_ref, a_ref, b_ref, eo_ref):
+    core0 = first_core()
+    column = sh.lanes() // sh.group
+    got = [
+        (jnp.where(core0, a_ref[i], b_ref[i]), jnp.where(core0, b_ref[i], a_ref[i]))
+        for i in range(2)
+    ]
+    for tile in range(sh.edge_tiles):
+        edge = e_ref[tile]
+        comp, t = divmod(tile, sh.field_tiles)
+        for side in range(2):
+            for d in range(HALO):
+                place = sh.cx + HALO + d if side == 0 else HALO - 1 - d
+                if tile == sh.edge_tiles - 1:
+                    source, block = got[1][side], d
+                else:
+                    source, block = got[0][side], sh.near_block(int(comp != side), t, d)
+                edge = jnp.where(column == place, lane_roll(source, (place - block) * sh.group), edge)
+        eo_ref[tile] = edge
 
 
 STRIP = "strip"
@@ -600,22 +637,24 @@
     flat = ocean_state.reshape(fields * lev * cx, rows)
     partner = swap(flat)
     inputs = (flat, irradiance, land_mask, bottom_level)
-    xo, eo = call(
+    near = tiles(sh, 2)
+    xo, own_near = call(
         load_kernel,
         sh,
-        [tiles(sh, fields * cx + 1), tiles(sh, sh.field_tiles + 1)],
+        [tiles(sh, fields * cx + 1), near],
         tuple(pltpu.with_memory_space_constraint(a, pltpu.HBM) for a in inputs),
         100_000,
         scratch=[pltpu.VMEM(a.shape, a.dtype) for a in inputs] + [pltpu.SemaphoreType.DMA((4,))],
         source=pltpu.HBM,
     )
     edge, message = tiles(sh, sh.edge_tiles), tiles(sh, 2 * sh.halo_tiles + 1)
-    xp, e0, m = call(
-        send_kernel, sh, [tiles(sh, fields * cx), edge, message], (partner, xo, eo), 100_000
+    xp, nx_edges, m = call(
+        send_kernel, sh, [tiles(sh, fields * cx), near, message], (partner, xo, own_near), 100_000
     )
-    ex = edges_x(e0)
+    ex = edges_x(nx_edges)
     rx = bulk_x(m)
     ep = swap(ex)
+    (e0,) = call(edge_kernel, sh, [edge], (xo, xp), 100_000)
     (e1,) = call(merge_kernel, sh, [edge], (e0, ex, ep), 10_000)
     y = along_y(e1)
     rp = swap(rx)

time: 23.1 us -> 22.9 us (level)
  waiting for transfers between devices: 7.88 us -> 7.61 us
    ppermute x7, waiting for transfers between devices: 7.88 us -> 7.61 us  [send(): return lax.ppermute(value, axes, pairs)]
    pallas_call x5 -> x6, Pallas kernels: 2.82 us -> 2.93 us  [call(): pl.pallas_call(lambda *refs: kernel(sh, *refs), out_shape=outs, in_specs=...]
where the time goes in v5:
time: 22.9 us; the launch traced here: 22.5 us
  starting transfers between devices  12 us (52%)
  waiting for transfers between devices  7.61 us (33%)
  Pallas kernels  2.93 us (13%)
    ppermute x7, starting transfers between devices, send(): return lax.ppermute(value, axes, pairs)  12 us
    ppermute x7, waiting for transfers between devices, send(): return lax.ppermute(value, axes, pairs)  7.61 us
    pallas_call x6, Pallas kernels, call(): pl.pallas_call(lambda *refs: kernel(sh, *refs), out_shape=outs, in_specs=...  2.93 us
  transfers between devices with their start and end apart: 7, of which 6 were waited for; matrix products, arithmetic and copies ran while one was open for 0% of the time, Pallas kernels for 7%

profile of v5, /device:TPU:1, one launch (start us, length us, event | category | flops | bytes accessed | tf_op | source)
XLA Modules:
  0.0 22.5 jit_solution(2393891609746919074)
XLA Ops:
  0.0 0.0 collective-permute-start
  0.0 1.0 %shard_map.46 = (f32[33,8,128]{2,1,0:T(8,128)S(1)}, f32[2,8,128]{2,1,0:T(8,128)S(1)}) custom-call(f32[256,128]{1,0:T(8,128)} %bitcast.3, f32[4,128]{1,0:T(4,128)} %refs_1_.1, s32[4,128]{1,0:T(4,128)} %refs_2_.1, s32[4,128]{1,0:T(4,128)} %refs_3_.1), custom_call_target="tpu_custom_call" | custom-call | flops 100000 | bytes 280576 | tf_op jit(solution)/shard_map/pallas_call | solution.py:591
  1.1 0.5 %collective-permute-done.refs_0_ = f32[256,128]{1,0:T(8,128)S(1)} collective-permute-done((f32[256,128]{1,0:T(8,128)}, f32[256,128]{1,0:T(8,128)S(1)}, u32[]{:S(2)}, u32[]{:S(2)}) %collective-permute-start) | collective-permute-done | bytes 131104 | tf_op jit(solution)/shard_map/ppermute | solution.py:617
  1.6 0.1 shard_map.47
  1.7 2.5 %collective-permute-start.1 = (f32[33,8,128]{2,1,0:T(8,128)S(1)}, f32[33,8,128]{2,1,0:T(8,128)S(1)}, u32[]{:S(2)}, u32[]{:S(2)}) collective-permute-start(f32[33,8,128]{2,1,0:T(8,128)S(1)} %get-tuple-element.15), channel_id=1, source_target_pairs={{0,3},{1,2},{2,1},{3,0},{4,7},{5,6},{6,5},{7,4},{8,11},{9,10},{10,... | collective-permute-start | bytes 405512 | tf_op jit(solution)/shard_map/ppermute | solution.py:617
  4.2 2.4 %collective-permute-done.1.refs_2_ = f32[33,8,128]{2,1,0:T(8,128)S(1)} collective-permute-done((f32[33,8,128]{2,1,0:T(8,128)S(1)}, f32[33,8,128]{2,1,0:T(8,128)S(1)}, u32[]{:S(2)}, u32[]{:S(2)}) %collective-permute-start.1) | collective-permute-done | bytes 135200 | tf_op jit(solution)/shard_map/ppermute | solution.py:617
  6.6 4.3 %collective-permute-start.2 = (f32[33,8,128]{2,1,0:T(8,128)S(1)}, f32[33,8,128]{2,1,0:T(8,128)S(1)}, u32[]{:S(2)}, u32[]{:S(2)}) collective-permute-start(f32[33,8,128]{2,1,0:T(8,128)S(1)} %collective-permute-done.1.refs_2_), channel_id=1, source_target_pairs={{0,16},{1,17},{2,18},{3,19},{4,20},{5,21},{6,22},{7,23},{8,24},{9,... | collective-permute-start | bytes 405512 | tf_op jit(solution)/shard_map/ppermute | solution.py:617
  10.9 2.5 %collective-permute-start.3 = (f32[2,8,128]{2,1,0:T(8,128)S(1)}, f32[2,8,128]{2,1,0:T(8,128)S(1)}, u32[]{:S(2)}, u32[]{:S(2)}) collective-permute-start(f32[2,8,128]{2,1,0:T(8,128)S(1)} %get-tuple-element.18), channel_id=1, source_target_pairs={{0,1},{1,0},{2,3},{3,2},{4,5},{5,4},{6,7},{7,6},{8,9},{9,8},{10,11... | collective-permute-start | bytes 24584 | tf_op jit(solution)/shard_map/ppermute | solution.py:617
  13.4 1.8 %collective-permute-done.3.refs_1_ = f32[2,8,128]{2,1,0:T(8,128)S(1)} collective-permute-done((f32[2,8,128]{2,1,0:T(8,128)S(1)}, f32[2,8,128]{2,1,0:T(8,128)S(1)}, u32[]{:S(2)}, u32[]{:S(2)}) %collective-permute-start.3) | collective-permute-done | bytes 8224 | tf_op jit(solution)/shard_map/ppermute | solution.py:617
  15.2 0.0 collective-permute-start.4
  15.2 0.1 shard_map.49.refs_0_
  15.3 1.0 %collective-permute-done.4.refs_2_ = f32[2,8,128]{2,1,0:T(8,128)S(1)} collective-permute-done((f32[2,8,128]{2,1,0:T(8,128)S(1)}, f32[2,8,128]{2,1,0:T(8,128)S(1)}, u32[]{:S(2)}, u32[]{:S(2)}) %collective-permute-start.4) | collective-permute-done | bytes 8224 | tf_op jit(solution)/shard_map/ppermute | solution.py:617
  16.4 0.1 shard_map.50.refs_3_
  16.5 2.2 %collective-permute-start.5 = (f32[5,8,128]{2,1,0:T(8,128)S(1)}, f32[5,8,128]{2,1,0:T(8,128)S(1)}, u32[]{:S(2)}, u32[]{:S(2)}) collective-permute-start(f32[5,8,128]{2,1,0:T(8,128)S(1)} %shard_map.50.refs_3_), channel_id=1, source_target_pairs={{0,4},{1,5},{2,6},{3,7},{4,0},{5,1},{6,2},{7,3},{8,12},{9,13},{10,... | collective-permute-start | bytes 61448 | tf_op jit(solution)/shard_map/ppermute | solution.py:617
  18.7 1.4 %collective-permute-done.5.refs_4_ = f32[5,8,128]{2,1,0:T(8,128)S(1)} collective-permute-done((f32[5,8,128]{2,1,0:T(8,128)S(1)}, f32[5,8,128]{2,1,0:T(8,128)S(1)}, u32[]{:S(2)}, u32[]{:S(2)}) %collective-permute-start.5) | collective-permute-done | bytes 20512 | tf_op jit(solution)/shard_map/ppermute | solution.py:617
  20.1 0.4 %collective-permute-start.6 = (f32[5,8,128]{2,1,0:T(8,128)S(1)}, f32[5,8,128]{2,1,0:T(8,128)S(1)}, u32[]{:S(2)}, u32[]{:S(2)}) collective-permute-start(f32[5,8,128]{2,1,0:T(8,128)S(1)} %collective-permute-done.5.refs_4_), channel_id=1, source_target_pairs={{0,16},{1,17},{2,18},{3,19},{4,20},{5,21},{6,22},{7,23},{8,24},{9,... | collective-permute-start | bytes 61448 | tf_op jit(solution)/shard_map/ppermute | solution.py:617
  20.5 0.0 collective-permute-done.2.refs_3_
  20.5 0.3 %shard_map.48 = (f32[72,8,128]{2,1,0:T(8,128)S(1)}, f32[8,8,128]{2,1,0:T(8,128)S(1)}) custom-call(f32[33,8,128]{2,1,0:T(8,128)S(1)} %get-tuple-element.12.refs_1_.refs_0_, f32[32,8,128]{2,1,0:T(8,128)S(1)} %get-tuple-element.14.refs_1_, f32[33,8,128]{2,1,0:T(8,128)S(1)} %collective-permute-done.1.refs_2_, f32[33,8,128]{2,1,0:T(8,128)S(1)} %collective-permute-done.2.refs_3_), custom_call_target="tpu_custom_call" | custom-call | flops 1000000 | bytes 864256 | tf_op jit(solution)/shard_map/pallas_call | solution.py:591
  20.8 0.5 %collective-permute-done.6.refs_5_ = f32[5,8,128]{2,1,0:T(8,128)S(1)} collective-permute-done((f32[5,8,128]{2,1,0:T(8,128)S(1)}, f32[5,8,128]{2,1,0:T(8,128)S(1)}, u32[]{:S(2)}, u32[]{:S(2)}) %collective-permute-start.6) | collective-permute-done | bytes 20512 | tf_op jit(solution)/shard_map/ppermute | solution.py:617
  21.3 1.2 %shard_map.51 = f32[256,128]{1,0:T(8,128)} custom-call(f32[33,8,128]{2,1,0:T(8,128)S(1)} %get-tuple-element.12.refs_1_.refs_0_, f32[8,8,128]{2,1,0:T(8,128)S(1)} %get-tuple-element.16.refs_1_, f32[72,8,128]{2,1,0:T(8,128)S(1)} %get-tuple-element.17.refs_2_, f32[5,8,128]{2,1,0:T(8,128)S(1)} %shard_map.50.refs_3_, ...), custom_call_target="tpu_custom_call" | custom-call | flops 1000000 | bytes 655360 | tf_op jit(solution)/shard_map/pallas_call | solution.py:591
Async XLA Ops:
  0.0 1.6 %collective-permute-start = (f32[256,128]{1,0:T(8,128)}, f32[256,128]{1,0:T(8,128)S(1)}, u32[]{:S(2)}, u32[]{:S(2)}) collective-permute-start(f32[256,128]{1,0:T(8,128)} %bitcast.2), channel_id=1, source_target_pairs={{0,16},{1,17},{2,18},{3,19},{4,20},{5,21},{6,22},{7,23},{8,24},{9,... | collective-permute-start | bytes 393224 | tf_op jit(solution)/shard_map/ppermute | solution.py:617
  1.7 4.9 %collective-permute-start.1 = (f32[33,8,128]{2,1,0:T(8,128)S(1)}, f32[33,8,128]{2,1,0:T(8,128)S(1)}, u32[]{:S(2)}, u32[]{:S(2)}) collective-permute-start(f32[33,8,128]{2,1,0:T(8,128)S(1)} %get-tuple-element.15), channel_id=1, source_target_pairs={{0,3},{1,2},{2,1},{3,0},{4,7},{5,6},{6,5},{7,4},{8,11},{9,10},{10,... | collective-permute-start | bytes 405512 | tf_op jit(solution)/shard_map/ppermute | solution.py:617
  6.6 13.9 %collective-permute-start.2 = (f32[33,8,128]{2,1,0:T(8,128)S(1)}, f32[33,8,128]{2,1,0:T(8,128)S(1)}, u32[]{:S(2)}, u32[]{:S(2)}) collective-permute-start(f32[33,8,128]{2,1,0:T(8,128)S(1)} %collective-permute-done.1.refs_2_), channel_id=1, source_target_pairs={{0,16},{1,17},{2,18},{3,19},{4,20},{5,21},{6,22},{7,23},{8,24},{9,... | collective-permute-start | bytes 405512 | tf_op jit(solution)/shard_map/ppermute | solution.py:617
  10.9 4.3 %collective-permute-start.3 = (f32[2,8,128]{2,1,0:T(8,128)S(1)}, f32[2,8,128]{2,1,0:T(8,128)S(1)}, u32[]{:S(2)}, u32[]{:S(2)}) collective-permute-start(f32[2,8,128]{2,1,0:T(8,128)S(1)} %get-tuple-element.18), channel_id=1, source_target_pairs={{0,1},{1,0},{2,3},{3,2},{4,5},{5,4},{6,7},{7,6},{8,9},{9,8},{10,11... | collective-permute-start | bytes 24584 | tf_op jit(solution)/shard_map/ppermute | solution.py:617
  15.2 1.2 %collective-permute-start.4 = (f32[2,8,128]{2,1,0:T(8,128)S(1)}, f32[2,8,128]{2,1,0:T(8,128)S(1)}, u32[]{:S(2)}, u32[]{:S(2)}) collective-permute-start(f32[2,8,128]{2,1,0:T(8,128)S(1)} %collective-permute-done.3.refs_1_), channel_id=1, source_target_pairs={{0,16},{1,17},{2,18},{3,19},{4,20},{5,21},{6,22},{7,23},{8,24},{9,... | collective-permute-start | bytes 24584 | tf_op jit(solution)/shard_map/ppermute | solution.py:617
  16.5 3.6 %collective-permute-start.5 = (f32[5,8,128]{2,1,0:T(8,128)S(1)}, f32[5,8,128]{2,1,0:T(8,128)S(1)}, u32[]{:S(2)}, u32[]{:S(2)}) collective-permute-start(f32[5,8,128]{2,1,0:T(8,128)S(1)} %shard_map.50.refs_3_), channel_id=1, source_target_pairs={{0,4},{1,5},{2,6},{3,7},{4,0},{5,1},{6,2},{7,3},{8,12},{9,13},{10,... | collective-permute-start | bytes 61448 | tf_op jit(solution)/shard_map/ppermute | solution.py:617
  20.1 1.3 %collective-permute-start.6 = (f32[5,8,128]{2,1,0:T(8,128)S(1)}, f32[5,8,128]{2,1,0:T(8,128)S(1)}, u32[]{:S(2)}, u32[]{:S(2)}) collective-permute-start(f32[5,8,128]{2,1,0:T(8,128)S(1)} %collective-permute-done.5.refs_4_), channel_id=1, source_target_pairs={{0,16},{1,17},{2,18},{3,19},{4,20},{5,21},{6,22},{7,23},{8,24},{9,... | collective-permute-start | bytes 61448 | tf_op jit(solution)/shard_map/ppermute | solution.py:617

commit v6 on v5

--- a/solution.py
+++ b/solution.py
@@ -109,7 +109,7 @@
 
 
 def is_odd(axis):
-    return lax.axis_index(axis) % 2 == 1
+    return lax.axis_index(axis) & 1 == 1
 
 
 def first_core():
@@ -460,13 +460,13 @@
     md = Model(sh)
     cx, lane, in_group = sh.cx, md.lane, md.in_group
     end = sh.rows - 1
-    even_y = md.gy % 2 == 0
+    even_y = md.gy & 1 == 0
     slot = lane % (2 * HALO)
     zero = jnp.zeros((sh.lev, sh.rows), jnp.float32)
 
-    def build_strips():
+    def build_strips(tracers):
         strips_of(2 * FIELDS, [sh.edge_tiles - 1], 2)
-        strips_of(0, range(2 * sh.field_tiles), sh.per_tile)
+        strips_of(0, range(2 * sh.field_tiles), FIELDS + tracers)
 
     def strips_of(base, tiles, channels):
         for t in tiles:
@@ -476,9 +476,10 @@
             right = jnp.where(md.gy < md.ny - 1, jnp.where(even_y, a, b), zero)
             low = jnp.where(slot < HALO, left, mine)
             high = jnp.where(slot < HALO, mine, right)
-            for q in range(channels):
+            first = (t - tiles[0]) * sh.per_tile
+            for q in range(min(channels - first, sh.per_tile)):
                 at = q * 2 * HALO
-                strips[base + (t - tiles[0]) * sh.per_tile + q] = jnp.where(
+                strips[base + first + q] = jnp.where(
                     in_group < sh.half, lane_roll(low, -at), lane_roll(high, sh.half - at)
                 )
 
@@ -500,8 +501,8 @@
     def seam_of(ref, index):
         return lambda site: to_ends(ref[index], site, HALO)
 
-    def prepare():
-        build_strips()
+    def prepare(tracers):
+        build_strips(tracers)
         wet_strip = md.wet_of(strips[2 * FIELDS + 1])
         wet_pair = beside(wet_strip, HALO - 1, HALO)
         md.wet = Field(
@@ -522,25 +523,35 @@
     def rim(index, site, value):
         rims[index] = value
 
-    def renewed(index, sites):
+    def straight(strip, site, low, high):
+        back = lane_roll(strip, end - (site * sh.group + sh.half + high))
+        front = lane_roll(strip, -(site * sh.group + low))
+        return jnp.where(lane < sh.half, front, back)
+
+    def renewed(index, sites, quick=False):
         value = rims[index]
-        seams[index] = beside(value, HALO - 1, HALO)
+        if not quick:
+            seams[index] = beside(value, HALO - 1, HALO)
         ends = beside(value, HALO, HALO - 1)
         for site in sites:
+            if quick:
+                rows = straight(value, site, HALO, HALO - 1)
+            else:
+                rows = to_ends(ends, site, HALO - 1)
             cols[md.fresh_at(index, site)] = jnp.where(
-                (lane == 0) | (lane == end),
-                to_ends(ends, site, HALO - 1),
-                fresh[md.fresh_at(index, site)],
+                (lane == 0) | (lane == end), rows, fresh[md.fresh_at(index, site)]
             )
-        return stored(index)
-
-    def stored(index):
+        return stored(index, quick)
+
+    def stored(index, quick):
         return Field(
             sh,
             lane,
             lambda j: cols[md.fresh_at(index, j)],
             lambda: rims[index],
-            seam_of(seams, index),
+            (lambda site: straight(rims[index], site, HALO - 1, HALO))
+            if quick
+            else seam_of(seams, index),
             lambda j: fresh[md.fresh_at(index, j)],
         )
 
@@ -557,12 +568,12 @@
 
     @pl.when(md.core0)
     def _():
-        d, c, pressure = prepare()
+        d, c, pressure = prepare(5)
         md.first_core_site(d, c, pressure, STRIP, rim, True)
         d1 = [renewed(ch, md.own if ch == V else md.first_step) for ch in range(FIELDS)]
         c1 = {i: renewed(GRAZED[i - 2], md.own) for i in (2, 3)}
         rim(PRESSURE, STRIP, md.pressure(d1, STRIP))
-        pressure1 = renewed(PRESSURE, md.first_step)
+        pressure1 = renewed(PRESSURE, md.first_step, True)
         for site in md.own:
             md.first_core_site(d1, c1, pressure1, site, keep, False)
         for ch in range(FIELDS):
@@ -571,7 +582,7 @@
 
     @pl.when(jnp.logical_not(md.core0))
     def _():
-        d, c, pressure = prepare()
+        d, c, pressure = prepare(FIELDS)
         md.second_core_site(d, c, pressure, STRIP, rim, True)
         c1 = [renewed(ch, md.first_step) for ch in range(FIELDS)]
         d1 = [renewed(FLOW[ch], md.first_step if ch == U else md.own) for ch in range(4)]

time: 22.9 us -> 22.9 us (level)
  no operation moved by 1% of the time
where the time goes in v6:
time: 22.9 us; the launch traced here: 22.5 us
  starting transfers between devices  12 us (52%)
  waiting for transfers between devices  7.6 us (33%)
  Pallas kernels  2.94 us (13%)
    ppermute x7, starting transfers between devices, send(): return lax.ppermute(value, axes, pairs)  12 us
    ppermute x7, waiting for transfers between devices, send(): return lax.ppermute(value, axes, pairs)  7.6 us
    pallas_call x6, Pallas kernels, call(): pl.pallas_call(lambda *refs: kernel(sh, *refs), out_shape=outs, in_specs=...  2.94 us
  transfers between devices with their start and end apart: 7, of which 6 were waited for; matrix products, arithmetic and copies ran while one was open for 0% of the time, Pallas kernels for 7%

profile of v6, /device:TPU:1, one launch (start us, length us, event | category | flops | bytes accessed | tf_op | source)
XLA Modules:
  0.0 22.5 jit_solution(9831302276542990023)
XLA Ops:
  0.0 0.0 collective-permute-start
  0.0 1.0 %shard_map.46 = (f32[33,8,128]{2,1,0:T(8,128)S(1)}, f32[2,8,128]{2,1,0:T(8,128)S(1)}) custom-call(f32[256,128]{1,0:T(8,128)} %bitcast.3, f32[4,128]{1,0:T(4,128)} %refs_1_.1, s32[4,128]{1,0:T(4,128)} %refs_2_.1, s32[4,128]{1,0:T(4,128)} %refs_3_.1), custom_call_target="tpu_custom_call" | custom-call | flops 100000 | bytes 280576 | tf_op jit(solution)/shard_map/pallas_call | solution.py:602
  1.1 0.5 %collective-permute-done.refs_0_ = f32[256,128]{1,0:T(8,128)S(1)} collective-permute-done((f32[256,128]{1,0:T(8,128)}, f32[256,128]{1,0:T(8,128)S(1)}, u32[]{:S(2)}, u32[]{:S(2)}) %collective-permute-start) | collective-permute-done | bytes 131104 | tf_op jit(solution)/shard_map/ppermute | solution.py:628
  1.6 0.1 shard_map.47
  1.7 2.5 %collective-permute-start.1 = (f32[33,8,128]{2,1,0:T(8,128)S(1)}, f32[33,8,128]{2,1,0:T(8,128)S(1)}, u32[]{:S(2)}, u32[]{:S(2)}) collective-permute-start(f32[33,8,128]{2,1,0:T(8,128)S(1)} %get-tuple-element.15), channel_id=1, source_target_pairs={{0,3},{1,2},{2,1},{3,0},{4,7},{5,6},{6,5},{7,4},{8,11},{9,10},{10,... | collective-permute-start | bytes 405512 | tf_op jit(solution)/shard_map/ppermute | solution.py:628
  4.2 2.4 %collective-permute-done.1.refs_2_ = f32[33,8,128]{2,1,0:T(8,128)S(1)} collective-permute-done((f32[33,8,128]{2,1,0:T(8,128)S(1)}, f32[33,8,128]{2,1,0:T(8,128)S(1)}, u32[]{:S(2)}, u32[]{:S(2)}) %collective-permute-start.1) | collective-permute-done | bytes 135200 | tf_op jit(solution)/shard_map/ppermute | solution.py:628
  6.6 4.3 %collective-permute-start.2 = (f32[33,8,128]{2,1,0:T(8,128)S(1)}, f32[33,8,128]{2,1,0:T(8,128)S(1)}, u32[]{:S(2)}, u32[]{:S(2)}) collective-permute-start(f32[33,8,128]{2,1,0:T(8,128)S(1)} %collective-permute-done.1.refs_2_), channel_id=1, source_target_pairs={{0,16},{1,17},{2,18},{3,19},{4,20},{5,21},{6,22},{7,23},{8,24},{9,... | collective-permute-start | bytes 405512 | tf_op jit(solution)/shard_map/ppermute | solution.py:628
  10.9 2.5 %collective-permute-start.3 = (f32[2,8,128]{2,1,0:T(8,128)S(1)}, f32[2,8,128]{2,1,0:T(8,128)S(1)}, u32[]{:S(2)}, u32[]{:S(2)}) collective-permute-start(f32[2,8,128]{2,1,0:T(8,128)S(1)} %get-tuple-element.18), channel_id=1, source_target_pairs={{0,1},{1,0},{2,3},{3,2},{4,5},{5,4},{6,7},{7,6},{8,9},{9,8},{10,11... | collective-permute-start | bytes 24584 | tf_op jit(solution)/shard_map/ppermute | solution.py:628
  13.4 1.8 %collective-permute-done.3.refs_1_ = f32[2,8,128]{2,1,0:T(8,128)S(1)} collective-permute-done((f32[2,8,128]{2,1,0:T(8,128)S(1)}, f32[2,8,128]{2,1,0:T(8,128)S(1)}, u32[]{:S(2)}, u32[]{:S(2)}) %collective-permute-start.3) | collective-permute-done | bytes 8224 | tf_op jit(solution)/shard_map/ppermute | solution.py:628
  15.2 0.0 collective-permute-start.4
  15.2 0.1 shard_map.49.refs_0_
  15.3 1.0 %collective-permute-done.4.refs_2_ = f32[2,8,128]{2,1,0:T(8,128)S(1)} collective-permute-done((f32[2,8,128]{2,1,0:T(8,128)S(1)}, f32[2,8,128]{2,1,0:T(8,128)S(1)}, u32[]{:S(2)}, u32[]{:S(2)}) %collective-permute-start.4) | collective-permute-done | bytes 8224 | tf_op jit(solution)/shard_map/ppermute | solution.py:628
  16.4 0.1 shard_map.50.refs_3_
  16.5 2.2 %collective-permute-start.5 = (f32[5,8,128]{2,1,0:T(8,128)S(1)}, f32[5,8,128]{2,1,0:T(8,128)S(1)}, u32[]{:S(2)}, u32[]{:S(2)}) collective-permute-start(f32[5,8,128]{2,1,0:T(8,128)S(1)} %shard_map.50.refs_3_), channel_id=1, source_target_pairs={{0,4},{1,5},{2,6},{3,7},{4,0},{5,1},{6,2},{7,3},{8,12},{9,13},{10,... | collective-permute-start | bytes 61448 | tf_op jit(solution)/shard_map/ppermute | solution.py:628
  18.7 1.4 %collective-permute-done.5.refs_4_ = f32[5,8,128]{2,1,0:T(8,128)S(1)} collective-permute-done((f32[5,8,128]{2,1,0:T(8,128)S(1)}, f32[5,8,128]{2,1,0:T(8,128)S(1)}, u32[]{:S(2)}, u32[]{:S(2)}) %collective-permute-start.5) | collective-permute-done | bytes 20512 | tf_op jit(solution)/shard_map/ppermute | solution.py:628
  20.1 0.4 %collective-permute-start.6 = (f32[5,8,128]{2,1,0:T(8,128)S(1)}, f32[5,8,128]{2,1,0:T(8,128)S(1)}, u32[]{:S(2)}, u32[]{:S(2)}) collective-permute-start(f32[5,8,128]{2,1,0:T(8,128)S(1)} %collective-permute-done.5.refs_4_), channel_id=1, source_target_pairs={{0,16},{1,17},{2,18},{3,19},{4,20},{5,21},{6,22},{7,23},{8,24},{9,... | collective-permute-start | bytes 61448 | tf_op jit(solution)/shard_map/ppermute | solution.py:628
  20.5 0.0 collective-permute-done.2.refs_3_
  20.5 0.3 %shard_map.48 = (f32[72,8,128]{2,1,0:T(8,128)S(1)}, f32[8,8,128]{2,1,0:T(8,128)S(1)}) custom-call(f32[33,8,128]{2,1,0:T(8,128)S(1)} %get-tuple-element.12.refs_1_.refs_0_, f32[32,8,128]{2,1,0:T(8,128)S(1)} %get-tuple-element.14.refs_1_, f32[33,8,128]{2,1,0:T(8,128)S(1)} %collective-permute-done.1.refs_2_, f32[33,8,128]{2,1,0:T(8,128)S(1)} %collective-permute-done.2.refs_3_), custom_call_target="tpu_custom_call" | custom-call | flops 1000000 | bytes 864256 | tf_op jit(solution)/shard_map/pallas_call | solution.py:602
  20.8 0.5 %collective-permute-done.6.refs_5_ = f32[5,8,128]{2,1,0:T(8,128)S(1)} collective-permute-done((f32[5,8,128]{2,1,0:T(8,128)S(1)}, f32[5,8,128]{2,1,0:T(8,128)S(1)}, u32[]{:S(2)}, u32[]{:S(2)}) %collective-permute-start.6) | collective-permute-done | bytes 20512 | tf_op jit(solution)/shard_map/ppermute | solution.py:628
  21.3 1.2 %shard_map.51 = f32[256,128]{1,0:T(8,128)} custom-call(f32[33,8,128]{2,1,0:T(8,128)S(1)} %get-tuple-element.12.refs_1_.refs_0_, f32[8,8,128]{2,1,0:T(8,128)S(1)} %get-tuple-element.16.refs_1_, f32[72,8,128]{2,1,0:T(8,128)S(1)} %get-tuple-element.17.refs_2_, f32[5,8,128]{2,1,0:T(8,128)S(1)} %shard_map.50.refs_3_, ...), custom_call_target="tpu_custom_call" | custom-call | flops 1000000 | bytes 655360 | tf_op jit(solution)/shard_map/pallas_call | solution.py:602
Async XLA Ops:
  0.0 1.6 %collective-permute-start = (f32[256,128]{1,0:T(8,128)}, f32[256,128]{1,0:T(8,128)S(1)}, u32[]{:S(2)}, u32[]{:S(2)}) collective-permute-start(f32[256,128]{1,0:T(8,128)} %bitcast.2), channel_id=1, source_target_pairs={{0,16},{1,17},{2,18},{3,19},{4,20},{5,21},{6,22},{7,23},{8,24},{9,... | collective-permute-start | bytes 393224 | tf_op jit(solution)/shard_map/ppermute | solution.py:628
  1.7 4.9 %collective-permute-start.1 = (f32[33,8,128]{2,1,0:T(8,128)S(1)}, f32[33,8,128]{2,1,0:T(8,128)S(1)}, u32[]{:S(2)}, u32[]{:S(2)}) collective-permute-start(f32[33,8,128]{2,1,0:T(8,128)S(1)} %get-tuple-element.15), channel_id=1, source_target_pairs={{0,3},{1,2},{2,1},{3,0},{4,7},{5,6},{6,5},{7,4},{8,11},{9,10},{10,... | collective-permute-start | bytes 405512 | tf_op jit(solution)/shard_map/ppermute | solution.py:628
  6.6 13.9 %collective-permute-start.2 = (f32[33,8,128]{2,1,0:T(8,128)S(1)}, f32[33,8,128]{2,1,0:T(8,128)S(1)}, u32[]{:S(2)}, u32[]{:S(2)}) collective-permute-start(f32[33,8,128]{2,1,0:T(8,128)S(1)} %collective-permute-done.1.refs_2_), channel_id=1, source_target_pairs={{0,16},{1,17},{2,18},{3,19},{4,20},{5,21},{6,22},{7,23},{8,24},{9,... | collective-permute-start | bytes 405512 | tf_op jit(solution)/shard_map/ppermute | solution.py:628
  10.9 4.3 %collective-permute-start.3 = (f32[2,8,128]{2,1,0:T(8,128)S(1)}, f32[2,8,128]{2,1,0:T(8,128)S(1)}, u32[]{:S(2)}, u32[]{:S(2)}) collective-permute-start(f32[2,8,128]{2,1,0:T(8,128)S(1)} %get-tuple-element.18), channel_id=1, source_target_pairs={{0,1},{1,0},{2,3},{3,2},{4,5},{5,4},{6,7},{7,6},{8,9},{9,8},{10,11... | collective-permute-start | bytes 24584 | tf_op jit(solution)/shard_map/ppermute | solution.py:628
  15.2 1.2 %collective-permute-start.4 = (f32[2,8,128]{2,1,0:T(8,128)S(1)}, f32[2,8,128]{2,1,0:T(8,128)S(1)}, u32[]{:S(2)}, u32[]{:S(2)}) collective-permute-start(f32[2,8,128]{2,1,0:T(8,128)S(1)} %collective-permute-done.3.refs_1_), channel_id=1, source_target_pairs={{0,16},{1,17},{2,18},{3,19},{4,20},{5,21},{6,22},{7,23},{8,24},{9,... | collective-permute-start | bytes 24584 | tf_op jit(solution)/shard_map/ppermute | solution.py:628
  16.5 3.6 %collective-permute-start.5 = (f32[5,8,128]{2,1,0:T(8,128)S(1)}, f32[5,8,128]{2,1,0:T(8,128)S(1)}, u32[]{:S(2)}, u32[]{:S(2)}) collective-permute-start(f32[5,8,128]{2,1,0:T(8,128)S(1)} %shard_map.50.refs_3_), channel_id=1, source_target_pairs={{0,4},{1,5},{2,6},{3,7},{4,0},{5,1},{6,2},{7,3},{8,12},{9,13},{10,... | collective-permute-start | bytes 61448 | tf_op jit(solution)/shard_map/ppermute | solution.py:628
  20.1 1.3 %collective-permute-start.6 = (f32[5,8,128]{2,1,0:T(8,128)S(1)}, f32[5,8,128]{2,1,0:T(8,128)S(1)}, u32[]{:S(2)}, u32[]{:S(2)}) collective-permute-start(f32[5,8,128]{2,1,0:T(8,128)S(1)} %collective-permute-done.5.refs_4_), channel_id=1, source_target_pairs={{0,16},{1,17},{2,18},{3,19},{4,20},{5,21},{6,22},{7,23},{8,24},{9,... | collective-permute-start | bytes 61448 | tf_op jit(solution)/shard_map/ppermute | solution.py:628

commit v7 on v6

--- a/solution.py
+++ b/solution.py
@@ -142,7 +142,7 @@
     m_ref[2 * sh.halo_tiles] = xo_ref[sh.mask_tile]
 
 
-def edge_kernel(sh, xo_ref, xp_ref, e_ref):
+def edge_kernel(sh, xo_ref, xp_ref, near_ref, e_ref):
     lane = sh.lanes()
     core0 = first_core()
     cx = sh.cx
@@ -158,29 +158,32 @@
         for k in range(cx):
             value = sh.row(xo_ref, sh.mask_tile, q * cx + k)
             edges[-1] = sh.edge_place(edges[-1], value, k + HALO, q, lane)
+    place_side(sh, edges, near_ref, core0)
     for t in range(sh.edge_tiles):
         e_ref[t] = edges[t]
 
 
-def merge_kernel(sh, e_ref, a_ref, b_ref, eo_ref):
-    core0 = first_core()
+def place_side(sh, edges, near_ref, first):
     column = sh.lanes() // sh.group
-    got = [
-        (jnp.where(core0, a_ref[i], b_ref[i]), jnp.where(core0, b_ref[i], a_ref[i]))
-        for i in range(2)
-    ]
+    got = near_ref[0], near_ref[1]
     for tile in range(sh.edge_tiles):
-        edge = e_ref[tile]
         comp, t = divmod(tile, sh.field_tiles)
-        for side in range(2):
-            for d in range(HALO):
-                place = sh.cx + HALO + d if side == 0 else HALO - 1 - d
-                if tile == sh.edge_tiles - 1:
-                    source, block = got[1][side], d
-                else:
-                    source, block = got[0][side], sh.near_block(int(comp != side), t, d)
-                edge = jnp.where(column == place, lane_roll(source, (place - block) * sh.group), edge)
-        eo_ref[tile] = edge
+        for d in range(HALO):
+            where = [sh.cx + HALO + d, HALO - 1 - d]
+            last = tile == sh.edge_tiles - 1
+            shifts = [
+                (place - (d if last else sh.near_block(int(comp != side), t, d))) * sh.group % sh.rows
+                for side, place in enumerate(where)
+            ]
+            moved = pltpu.roll(got[int(last)], jnp.where(first, *shifts), 1)
+            edges[tile] = jnp.where(column == jnp.where(first, *where), moved, edges[tile])
+
+
+def merge_kernel(sh, e_ref, near_ref, eo_ref):
+    edges = [e_ref[t] for t in range(sh.edge_tiles)]
+    place_side(sh, edges, near_ref, jnp.logical_not(first_core()))
+    for t in range(sh.edge_tiles):
+        eo_ref[t] = edges[t]
 
 
 STRIP = "strip"
@@ -665,8 +668,8 @@
     ex = edges_x(nx_edges)
     rx = bulk_x(m)
     ep = swap(ex)
-    (e0,) = call(edge_kernel, sh, [edge], (xo, xp), 100_000)
-    (e1,) = call(merge_kernel, sh, [edge], (e0, ex, ep), 10_000)
+    (e0,) = call(edge_kernel, sh, [edge], (xo, xp, ex), 100_000)
+    (e1,) = call(merge_kernel, sh, [edge], (e0, ep), 10_000)
     y = along_y(e1)
     rp = swap(rx)
     yp = swap(y)

time: 22.9 us -> 22.9 us (level)
  no operation moved by 1% of the time
where the time goes in v7:
time: 22.9 us; the launch traced here: 22.5 us
  starting transfers between devices  11.9 us (52%)
  waiting for transfers between devices  7.59 us (33%)
  Pallas kernels  2.95 us (13%)
    ppermute x7, starting transfers between devices, send(): return lax.ppermute(value, axes, pairs)  11.9 us
    ppermute x7, waiting for transfers between devices, send(): return lax.ppermute(value, axes, pairs)  7.59 us
    pallas_call x6, Pallas kernels, call(): pl.pallas_call(lambda *refs: kernel(sh, *refs), out_shape=outs, in_specs=...  2.95 us
  transfers between devices with their start and end apart: 7, of which 6 were waited for; matrix products, arithmetic and copies ran while one was open for 0% of the time, Pallas kernels for 7%

profile of v7, /device:TPU:1, one launch (start us, length us, event | category | flops | bytes accessed | tf_op | source)
XLA Modules:
  0.0 22.5 jit_solution(7586975932668503513)
XLA Ops:
  0.0 0.0 collective-permute-start
  0.0 1.0 %shard_map.46 = (f32[33,8,128]{2,1,0:T(8,128)S(1)}, f32[2,8,128]{2,1,0:T(8,128)S(1)}) custom-call(f32[256,128]{1,0:T(8,128)} %bitcast.3, f32[4,128]{1,0:T(4,128)} %refs_1_.1, s32[4,128]{1,0:T(4,128)} %refs_2_.1, s32[4,128]{1,0:T(4,128)} %refs_3_.1), custom_call_target="tpu_custom_call" | custom-call | flops 100000 | bytes 280576 | tf_op jit(solution)/shard_map/pallas_call | solution.py:605
  1.1 0.5 %collective-permute-done.refs_0_ = f32[256,128]{1,0:T(8,128)S(1)} collective-permute-done((f32[256,128]{1,0:T(8,128)}, f32[256,128]{1,0:T(8,128)S(1)}, u32[]{:S(2)}, u32[]{:S(2)}) %collective-permute-start) | collective-permute-done | bytes 131104 | tf_op jit(solution)/shard_map/ppermute | solution.py:631
  1.6 0.1 shard_map.47
  1.7 2.5 %collective-permute-start.1 = (f32[33,8,128]{2,1,0:T(8,128)S(1)}, f32[33,8,128]{2,1,0:T(8,128)S(1)}, u32[]{:S(2)}, u32[]{:S(2)}) collective-permute-start(f32[33,8,128]{2,1,0:T(8,128)S(1)} %get-tuple-element.15), channel_id=1, source_target_pairs={{0,3},{1,2},{2,1},{3,0},{4,7},{5,6},{6,5},{7,4},{8,11},{9,10},{10,... | collective-permute-start | bytes 405512 | tf_op jit(solution)/shard_map/ppermute | solution.py:631
  4.2 2.4 %collective-permute-done.1.refs_2_ = f32[33,8,128]{2,1,0:T(8,128)S(1)} collective-permute-done((f32[33,8,128]{2,1,0:T(8,128)S(1)}, f32[33,8,128]{2,1,0:T(8,128)S(1)}, u32[]{:S(2)}, u32[]{:S(2)}) %collective-permute-start.1) | collective-permute-done | bytes 135200 | tf_op jit(solution)/shard_map/ppermute | solution.py:631
  6.6 4.3 %collective-permute-start.2 = (f32[33,8,128]{2,1,0:T(8,128)S(1)}, f32[33,8,128]{2,1,0:T(8,128)S(1)}, u32[]{:S(2)}, u32[]{:S(2)}) collective-permute-start(f32[33,8,128]{2,1,0:T(8,128)S(1)} %collective-permute-done.1.refs_2_), channel_id=1, source_target_pairs={{0,16},{1,17},{2,18},{3,19},{4,20},{5,21},{6,22},{7,23},{8,24},{9,... | collective-permute-start | bytes 405512 | tf_op jit(solution)/shard_map/ppermute | solution.py:631
  10.9 2.5 %collective-permute-start.3 = (f32[2,8,128]{2,1,0:T(8,128)S(1)}, f32[2,8,128]{2,1,0:T(8,128)S(1)}, u32[]{:S(2)}, u32[]{:S(2)}) collective-permute-start(f32[2,8,128]{2,1,0:T(8,128)S(1)} %get-tuple-element.18), channel_id=1, source_target_pairs={{0,1},{1,0},{2,3},{3,2},{4,5},{5,4},{6,7},{7,6},{8,9},{9,8},{10,11... | collective-permute-start | bytes 24584 | tf_op jit(solution)/shard_map/ppermute | solution.py:631
  13.4 1.8 %collective-permute-done.3.refs_2_ = f32[2,8,128]{2,1,0:T(8,128)S(1)} collective-permute-done((f32[2,8,128]{2,1,0:T(8,128)S(1)}, f32[2,8,128]{2,1,0:T(8,128)S(1)}, u32[]{:S(2)}, u32[]{:S(2)}) %collective-permute-start.3) | collective-permute-done | bytes 8224 | tf_op jit(solution)/shard_map/ppermute | solution.py:631
  15.2 0.0 collective-permute-start.4
  15.2 0.2 shard_map.49.refs_0_
  15.4 1.0 %collective-permute-done.4.refs_1_ = f32[2,8,128]{2,1,0:T(8,128)S(1)} collective-permute-done((f32[2,8,128]{2,1,0:T(8,128)S(1)}, f32[2,8,128]{2,1,0:T(8,128)S(1)}, u32[]{:S(2)}, u32[]{:S(2)}) %collective-permute-start.4) | collective-permute-done | bytes 8224 | tf_op jit(solution)/shard_map/ppermute | solution.py:631
  16.4 0.1 shard_map.50.refs_3_
  16.4 2.2 %collective-permute-start.5 = (f32[5,8,128]{2,1,0:T(8,128)S(1)}, f32[5,8,128]{2,1,0:T(8,128)S(1)}, u32[]{:S(2)}, u32[]{:S(2)}) collective-permute-start(f32[5,8,128]{2,1,0:T(8,128)S(1)} %shard_map.50.refs_3_), channel_id=1, source_target_pairs={{0,4},{1,5},{2,6},{3,7},{4,0},{5,1},{6,2},{7,3},{8,12},{9,13},{10,... | collective-permute-start | bytes 61448 | tf_op jit(solution)/shard_map/ppermute | solution.py:631
  18.7 1.4 %collective-permute-done.5.refs_4_ = f32[5,8,128]{2,1,0:T(8,128)S(1)} collective-permute-done((f32[5,8,128]{2,1,0:T(8,128)S(1)}, f32[5,8,128]{2,1,0:T(8,128)S(1)}, u32[]{:S(2)}, u32[]{:S(2)}) %collective-permute-start.5) | collective-permute-done | bytes 20512 | tf_op jit(solution)/shard_map/ppermute | solution.py:631
  20.0 0.4 %collective-permute-start.6 = (f32[5,8,128]{2,1,0:T(8,128)S(1)}, f32[5,8,128]{2,1,0:T(8,128)S(1)}, u32[]{:S(2)}, u32[]{:S(2)}) collective-permute-start(f32[5,8,128]{2,1,0:T(8,128)S(1)} %collective-permute-done.5.refs_4_), channel_id=1, source_target_pairs={{0,16},{1,17},{2,18},{3,19},{4,20},{5,21},{6,22},{7,23},{8,24},{9,... | collective-permute-start | bytes 61448 | tf_op jit(solution)/shard_map/ppermute | solution.py:631
  20.4 0.0 collective-permute-done.2.refs_3_
  20.4 0.3 %shard_map.48 = (f32[72,8,128]{2,1,0:T(8,128)S(1)}, f32[8,8,128]{2,1,0:T(8,128)S(1)}) custom-call(f32[33,8,128]{2,1,0:T(8,128)S(1)} %get-tuple-element.12.refs_1_.refs_0_, f32[32,8,128]{2,1,0:T(8,128)S(1)} %get-tuple-element.14.refs_1_, f32[33,8,128]{2,1,0:T(8,128)S(1)} %collective-permute-done.1.refs_2_, f32[33,8,128]{2,1,0:T(8,128)S(1)} %collective-permute-done.2.refs_3_), custom_call_target="tpu_custom_call" | custom-call | flops 1000000 | bytes 864256 | tf_op jit(solution)/shard_map/pallas_call | solution.py:605
  20.8 0.5 %collective-permute-done.6.refs_5_ = f32[5,8,128]{2,1,0:T(8,128)S(1)} collective-permute-done((f32[5,8,128]{2,1,0:T(8,128)S(1)}, f32[5,8,128]{2,1,0:T(8,128)S(1)}, u32[]{:S(2)}, u32[]{:S(2)}) %collective-permute-start.6) | collective-permute-done | bytes 20512 | tf_op jit(solution)/shard_map/ppermute | solution.py:631
  21.3 1.2 %shard_map.51 = f32[256,128]{1,0:T(8,128)} custom-call(f32[33,8,128]{2,1,0:T(8,128)S(1)} %get-tuple-element.12.refs_1_.refs_0_, f32[8,8,128]{2,1,0:T(8,128)S(1)} %get-tuple-element.16.refs_1_, f32[72,8,128]{2,1,0:T(8,128)S(1)} %get-tuple-element.17.refs_2_, f32[5,8,128]{2,1,0:T(8,128)S(1)} %shard_map.50.refs_3_, ...), custom_call_target="tpu_custom_call" | custom-call | flops 1000000 | bytes 655360 | tf_op jit(solution)/shard_map/pallas_call | solution.py:605
Async XLA Ops:
  0.0 1.6 %collective-permute-start = (f32[256,128]{1,0:T(8,128)}, f32[256,128]{1,0:T(8,128)S(1)}, u32[]{:S(2)}, u32[]{:S(2)}) collective-permute-start(f32[256,128]{1,0:T(8,128)} %bitcast.2), channel_id=1, source_target_pairs={{0,16},{1,17},{2,18},{3,19},{4,20},{5,21},{6,22},{7,23},{8,24},{9,... | collective-permute-start | bytes 393224 | tf_op jit(solution)/shard_map/ppermute | solution.py:631
  1.7 4.9 %collective-permute-start.1 = (f32[33,8,128]{2,1,0:T(8,128)S(1)}, f32[33,8,128]{2,1,0:T(8,128)S(1)}, u32[]{:S(2)}, u32[]{:S(2)}) collective-permute-start(f32[33,8,128]{2,1,0:T(8,128)S(1)} %get-tuple-element.15), channel_id=1, source_target_pairs={{0,3},{1,2},{2,1},{3,0},{4,7},{5,6},{6,5},{7,4},{8,11},{9,10},{10,... | collective-permute-start | bytes 405512 | tf_op jit(solution)/shard_map/ppermute | solution.py:631
  6.6 13.9 %collective-permute-start.2 = (f32[33,8,128]{2,1,0:T(8,128)S(1)}, f32[33,8,128]{2,1,0:T(8,128)S(1)}, u32[]{:S(2)}, u32[]{:S(2)}) collective-permute-start(f32[33,8,128]{2,1,0:T(8,128)S(1)} %collective-permute-done.1.refs_2_), channel_id=1, source_target_pairs={{0,16},{1,17},{2,18},{3,19},{4,20},{5,21},{6,22},{7,23},{8,24},{9,... | collective-permute-start | bytes 405512 | tf_op jit(solution)/shard_map/ppermute | solution.py:631
  10.9 4.3 %collective-permute-start.3 = (f32[2,8,128]{2,1,0:T(8,128)S(1)}, f32[2,8,128]{2,1,0:T(8,128)S(1)}, u32[]{:S(2)}, u32[]{:S(2)}) collective-permute-start(f32[2,8,128]{2,1,0:T(8,128)S(1)} %get-tuple-element.18), channel_id=1, source_target_pairs={{0,1},{1,0},{2,3},{3,2},{4,5},{5,4},{6,7},{7,6},{8,9},{9,8},{10,11... | collective-permute-start | bytes 24584 | tf_op jit(solution)/shard_map/ppermute | solution.py:631
  15.2 1.2 %collective-permute-start.4 = (f32[2,8,128]{2,1,0:T(8,128)S(1)}, f32[2,8,128]{2,1,0:T(8,128)S(1)}, u32[]{:S(2)}, u32[]{:S(2)}) collective-permute-start(f32[2,8,128]{2,1,0:T(8,128)S(1)} %collective-permute-done.3.refs_2_), channel_id=1, source_target_pairs={{0,16},{1,17},{2,18},{3,19},{4,20},{5,21},{6,22},{7,23},{8,24},{9,... | collective-permute-start | bytes 24584 | tf_op jit(solution)/shard_map/ppermute | solution.py:631
  16.4 3.6 %collective-permute-start.5 = (f32[5,8,128]{2,1,0:T(8,128)S(1)}, f32[5,8,128]{2,1,0:T(8,128)S(1)}, u32[]{:S(2)}, u32[]{:S(2)}) collective-permute-start(f32[5,8,128]{2,1,0:T(8,128)S(1)} %shard_map.50.refs_3_), channel_id=1, source_target_pairs={{0,4},{1,5},{2,6},{3,7},{4,0},{5,1},{6,2},{7,3},{8,12},{9,13},{10,... | collective-permute-start | bytes 61448 | tf_op jit(solution)/shard_map/ppermute | solution.py:631
  20.0 1.3 %collective-permute-start.6 = (f32[5,8,128]{2,1,0:T(8,128)S(1)}, f32[5,8,128]{2,1,0:T(8,128)S(1)}, u32[]{:S(2)}, u32[]{:S(2)}) collective-permute-start(f32[5,8,128]{2,1,0:T(8,128)S(1)} %collective-permute-done.5.refs_4_), channel_id=1, source_target_pairs={{0,16},{1,17},{2,18},{3,19},{4,20},{5,21},{6,22},{7,23},{8,24},{9,... | collective-permute-start | bytes 61448 | tf_op jit(solution)/shard_map/ppermute | solution.py:631

commit v8 on v7

--- a/solution.py
+++ b/solution.py
@@ -205,8 +205,11 @@
 
     def along_rows(self, site):
         inner = site == STRIP or self.rough is None
-        value = self.centre(site) if inner else self.rough(site)
-        north, south = lane_roll(value, -1), lane_roll(value, 1)
+        if inner:
+            value = self.centre(site)
+            north, south = lane_roll(value, -1), lane_roll(value, 1)
+        else:
+            north, south = self.rough(site)
         if site == STRIP or self.seam is None:
             return north, south
         beyond = self.seam(site)
@@ -240,6 +243,9 @@
 
     def fresh_at(self, index, site):
         return index * self.n_sites + site - 1
+
+    def beside_at(self, index, site):
+        return (index * self.sh.cx + site - HALO) * 2
 
     def cumulate(self, x):
         reach = 1
@@ -396,7 +402,7 @@
             store(i, site, value)
 
 
-def column_kernel(sh, xo, xp, rx, rp, fresh, wet_ref, press):
+def column_kernel(sh, xo, xp, rx, rp, fresh, wet_ref, beside_ref, press):
     md = Model(sh)
     cx = sh.cx
 
@@ -434,6 +440,13 @@
     def fields(x, sides, comp):
         return [raw(x, sides, comp, ch) for ch in range(FIELDS)]
 
+    def rotate(indices):
+        for index in indices:
+            for site in md.own:
+                value, at = fresh[md.fresh_at(index, site)], md.beside_at(index, site)
+                beside_ref[at] = lane_roll(value, -1)
+                beside_ref[at + 1] = lane_roll(value, 1)
+
     def pressure_of(d):
         for j in range(sh.cols):
             press[j] = md.pressure(d, j)
@@ -450,6 +463,7 @@
         ]
         for site in md.first_step:
             store(PRESSURE, site, md.pressure(d, site))
+        rotate([ch for ch in range(FIELDS) if ch != U] + [PRESSURE])
 
     @pl.when(jnp.logical_not(md.core0))
     def _():
@@ -457,9 +471,10 @@
         pressure = pressure_of(d)
         for site in md.first_step:
             md.second_core_site(d, c, pressure, site, store, site in md.own)
-
-
-def step_kernel(sh, xo, wet_ref, fresh, edges, y, yp, out_ref, strips, cols, rims, seams):
+        rotate(list(range(FIELDS)) + [FLOW[V]])
+
+
+def step_kernel(sh, xo, wet_ref, fresh, beside_ref, edges, y, yp, out_ref, strips, cols, rims, seams):
     md = Model(sh)
     cx, lane, in_group = sh.cx, md.lane, md.in_group
     end = sh.rows - 1
@@ -555,7 +570,7 @@
             (lambda site: straight(rims[index], site, HALO - 1, HALO))
             if quick
             else seam_of(seams, index),
-            lambda j: fresh[md.fresh_at(index, j)],
+            lambda j: [beside_ref[md.beside_at(index, j) + n] for n in range(2)],
         )
 
     def write(ch, k_values):
@@ -674,10 +689,10 @@
     rp = swap(rx)
     yp = swap(y)
     n_sites = sh.cols - 2
-    fresh, wet = call(
+    fresh, wet, rotated = call(
         column_kernel,
         sh,
-        [tiles(sh, FRESH * n_sites), tiles(sh, sh.cols)],
+        [tiles(sh, FRESH * n_sites), tiles(sh, sh.cols), tiles(sh, FRESH * cx * 2)],
         (xo, xp, rx, rp),
         1_000_000,
         scratch=[pltpu.VMEM((sh.cols, lev, rows), jnp.float32)],
@@ -686,7 +701,7 @@
         step_kernel,
         sh,
         [jax.ShapeDtypeStruct(flat.shape, jnp.float32)],
-        (xo, wet, fresh, e1, y, yp),
+        (xo, wet, fresh, rotated, e1, y, yp),
         1_000_000,
         scratch=[
             pltpu.VMEM((2 * FIELDS + 2, lev, rows), jnp.float32),

time: 22.9 us -> 22.9 us (level)
  transfers between devices with their start and end apart: 7 -> 7, of which waited for: 6 -> 6; matrix products, arithmetic and copies ran while one was open for 0% -> 0% of each run, Pallas kernels for 7% -> 8%
where the time goes in v8:
time: 22.9 us; the launch traced here: 22.5 us
  starting transfers between devices  11.9 us (52%)
  waiting for transfers between devices  7.51 us (33%)
  Pallas kernels  3.01 us (13%)
    ppermute x7, starting transfers between devices, send(): return lax.ppermute(value, axes, pairs)  11.9 us
    ppermute x7, waiting for transfers between devices, send(): return lax.ppermute(value, axes, pairs)  7.51 us
    pallas_call x6, Pallas kernels, call(): pl.pallas_call(lambda *refs: kernel(sh, *refs), out_shape=outs, in_specs=...  3.01 us
  transfers between devices with their start and end apart: 7, of which 6 were waited for; matrix products, arithmetic and copies ran while one was open for 0% of the time, Pallas kernels for 8%

profile of v8, /device:TPU:1, one launch (start us, length us, event | category | flops | bytes accessed | tf_op | source)
XLA Modules:
  0.0 22.5 jit_solution(8247910375629727725)
XLA Ops:
  0.0 0.0 collective-permute-start
  0.0 1.0 %shard_map.46 = (f32[33,8,128]{2,1,0:T(8,128)S(1)}, f32[2,8,128]{2,1,0:T(8,128)S(1)}) custom-call(f32[256,128]{1,0:T(8,128)} %bitcast.3, f32[4,128]{1,0:T(4,128)} %refs_1_.1, s32[4,128]{1,0:T(4,128)} %refs_2_.1, s32[4,128]{1,0:T(4,128)} %refs_3_.1), custom_call_target="tpu_custom_call" | custom-call | flops 100000 | bytes 280576 | tf_op jit(solution)/shard_map/pallas_call | solution.py:620
  1.1 0.5 %collective-permute-done.refs_0_ = f32[256,128]{1,0:T(8,128)S(1)} collective-permute-done((f32[256,128]{1,0:T(8,128)}, f32[256,128]{1,0:T(8,128)S(1)}, u32[]{:S(2)}, u32[]{:S(2)}) %collective-permute-start) | collective-permute-done | bytes 131104 | tf_op jit(solution)/shard_map/ppermute | solution.py:646
  1.6 0.1 shard_map.47
  1.7 2.5 %collective-permute-start.1 = (f32[33,8,128]{2,1,0:T(8,128)S(1)}, f32[33,8,128]{2,1,0:T(8,128)S(1)}, u32[]{:S(2)}, u32[]{:S(2)}) collective-permute-start(f32[33,8,128]{2,1,0:T(8,128)S(1)} %get-tuple-element.16), channel_id=1, source_target_pairs={{0,3},{1,2},{2,1},{3,0},{4,7},{5,6},{6,5},{7,4},{8,11},{9,10},{10,... | collective-permute-start | bytes 405512 | tf_op jit(solution)/shard_map/ppermute | solution.py:646
  4.2 2.4 %collective-permute-done.1.refs_2_ = f32[33,8,128]{2,1,0:T(8,128)S(1)} collective-permute-done((f32[33,8,128]{2,1,0:T(8,128)S(1)}, f32[33,8,128]{2,1,0:T(8,128)S(1)}, u32[]{:S(2)}, u32[]{:S(2)}) %collective-permute-start.1) | collective-permute-done | bytes 135200 | tf_op jit(solution)/shard_map/ppermute | solution.py:646
  6.6 4.3 %collective-permute-start.2 = (f32[33,8,128]{2,1,0:T(8,128)S(1)}, f32[33,8,128]{2,1,0:T(8,128)S(1)}, u32[]{:S(2)}, u32[]{:S(2)}) collective-permute-start(f32[33,8,128]{2,1,0:T(8,128)S(1)} %collective-permute-done.1.refs_2_), channel_id=1, source_target_pairs={{0,16},{1,17},{2,18},{3,19},{4,20},{5,21},{6,22},{7,23},{8,24},{9,... | collective-permute-start | bytes 405512 | tf_op jit(solution)/shard_map/ppermute | solution.py:646
  10.9 2.5 %collective-permute-start.3 = (f32[2,8,128]{2,1,0:T(8,128)S(1)}, f32[2,8,128]{2,1,0:T(8,128)S(1)}, u32[]{:S(2)}, u32[]{:S(2)}) collective-permute-start(f32[2,8,128]{2,1,0:T(8,128)S(1)} %get-tuple-element.20), channel_id=1, source_target_pairs={{0,1},{1,0},{2,3},{3,2},{4,5},{5,4},{6,7},{7,6},{8,9},{9,8},{10,11... | collective-permute-start | bytes 24584 | tf_op jit(solution)/shard_map/ppermute | solution.py:646
  13.4 1.8 %collective-permute-done.3.refs_2_ = f32[2,8,128]{2,1,0:T(8,128)S(1)} collective-permute-done((f32[2,8,128]{2,1,0:T(8,128)S(1)}, f32[2,8,128]{2,1,0:T(8,128)S(1)}, u32[]{:S(2)}, u32[]{:S(2)}) %collective-permute-start.3) | collective-permute-done | bytes 8224 | tf_op jit(solution)/shard_map/ppermute | solution.py:646
  15.2 0.0 collective-permute-start.4
  15.2 0.2 shard_map.49.refs_0_
  15.4 1.0 %collective-permute-done.4.refs_1_ = f32[2,8,128]{2,1,0:T(8,128)S(1)} collective-permute-done((f32[2,8,128]{2,1,0:T(8,128)S(1)}, f32[2,8,128]{2,1,0:T(8,128)S(1)}, u32[]{:S(2)}, u32[]{:S(2)}) %collective-permute-start.4) | collective-permute-done | bytes 8224 | tf_op jit(solution)/shard_map/ppermute | solution.py:646
  16.4 0.1 shard_map.50.refs_4_
  16.4 2.2 %collective-permute-start.5 = (f32[5,8,128]{2,1,0:T(8,128)S(1)}, f32[5,8,128]{2,1,0:T(8,128)S(1)}, u32[]{:S(2)}, u32[]{:S(2)}) collective-permute-start(f32[5,8,128]{2,1,0:T(8,128)S(1)} %shard_map.50.refs_4_), channel_id=1, source_target_pairs={{0,4},{1,5},{2,6},{3,7},{4,0},{5,1},{6,2},{7,3},{8,12},{9,13},{10,... | collective-permute-start | bytes 61448 | tf_op jit(solution)/shard_map/ppermute | solution.py:646
  18.7 1.4 %collective-permute-done.5.refs_5_ = f32[5,8,128]{2,1,0:T(8,128)S(1)} collective-permute-done((f32[5,8,128]{2,1,0:T(8,128)S(1)}, f32[5,8,128]{2,1,0:T(8,128)S(1)}, u32[]{:S(2)}, u32[]{:S(2)}) %collective-permute-start.5) | collective-permute-done | bytes 20512 | tf_op jit(solution)/shard_map/ppermute | solution.py:646
  20.0 0.4 %collective-permute-start.6 = (f32[5,8,128]{2,1,0:T(8,128)S(1)}, f32[5,8,128]{2,1,0:T(8,128)S(1)}, u32[]{:S(2)}, u32[]{:S(2)}) collective-permute-start(f32[5,8,128]{2,1,0:T(8,128)S(1)} %collective-permute-done.5.refs_5_), channel_id=1, source_target_pairs={{0,16},{1,17},{2,18},{3,19},{4,20},{5,21},{6,22},{7,23},{8,24},{9,... | collective-permute-start | bytes 61448 | tf_op jit(solution)/shard_map/ppermute | solution.py:646
  20.4 0.0 collective-permute-done.2.refs_3_
  20.4 0.4 %shard_map.48 = (f32[72,8,128]{2,1,0:T(8,128)S(1)}, f32[8,8,128]{2,1,0:T(8,128)S(1)}, f32[96,8,128]{2,1,0:T(8,128)S(1)}) custom-call(f32[33,8,128]{2,1,0:T(8,128)S(1)} %get-tuple-element.13.refs_1_.refs_0_, f32[32,8,128]{2,1,0:T(8,128)S(1)} %get-tuple-element.15.refs_1_, f32[33,8,128]{2,1,0:T(8,128)S(1)} %collective-permute-done.1.refs_2_, ...), custom_call_target="tpu_custom_call" | custom-call | flops 1000000 | bytes 1257472 | tf_op jit(solution)/shard_map/pallas_call | solution.py:620
  20.9 0.4 %collective-permute-done.6.refs_6_ = f32[5,8,128]{2,1,0:T(8,128)S(1)} collective-permute-done((f32[5,8,128]{2,1,0:T(8,128)S(1)}, f32[5,8,128]{2,1,0:T(8,128)S(1)}, u32[]{:S(2)}, u32[]{:S(2)}) %collective-permute-start.6) | collective-permute-done | bytes 20512 | tf_op jit(solution)/shard_map/ppermute | solution.py:646
  21.3 1.2 %shard_map.51 = f32[256,128]{1,0:T(8,128)} custom-call(f32[33,8,128]{2,1,0:T(8,128)S(1)} %get-tuple-element.13.refs_1_.refs_0_, f32[8,8,128]{2,1,0:T(8,128)S(1)} %get-tuple-element.17.refs_1_, f32[72,8,128]{2,1,0:T(8,128)S(1)} %get-tuple-element.18.refs_2_, f32[96,8,128]{2,1,0:T(8,128)S(1)} %get-tuple-element.19.refs_3_, ...), custom_call_target="tpu_custom_call" | custom-call | flops 1000000 | bytes 1048576 | tf_op jit(solution)/shard_map/pallas_call | solution.py:620
Async XLA Ops:
  0.0 1.6 %collective-permute-start = (f32[256,128]{1,0:T(8,128)}, f32[256,128]{1,0:T(8,128)S(1)}, u32[]{:S(2)}, u32[]{:S(2)}) collective-permute-start(f32[256,128]{1,0:T(8,128)} %bitcast.2), channel_id=1, source_target_pairs={{0,16},{1,17},{2,18},{3,19},{4,20},{5,21},{6,22},{7,23},{8,24},{9,... | collective-permute-start | bytes 393224 | tf_op jit(solution)/shard_map/ppermute | solution.py:646
  1.7 4.9 %collective-permute-start.1 = (f32[33,8,128]{2,1,0:T(8,128)S(1)}, f32[33,8,128]{2,1,0:T(8,128)S(1)}, u32[]{:S(2)}, u32[]{:S(2)}) collective-permute-start(f32[33,8,128]{2,1,0:T(8,128)S(1)} %get-tuple-element.16), channel_id=1, source_target_pairs={{0,3},{1,2},{2,1},{3,0},{4,7},{5,6},{6,5},{7,4},{8,11},{9,10},{10,... | collective-permute-start | bytes 405512 | tf_op jit(solution)/shard_map/ppermute | solution.py:646
  6.6 13.9 %collective-permute-start.2 = (f32[33,8,128]{2,1,0:T(8,128)S(1)}, f32[33,8,128]{2,1,0:T(8,128)S(1)}, u32[]{:S(2)}, u32[]{:S(2)}) collective-permute-start(f32[33,8,128]{2,1,0:T(8,128)S(1)} %collective-permute-done.1.refs_2_), channel_id=1, source_target_pairs={{0,16},{1,17},{2,18},{3,19},{4,20},{5,21},{6,22},{7,23},{8,24},{9,... | collective-permute-start | bytes 405512 | tf_op jit(solution)/shard_map/ppermute | solution.py:646
  10.9 4.3 %collective-permute-start.3 = (f32[2,8,128]{2,1,0:T(8,128)S(1)}, f32[2,8,128]{2,1,0:T(8,128)S(1)}, u32[]{:S(2)}, u32[]{:S(2)}) collective-permute-start(f32[2,8,128]{2,1,0:T(8,128)S(1)} %get-tuple-element.20), channel_id=1, source_target_pairs={{0,1},{1,0},{2,3},{3,2},{4,5},{5,4},{6,7},{7,6},{8,9},{9,8},{10,11... | collective-permute-start | bytes 24584 | tf_op jit(solution)/shard_map/ppermute | solution.py:646
  15.2 1.2 %collective-permute-start.4 = (f32[2,8,128]{2,1,0:T(8,128)S(1)}, f32[2,8,128]{2,1,0:T(8,128)S(1)}, u32[]{:S(2)}, u32[]{:S(2)}) collective-permute-start(f32[2,8,128]{2,1,0:T(8,128)S(1)} %collective-permute-done.3.refs_2_), channel_id=1, source_target_pairs={{0,16},{1,17},{2,18},{3,19},{4,20},{5,21},{6,22},{7,23},{8,24},{9,... | collective-permute-start | bytes 24584 | tf_op jit(solution)/shard_map/ppermute | solution.py:646
  16.4 3.6 %collective-permute-start.5 = (f32[5,8,128]{2,1,0:T(8,128)S(1)}, f32[5,8,128]{2,1,0:T(8,128)S(1)}, u32[]{:S(2)}, u32[]{:S(2)}) collective-permute-start(f32[5,8,128]{2,1,0:T(8,128)S(1)} %shard_map.50.refs_4_), channel_id=1, source_target_pairs={{0,4},{1,5},{2,6},{3,7},{4,0},{5,1},{6,2},{7,3},{8,12},{9,13},{10,... | collective-permute-start | bytes 61448 | tf_op jit(solution)/shard_map/ppermute | solution.py:646
  20.0 1.3 %collective-permute-start.6 = (f32[5,8,128]{2,1,0:T(8,128)S(1)}, f32[5,8,128]{2,1,0:T(8,128)S(1)}, u32[]{:S(2)}, u32[]{:S(2)}) collective-permute-start(f32[5,8,128]{2,1,0:T(8,128)S(1)} %collective-permute-done.5.refs_5_), channel_id=1, source_target_pairs={{0,16},{1,17},{2,18},{3,19},{4,20},{5,21},{6,22},{7,23},{8,24},{9,... | collective-permute-start | bytes 61448 | tf_op jit(solution)/shard_map/ppermute | solution.py:646
